TPU v7x, 128 devices: a whole 4x4x4 slice. The times are simulated.
128 devices in a mesh: gx: 4 (over x), gy: 8 (over y_hi, z), gz: 4 (over y_lo, core).
Axes of the slice: x: 4, y: 4 (y_hi: 2, y_lo: 2; y = y_hi * 2 + y_lo), z: 4, core: 2. Of those that a mesh axis runs over, the one named last changes fastest.
Arguments:
- intensity: float32 [32, 64, 512], P('gx', 'gy', 'gz'), may hold values from -6 to 6
- cotangent: float32 [32, 64, 512], P('gx', 'gy', 'gz'), may hold values from -6 to 6
- departure_cells: int32 [2, 2, 3, 32, 64, 512], P(None, None, None, 'gx', 'gy', 'gz'), may hold values from -2 to 2
- departure_fracs: float32 [2, 2, 3, 32, 64, 512], P(None, None, None, 'gx', 'gy', 'gz'), may hold values from 0 to 1
Outputs:
- intensity_adjoint: float32 [32, 64, 512], P('gx', 'gy', 'gz')
- velocity_adjoint: float32 [3, 32, 64, 512], P(None, 'gx', 'gy', 'gz')
All inputs are finite; a program needn't handle non-finite values.
Results may differ from a plain program's by a relative error of at most 0.00002.
Values sent between devices are 32-bit elements; how exact they have to be, the bound alone decides.
A program may use at most 128 MiB of HBM per device.

v0:
```python
import functools

import jax
import jax.numpy as jnp
from jax import lax
from jax.experimental import pallas as pl
from jax.experimental.pallas import tpu as pltpu
from jax.sharding import PartitionSpec as P

MARGIN = 4
SHIFTS = 8
AXES = (("gx", 0), ("gy", 1), ("gz", 2))


def cubic_taps(fraction):
    fraction_squared = fraction * fraction
    fraction_cubed = fraction_squared * fraction
    weights = [
        0.5 * (2.0 * fraction_squared - fraction_cubed - fraction),
        0.5 * (3.0 * fraction_cubed - 5.0 * fraction_squared + 2.0),
        0.5 * (4.0 * fraction_squared - 3.0 * fraction_cubed + fraction),
        0.5 * (fraction_cubed - fraction_squared),
    ]
    slopes = [
        0.5 * (4.0 * fraction - 3.0 * fraction_squared - 1.0),
        0.5 * (9.0 * fraction_squared - 10.0 * fraction),
        0.5 * (8.0 * fraction - 9.0 * fraction_squared + 1.0),
        0.5 * (3.0 * fraction_squared - 2.0 * fraction),
    ]
    return (weights, slopes)


def build_tables(cells_ref, fracs_ref, step, section, weight_refs, slope_refs):
    for component in range(3):
        offsets = cells_ref[step, section, component]
        weights, slopes = cubic_taps(fracs_ref[step, section, component])
        for shift in range(SHIFTS):
            target = shift - 3
            summed = jnp.zeros(offsets.shape, jnp.float32)
            slope_sum = jnp.zeros(offsets.shape, jnp.float32)
            for tap_index in range(4):
                hit = offsets + (tap_index - 1) == target
                summed = summed + jnp.where(hit, weights[tap_index], 0.0)
                if slope_refs is not None:
                    slope_sum = slope_sum + jnp.where(hit, slopes[tap_index], 0.0)
            weight_refs[component][shift] = summed
            if slope_refs is not None:
                slope_refs[component][shift] = slope_sum


def roll_lanes(field, shift):
    shift = shift % field.shape[-1]
    if shift == 0:
        return field
    return pltpu.roll(field, shift, field.ndim - 1)


def sample_block(wrapped_ref, rolled_ref, window_ref, weight_refs, slope_refs, with_value):
    px, py, pz = wrapped_ref.shape
    nx, ny, nz = px - 2 * MARGIN, py - 2 * MARGIN, window_ref.shape[-1]
    field = wrapped_ref[...]
    for sz in range(SHIFTS):
        rolled_ref[...] = roll_lanes(field, 3 - sz)[:, :, :nz]
        for sy in range(SHIFTS):
            window_ref[sy, sz] = rolled_ref[:, sy + 1 : sy + 1 + ny, :]
    table_x, table_y, table_z = weight_refs
    shape = (nx, ny, nz)

    def along_y(sy, carry):
        value, grad_x, grad_y, grad_z = carry
        along_x = jnp.zeros(shape, jnp.float32)
        along_x_slope = jnp.zeros(shape, jnp.float32)
        along_x_zslope = jnp.zeros(shape, jnp.float32)
        for sx in range(SHIFTS):
            column = jnp.zeros(shape, jnp.float32)
            slope_column = jnp.zeros(shape, jnp.float32)
            for sz in range(SHIFTS):
                window = window_ref[sy, sz, sx + 1 : sx + 1 + nx]
                column = column + table_z[sz] * window
                if slope_refs is not None:
                    slope_column = slope_column + slope_refs[2][sz] * window
            along_x = along_x + table_x[sx] * column
            if slope_refs is not None:
                along_x_slope = along_x_slope + slope_refs[0][sx] * column
                along_x_zslope = along_x_zslope + table_x[sx] * slope_column
        weight_y = table_y[sy]
        if with_value:
            value = value + weight_y * along_x
        if slope_refs is not None:
            grad_x = grad_x + weight_y * along_x_slope
            grad_y = grad_y + slope_refs[1][sy] * along_x
            grad_z = grad_z + weight_y * along_x_zslope
        return value, grad_x, grad_y, grad_z

    zero = jnp.zeros(shape, jnp.float32)
    value, grad_x, grad_y, grad_z = lax.fori_loop(0, SHIFTS, along_y, (zero,) * 4)
    return value, (grad_x, grad_y, grad_z)


def spread_block(field, weight_refs, product_ref, staged_ref, pz):
    table_x, table_y, table_z = weight_refs
    nx, ny, nz = field.shape
    px, py = nx + 2 * MARGIN, ny + 2 * MARGIN
    for sy in range(SHIFTS):
        weighted = table_y[sy] * field
        for sx in range(SHIFTS):
            product_ref[sy, sx] = table_x[sx] * weighted
    def along_z(sz, total):
        weight_z = table_z[sz]
        for sy in range(SHIFTS):
            rows = [None] * px
            for sx in range(SHIFTS):
                deposit = weight_z * product_ref[sy, sx]
                for x in range(nx):
                    slot = x + sx + 1
                    rows[slot] = deposit[x] if rows[slot] is None else rows[slot] + deposit[x]
            rows[0] = jnp.zeros((ny, nz), jnp.float32)
            for slot in range(px):
                staged_ref[sy, slot, 8 : 8 + ny, :] = rows[slot]
        summed = jnp.zeros((px, py, nz), jnp.float32)
        for sy in range(SHIFTS):
            summed = summed + staged_ref[sy, :, 7 - sy : 7 - sy + py, :]
        padded = jnp.concatenate([summed, jnp.zeros((px, py, pz - nz), jnp.float32)], axis=2)
        shift = lax.rem(sz + (pz - 3), pz)
        return total + pltpu.roll(padded, shift, 2)

    total = lax.fori_loop(0, SHIFTS, along_z, jnp.zeros((px, py, pz), jnp.float32))
    return total


def table_scratch(shape, count):
    return [pltpu.VMEM((SHIFTS,) + shape, jnp.float32) for _ in range(count)]


def clear_rims(staged_ref):
    staged_ref[...] = jnp.zeros(staged_ref.shape, jnp.float32)


def early_sample_kernel(wrapped_ref, cells_ref, fracs_ref, image_ref, grad_ref,
                        rolled_ref, window_ref, *tables):
    weights, slopes = tables[:3], tables[3:]
    build_tables(cells_ref, fracs_ref, 0, 1, weights, slopes)
    value, grads = sample_block(wrapped_ref, rolled_ref, window_ref, weights, slopes, True)
    image_ref[...] = value
    for component in range(3):
        grad_ref[component] = grads[component]


def late_spread_kernel(cot_ref, cells_ref, fracs_ref, out_ref, product_ref, staged_ref, *tables):
    build_tables(cells_ref, fracs_ref, 1, 1, tables, None)
    clear_rims(staged_ref)
    out_ref[...] = spread_block(cot_ref[...], tables, product_ref, staged_ref, out_ref.shape[-1])


def late_velocity_kernel(wrapped_ref, cot_ref, cells_ref, fracs_ref, out_ref,
                         rolled_ref, window_ref, product_ref, staged_ref, *tables):
    weights, slopes, mid = tables[:3], tables[3:6], tables[6:]
    build_tables(cells_ref, fracs_ref, 1, 1, weights, slopes)
    build_tables(cells_ref, fracs_ref, 1, 0, mid, None)
    _, grads = sample_block(wrapped_ref, rolled_ref, window_ref, weights, slopes, False)
    cot = cot_ref[...]
    clear_rims(staged_ref)
    for component in range(3):
        out_ref[component] = spread_block(cot * grads[component], mid, product_ref, staged_ref,
                                          out_ref.shape[-1])


def early_spread_kernel(adjoint_ref, grad_ref, cells_ref, fracs_ref, out_ref,
                        product_ref, staged_ref, *tables):
    dep, mid = tables[:3], tables[3:]
    build_tables(cells_ref, fracs_ref, 0, 1, dep, None)
    build_tables(cells_ref, fracs_ref, 0, 0, mid, None)
    adjoint = adjoint_ref[...]
    clear_rims(staged_ref)
    pz = out_ref.shape[-1]
    out_ref[0] = spread_block(adjoint, dep, product_ref, staged_ref, pz)
    for component in range(3):
        out_ref[1 + component] = spread_block(adjoint * grad_ref[component], mid, product_ref,
                                              staged_ref, pz)


def vmem_call(kernel, out_shapes, scratch, *args):
    return pl.pallas_call(
        kernel,
        out_shape=out_shapes,
        in_specs=[pl.BlockSpec(memory_space=pltpu.VMEM)] * len(args),
        out_specs=jax.tree.map(lambda _: pl.BlockSpec(memory_space=pltpu.VMEM), out_shapes),
        scratch_shapes=scratch,
        compiler_params=pltpu.CompilerParams(vmem_limit_bytes=48 * 1024 * 1024),
    )(*args)


def shift_from(piece, axis, upward):
    count = lax.axis_size(axis)
    if upward:
        pairs = [(i, (i + 1) % count) for i in range(count)]
    else:
        pairs = [((i + 1) % count, i) for i in range(count)]
    shape = piece.shape
    if shape[-1] < 128 and piece.size % 1024 == 0:
        flat = lax.ppermute(piece.reshape(-1, 128), axis, pairs)
        return flat.reshape(shape)
    return lax.ppermute(piece, axis, pairs)


def widen(block, pz):
    for axis, dim in AXES[:2]:
        size = block.shape[dim]
        head = lax.slice_in_dim(block, 0, MARGIN, axis=dim)
        tail = lax.slice_in_dim(block, size - MARGIN, size, axis=dim)
        block = jnp.concatenate(
            [shift_from(tail, axis, True), block, shift_from(head, axis, False)], axis=dim
        )
    nz = block.shape[2]
    head = block[:, :, :MARGIN]
    tail = block[:, :, nz - MARGIN :]
    gap = jnp.zeros(block.shape[:2] + (pz - nz - 2 * MARGIN,), jnp.float32)
    return jnp.concatenate(
        [block, shift_from(head, "gz", False), gap, shift_from(tail, "gz", True)], axis=2
    )


def place_rim(rim, dim, start, size):
    widths = [(0, 0)] * rim.ndim
    widths[dim] = (start, size - start - rim.shape[dim])
    return jnp.pad(rim, widths)


def fold(wrapped, nz):
    pz = wrapped.shape[3]
    upper = wrapped[..., nz : nz + MARGIN]
    lower = wrapped[..., pz - MARGIN :]
    block = wrapped[..., :nz]
    from_below = shift_from(upper, "gz", True)
    from_above = shift_from(lower, "gz", False)
    block = block + place_rim(from_below, 3, 0, nz)
    block = block + place_rim(from_above, 3, nz - MARGIN, nz)
    for axis, dim in (("gy", 2), ("gx", 1)):
        size = block.shape[dim] - 2 * MARGIN
        low = lax.slice_in_dim(block, 0, MARGIN, axis=dim)
        high = lax.slice_in_dim(block, size + MARGIN, size + 2 * MARGIN, axis=dim)
        block = lax.slice_in_dim(block, MARGIN, size + MARGIN, axis=dim)
        got_low = shift_from(high, axis, True)
        got_high = shift_from(low, axis, False)
        block = block + place_rim(got_low, dim, 0, size)
        block = block + place_rim(got_high, dim, size - MARGIN, size)
    return block


def body(intensity, cotangent, departure_cells, departure_fracs):
    cells = departure_cells
    fracs = departure_fracs
    nx, ny, nz = intensity.shape
    px, py, pz = nx + 2 * MARGIN, ny + 2 * MARGIN, nz + 128
    block = (nx, ny, nz)
    f32 = jnp.float32
    rolled = pltpu.VMEM((px, py, nz), f32)
    windows = pltpu.VMEM((SHIFTS, SHIFTS, px, ny, nz), f32)
    products = pltpu.VMEM((SHIFTS, SHIFTS) + block, f32)
    staged = pltpu.VMEM((SHIFTS, px, ny + 16, nz), f32)

    wrapped = widen(intensity, pz)
    image_mid, grad_raw = vmem_call(
        early_sample_kernel,
        (jax.ShapeDtypeStruct(block, f32), jax.ShapeDtypeStruct((3,) + block, f32)),
        [rolled, windows] + table_scratch(block, 6),
        wrapped, cells, fracs,
    )
    adjoint_padded = vmem_call(
        late_spread_kernel,
        jax.ShapeDtypeStruct((px, py, pz), f32),
        [products, staged] + table_scratch(block, 3),
        cotangent, cells, fracs,
    )
    wrapped_mid = widen(image_mid, pz)
    velocity_padded = vmem_call(
        late_velocity_kernel,
        jax.ShapeDtypeStruct((3, px, py, pz), f32),
        [rolled, windows, products, staged] + table_scratch(block, 9),
        wrapped_mid, cotangent, cells, fracs,
    )
    folded = fold(jnp.concatenate([adjoint_padded[None], velocity_padded]), nz)
    adjoint_mid = folded[0]
    velocity_late = folded[1:]
    early_padded = vmem_call(
        early_spread_kernel,
        jax.ShapeDtypeStruct((4, px, py, pz), f32),
        [products, staged] + table_scratch(block, 6),
        adjoint_mid, grad_raw, cells, fracs,
    )
    folded = fold(early_padded, nz)
    return (folded[0], velocity_late + folded[1:])


def solution(mesh):
    in_specs = (
        P("gx", "gy", "gz"),
        P("gx", "gy", "gz"),
        P(None, None, None, "gx", "gy", "gz"),
        P(None, None, None, "gx", "gy", "gz"),
    )
    out_specs = (P("gx", "gy", "gz"), P(None, "gx", "gy", "gz"))
    return jax.shard_map(body, mesh=mesh, in_specs=in_specs, out_specs=out_specs, check_vma=False)
```

profile of v0, /device:TPU:102, one launch (start us, length us, event | category | flops | bytes accessed | tf_op | source)
XLA Modules:
  0.0 111.7 jit_solution(3753327918418819437)
XLA Ops:
  0.6 0.7 fusion.19
  1.4 0.5 collective-permute-start
  1.9 1.5 %collective-permute-start.1 = (f32[4,8,128]{2,1,0:T(8,128)S(1)}, f32[4,8,128]{2,1,0:T(8,128)S(1)}, u32[]{:S(2)}, u32[]{:S(2)}) collective-permute-start(f32[4,8,128]{2,1,0:T(8,128)S(1)} %get-tuple-element.28), channel_id=1, source_target_pairs={{32,0},{64,32},{96,64},{0,96},{33,1},{65,33},{97,65},{1,97},{34,2}... | collective-permute-start | bytes 49160 | tf_op jit(solution)/shard_map/ppermute | solution.py:203
  3.4 1.7 %collective-permute-done = f32[4,8,128]{2,1,0:T(8,128)S(1)} collective-permute-done((f32[4,8,128]{2,1,0:T(8,128)S(1)}, f32[4,8,128]{2,1,0:T(8,128)S(1)}, u32[]{:S(2)}, u32[]{:S(2)}) %collective-permute-start) | collective-permute-done | bytes 16416 | tf_op jit(solution)/shard_map/ppermute | solution.py:203
  5.1 1.7 %collective-permute-done.1 = f32[4,8,128]{2,1,0:T(8,128)S(1)} collective-permute-done((f32[4,8,128]{2,1,0:T(8,128)S(1)}, f32[4,8,128]{2,1,0:T(8,128)S(1)}, u32[]{:S(2)}, u32[]{:S(2)}) %collective-permute-start.1) | collective-permute-done | bytes 16416 | tf_op jit(solution)/shard_map/ppermute | solution.py:203
  6.8 1.9 %collective-permute-start.2 = (f32[16,4,128]{2,1,0:T(4,128)S(1)}, f32[16,4,128]{2,1,0:T(4,128)S(1)}, u32[]{:S(2)}, u32[]{:S(2)}) collective-permute-start(f32[16,4,128]{2,1,0:T(4,128)S(1)} %get-tuple-element.24), channel_id=1, source_target_pairs={{0,4},{4,8},{8,12},{12,16},{16,20},{20,24},{24,28},{28,0},{1,5},{5... | collective-permute-start | bytes 98312 | tf_op jit(solution)/shard_map/ppermute | solution.py:203
  8.9 1.9 %collective-permute-done.2 = f32[16,4,128]{2,1,0:T(4,128)S(1)} collective-permute-done((f32[16,4,128]{2,1,0:T(4,128)S(1)}, f32[16,4,128]{2,1,0:T(4,128)S(1)}, u32[]{:S(2)}, u32[]{:S(2)}) %collective-permute-start.2) | collective-permute-done | bytes 32800 | tf_op jit(solution)/shard_map/ppermute | solution.py:203
  10.8 5.4 %collective-permute-done.3 = f32[16,4,128]{2,1,0:T(4,128)S(1)} collective-permute-done((f32[16,4,128]{2,1,0:T(4,128)S(1)}, f32[16,4,128]{2,1,0:T(4,128)S(1)}, u32[]{:S(2)}, u32[]{:S(2)}) %collective-permute-start.3) | collective-permute-done | bytes 32800 | tf_op jit(solution)/shard_map/ppermute | solution.py:203
  16.7 0.6 collective-permute-start.5
  17.3 0.6 collective-permute-done.4
  18.1 1.7 %collective-permute-done.5 = f32[8,128]{1,0:T(8,128)S(1)} collective-permute-done((f32[8,128]{1,0:T(8,128)S(1)}, f32[8,128]{1,0:T(8,128)S(1)}, u32[]{:S(2)}, u32[]{:S(2)}) %collective-permute-start.5) | collective-permute-done | bytes 4128 | tf_op jit(solution)/shard_map/ppermute | solution.py:201
  20.1 4.2 %shard_map.60 = (f32[8,8,128]{2,1,0:T(8,128)S(1)}, f32[3,8,8,128]{3,2,1,0:T(8,128)S(1)}) custom-call(f32[16,16,256]{2,1,0:T(8,128)S(1)} %pad_maximum_fusion.1.wrapped_ref, s32[2,2,3,8,8,128]{5,4,3,2,1,0:T(8,128)S(1)} %copy-done, f32[2,2,3,8,8,128]{5,4,3,2,1,0:T(8,128)S(1)} %copy-done.1), custom_call_target="tpu_custom_call" | custom-call | tf_op jit(solution)/shard_map/pallas_call | solution.py:183
  24.3 0.3 collective-permute-start.6
  24.6 1.7 %collective-permute-start.7 = (f32[4,8,128]{2,1,0:T(8,128)S(1)}, f32[4,8,128]{2,1,0:T(8,128)S(1)}, u32[]{:S(2)}, u32[]{:S(2)}) collective-permute-start(f32[4,8,128]{2,1,0:T(8,128)S(1)} %get-tuple-element.26), channel_id=1, source_target_pairs={{32,0},{64,32},{96,64},{0,96},{33,1},{65,33},{97,65},{1,97},{34,2}... | collective-permute-start | bytes 49160 | tf_op jit(solution)/shard_map/ppermute | solution.py:203
  26.4 1.7 %collective-permute-done.6 = f32[4,8,128]{2,1,0:T(8,128)S(1)} collective-permute-done((f32[4,8,128]{2,1,0:T(8,128)S(1)}, f32[4,8,128]{2,1,0:T(8,128)S(1)}, u32[]{:S(2)}, u32[]{:S(2)}) %collective-permute-start.6) | collective-permute-done | bytes 16416 | tf_op jit(solution)/shard_map/ppermute | solution.py:203
  28.1 1.5 %collective-permute-done.7 = f32[4,8,128]{2,1,0:T(8,128)S(1)} collective-permute-done((f32[4,8,128]{2,1,0:T(8,128)S(1)}, f32[4,8,128]{2,1,0:T(8,128)S(1)}, u32[]{:S(2)}, u32[]{:S(2)}) %collective-permute-start.7) | collective-permute-done | bytes 16416 | tf_op jit(solution)/shard_map/ppermute | solution.py:203
  29.7 2.0 %collective-permute-start.9 = (f32[16,4,128]{2,1,0:T(4,128)S(1)}, f32[16,4,128]{2,1,0:T(4,128)S(1)}, u32[]{:S(2)}, u32[]{:S(2)}) collective-permute-start(f32[16,4,128]{2,1,0:T(4,128)S(1)} %get-tuple-element.23), channel_id=1, source_target_pairs={{4,0},{8,4},{12,8},{16,12},{20,16},{24,20},{28,24},{0,28},{5,1},{9... | collective-permute-start | bytes 98312 | tf_op jit(solution)/shard_map/ppermute | solution.py:203
  31.7 1.9 %collective-permute-done.8 = f32[16,4,128]{2,1,0:T(4,128)S(1)} collective-permute-done((f32[16,4,128]{2,1,0:T(4,128)S(1)}, f32[16,4,128]{2,1,0:T(4,128)S(1)}, u32[]{:S(2)}, u32[]{:S(2)}) %collective-permute-start.8) | collective-permute-done | bytes 32800 | tf_op jit(solution)/shard_map/ppermute | solution.py:203
  33.6 3.7 %collective-permute-done.9 = f32[16,4,128]{2,1,0:T(4,128)S(1)} collective-permute-done((f32[16,4,128]{2,1,0:T(4,128)S(1)}, f32[16,4,128]{2,1,0:T(4,128)S(1)}, u32[]{:S(2)}, u32[]{:S(2)}) %collective-permute-start.9) | collective-permute-done | bytes 32800 | tf_op jit(solution)/shard_map/ppermute | solution.py:203
  37.8 0.7 collective-permute-start.11
  38.5 3.5 %shard_map.59 = f32[16,16,256]{2,1,0:T(8,128)S(1)} custom-call(f32[8,8,128]{2,1,0:T(8,128)S(1)} %copy-done.2, s32[2,2,3,8,8,128]{5,4,3,2,1,0:T(8,128)S(1)} %copy-done, f32[2,2,3,8,8,128]{5,4,3,2,1,0:T(8,128)S(1)} %copy-done.1), custom_call_target="tpu_custom_call" | custom-call | tf_op jit(solution)/shard_map/pallas_call | solution.py:183
  42.4 13.6 %shard_map.61 = f32[3,16,16,256]{3,2,1,0:T(8,128)S(1)} custom-call(f32[16,16,256]{2,1,0:T(8,128)S(1)} %pad_maximum_fusion.2.wrapped_ref, f32[8,8,128]{2,1,0:T(8,128)S(1)} %copy-done.2, s32[2,2,3,8,8,128]{5,4,3,2,1,0:T(8,128)S(1)} %copy-done, f32[2,2,3,8,8,128]{5,4,3,2,1,0:T(8,128)S(1)} %copy-done.1), custom_call_target="tpu_custom_call" | custom-call | tf_op jit(solution)/shard_map/pallas_call | solution.py:183
  56.5 0.5 collective-permute-start.12
  57.2 1.4 %collective-permute-start.13 = (f32[32,128]{1,0:T(8,128)S(1)}, f32[32,128]{1,0:T(8,128)S(1)}, u32[]{:S(2)}, u32[]{:S(2)}) collective-permute-start(f32[32,128]{1,0:T(8,128)S(1)} %reshape.62), channel_id=1, source_target_pairs={{1,0},{2,1},{3,2},{0,3},{5,4},{6,5},{7,6},{4,7},{9,8},{10,9},{11,1... | collective-permute-start | bytes 49160 | tf_op jit(solution)/shard_map/ppermute | solution.py:201
  58.6 1.1 collective-permute-done.12
  59.7 0.5 reshape.61
  60.3 0.5 reshape.63
  61.2 2.0 %collective-permute-start.15 = (f32[4,16,4,128]{3,2,1,0:T(4,128)S(1)}, f32[4,16,4,128]{3,2,1,0:T(4,128)S(1)}, u32[]{:S(2)}, u32[]{:S(2)}) collective-permute-start(f32[4,16,4,128]{3,2,1,0:T(4,128)S(1)} %get-tuple-element.13), channel_id=1, source_target_pairs={{4,0},{8,4},{12,8},{16,12},{20,16},{24,20},{28,24},{0,28},{5,1},{9... | collective-permute-start | bytes 393224 | tf_op jit(solution)/shard_map/ppermute | solution.py:203
  63.2 4.0 %collective-permute-done.14 = f32[4,16,4,128]{3,2,1,0:T(4,128)S(1)} collective-permute-done((f32[4,16,4,128]{3,2,1,0:T(4,128)S(1)}, f32[4,16,4,128]{3,2,1,0:T(4,128)S(1)}, u32[]{:S(2)}, u32[]{:S(2)}) %collective-permute-start.14) | collective-permute-done | bytes 131104 | tf_op jit(solution)/shard_map/ppermute | solution.py:203
  67.1 3.9 %collective-permute-done.15 = f32[4,16,4,128]{3,2,1,0:T(4,128)S(1)} collective-permute-done((f32[4,16,4,128]{3,2,1,0:T(4,128)S(1)}, f32[4,16,4,128]{3,2,1,0:T(4,128)S(1)}, u32[]{:S(2)}, u32[]{:S(2)}) %collective-permute-start.15) | collective-permute-done | bytes 131104 | tf_op jit(solution)/shard_map/ppermute | solution.py:203
  71.1 0.3 collective-permute-start.16
  71.4 1.7 %collective-permute-start.17 = (f32[4,4,8,128]{3,2,1,0:T(8,128)S(1)}, f32[4,4,8,128]{3,2,1,0:T(8,128)S(1)}, u32[]{:S(2)}, u32[]{:S(2)}) collective-permute-start(f32[4,4,8,128]{3,2,1,0:T(8,128)S(1)} %get-tuple-element.17), channel_id=1, source_target_pairs={{32,0},{64,32},{96,64},{0,96},{33,1},{65,33},{97,65},{1,97},{34,2}... | collective-permute-start | bytes 196616 | tf_op jit(solution)/shard_map/ppermute | solution.py:203
  73.2 2.2 %collective-permute-done.16 = f32[4,4,8,128]{3,2,1,0:T(8,128)S(1)} collective-permute-done((f32[4,4,8,128]{3,2,1,0:T(8,128)S(1)}, f32[4,4,8,128]{3,2,1,0:T(8,128)S(1)}, u32[]{:S(2)}, u32[]{:S(2)}) %collective-permute-start.16) | collective-permute-done | bytes 65568 | tf_op jit(solution)/shard_map/ppermute | solution.py:203
  75.4 1.5 %collective-permute-done.17 = f32[4,4,8,128]{3,2,1,0:T(8,128)S(1)} collective-permute-done((f32[4,4,8,128]{3,2,1,0:T(8,128)S(1)}, f32[4,4,8,128]{3,2,1,0:T(8,128)S(1)}, u32[]{:S(2)}, u32[]{:S(2)}) %collective-permute-start.17) | collective-permute-done | bytes 65568 | tf_op jit(solution)/shard_map/ppermute | solution.py:203
  77.0 12.8 %shard_map.62 = f32[4,16,16,256]{3,2,1,0:T(8,128)S(1)} custom-call(f32[8,8,128]{2,1,0:T(8,128)S(1)} %slice_bitcast_fusion.1.adjoint_ref, f32[3,8,8,128]{3,2,1,0:T(8,128)S(1)} %get-tuple-element.5.grad_ref, s32[2,2,3,8,8,128]{5,4,3,2,1,0:T(8,128)S(1)} %copy-done, f32[2,2,3,8,8,128]{5,4,3,2,1,0:T(8,128)S(1)} %copy-done.1), custom_call_target="tpu_custom_call" | custom-call | tf_op jit(solution)/shard_map/pallas_call | solution.py:183
  90.2 0.3 collective-permute-start.18
  90.8 1.8 %collective-permute-start.19 = (f32[32,128]{1,0:T(8,128)S(1)}, f32[32,128]{1,0:T(8,128)S(1)}, u32[]{:S(2)}, u32[]{:S(2)}) collective-permute-start(f32[32,128]{1,0:T(8,128)S(1)} %reshape.66), channel_id=1, source_target_pairs={{1,0},{2,1},{3,2},{0,3},{5,4},{6,5},{7,6},{4,7},{9,8},{10,9},{11,1... | collective-permute-start | bytes 49160 | tf_op jit(solution)/shard_map/ppermute | solution.py:201
  92.6 1.1 collective-permute-done.18
  93.7 0.5 reshape.65
  94.2 0.5 reshape.67
  95.1 2.0 %collective-permute-start.21 = (f32[4,16,4,128]{3,2,1,0:T(4,128)S(1)}, f32[4,16,4,128]{3,2,1,0:T(4,128)S(1)}, u32[]{:S(2)}, u32[]{:S(2)}) collective-permute-start(f32[4,16,4,128]{3,2,1,0:T(4,128)S(1)} %get-tuple-element.11), channel_id=1, source_target_pairs={{4,0},{8,4},{12,8},{16,12},{20,16},{24,20},{28,24},{0,28},{5,1},{9... | collective-permute-start | bytes 393224 | tf_op jit(solution)/shard_map/ppermute | solution.py:203
  97.1 3.9 %collective-permute-done.20 = f32[4,16,4,128]{3,2,1,0:T(4,128)S(1)} collective-permute-done((f32[4,16,4,128]{3,2,1,0:T(4,128)S(1)}, f32[4,16,4,128]{3,2,1,0:T(4,128)S(1)}, u32[]{:S(2)}, u32[]{:S(2)}) %collective-permute-start.20) | collective-permute-done | bytes 131104 | tf_op jit(solution)/shard_map/ppermute | solution.py:203
  101.0 3.7 %collective-permute-done.21 = f32[4,16,4,128]{3,2,1,0:T(4,128)S(1)} collective-permute-done((f32[4,16,4,128]{3,2,1,0:T(4,128)S(1)}, f32[4,16,4,128]{3,2,1,0:T(4,128)S(1)}, u32[]{:S(2)}, u32[]{:S(2)}) %collective-permute-start.21) | collective-permute-done | bytes 131104 | tf_op jit(solution)/shard_map/ppermute | solution.py:203
  104.9 2.0 %collective-permute-start.23 = (f32[4,4,8,128]{3,2,1,0:T(8,128)S(1)}, f32[4,4,8,128]{3,2,1,0:T(8,128)S(1)}, u32[]{:S(2)}, u32[]{:S(2)}) collective-permute-start(f32[4,4,8,128]{3,2,1,0:T(8,128)S(1)} %get-tuple-element.15), channel_id=1, source_target_pairs={{32,0},{64,32},{96,64},{0,96},{33,1},{65,33},{97,65},{1,97},{34,2}... | collective-permute-start | bytes 196616 | tf_op jit(solution)/shard_map/ppermute | solution.py:203
  106.9 2.2 %collective-permute-done.22 = f32[4,4,8,128]{3,2,1,0:T(8,128)S(1)} collective-permute-done((f32[4,4,8,128]{3,2,1,0:T(8,128)S(1)}, f32[4,4,8,128]{3,2,1,0:T(8,128)S(1)}, u32[]{:S(2)}, u32[]{:S(2)}) %collective-permute-start.22) | collective-permute-done | bytes 65568 | tf_op jit(solution)/shard_map/ppermute | solution.py:203
  109.2 1.3 %collective-permute-done.23 = f32[4,4,8,128]{3,2,1,0:T(8,128)S(1)} collective-permute-done((f32[4,4,8,128]{3,2,1,0:T(8,128)S(1)}, f32[4,4,8,128]{3,2,1,0:T(8,128)S(1)}, u32[]{:S(2)}, u32[]{:S(2)}) %collective-permute-start.23) | collective-permute-done | bytes 65568 | tf_op jit(solution)/shard_map/ppermute | solution.py:203
  110.5 0.7 slice_add_fusion.5
  111.1 0.6 slice_bitcast_fusion
  (61 shorter events, 4.5 us)
Async XLA Ops:
  1.4 3.7 %copy-start.3 = (f32[8,8,128]{2,1,0:T(8,128)S(1)}, f32[8,8,128]{2,1,0:T(8,128)}, u32[]{:S(2)}) copy-start(f32[8,8,128]{2,1,0:T(8,128)} %param.4) | copy-start | bytes 98308
  1.4 3.7 %collective-permute-start = (f32[4,8,128]{2,1,0:T(8,128)S(1)}, f32[4,8,128]{2,1,0:T(8,128)S(1)}, u32[]{:S(2)}, u32[]{:S(2)}) collective-permute-start(f32[4,8,128]{2,1,0:T(8,128)S(1)} %get-tuple-element.29), channel_id=1, source_target_pairs={{0,32},{32,64},{64,96},{96,0},{1,33},{33,65},{65,97},{97,1},{2,34}... | collective-permute-start | bytes 49160 | tf_op jit(solution)/shard_map/ppermute | solution.py:203
  1.9 4.9 %collective-permute-start.1 = (f32[4,8,128]{2,1,0:T(8,128)S(1)}, f32[4,8,128]{2,1,0:T(8,128)S(1)}, u32[]{:S(2)}, u32[]{:S(2)}) collective-permute-start(f32[4,8,128]{2,1,0:T(8,128)S(1)} %get-tuple-element.28), channel_id=1, source_target_pairs={{32,0},{64,32},{96,64},{0,96},{33,1},{65,33},{97,65},{1,97},{34,2}... | collective-permute-start | bytes 49160 | tf_op jit(solution)/shard_map/ppermute | solution.py:203
  6.8 4.0 %collective-permute-start.2 = (f32[16,4,128]{2,1,0:T(4,128)S(1)}, f32[16,4,128]{2,1,0:T(4,128)S(1)}, u32[]{:S(2)}, u32[]{:S(2)}) collective-permute-start(f32[16,4,128]{2,1,0:T(4,128)S(1)} %get-tuple-element.24), channel_id=1, source_target_pairs={{0,4},{4,8},{8,12},{12,16},{16,20},{20,24},{24,28},{28,0},{1,5},{5... | collective-permute-start | bytes 98312 | tf_op jit(solution)/shard_map/ppermute | solution.py:203
  8.7 7.5 %collective-permute-start.3 = (f32[16,4,128]{2,1,0:T(4,128)S(1)}, f32[16,4,128]{2,1,0:T(4,128)S(1)}, u32[]{:S(2)}, u32[]{:S(2)}) collective-permute-start(f32[16,4,128]{2,1,0:T(4,128)S(1)} %get-tuple-element.25), channel_id=1, source_target_pairs={{4,0},{8,4},{12,8},{16,12},{20,16},{24,20},{28,24},{0,28},{5,1},{9... | collective-permute-start | bytes 98312 | tf_op jit(solution)/shard_map/ppermute | solution.py:203
  16.5 1.4 %collective-permute-start.4 = (f32[8,128]{1,0:T(8,128)S(1)}, f32[8,128]{1,0:T(8,128)S(1)}, u32[]{:S(2)}, u32[]{:S(2)}) collective-permute-start(f32[8,128]{1,0:T(8,128)S(1)} %reshape.52), channel_id=1, source_target_pairs={{1,0},{2,1},{3,2},{0,3},{5,4},{6,5},{7,6},{4,7},{9,8},{10,9},{11,1... | collective-permute-start | bytes 12296 | tf_op jit(solution)/shard_map/ppermute | solution.py:201
  16.7 3.1 %collective-permute-start.5 = (f32[8,128]{1,0:T(8,128)S(1)}, f32[8,128]{1,0:T(8,128)S(1)}, u32[]{:S(2)}, u32[]{:S(2)}) collective-permute-start(f32[8,128]{1,0:T(8,128)S(1)} %reshape.54), channel_id=1, source_target_pairs={{0,1},{1,2},{2,3},{3,0},{4,5},{5,6},{6,7},{7,4},{8,9},{9,10},{10,1... | collective-permute-start | bytes 12296 | tf_op jit(solution)/shard_map/ppermute | solution.py:201
  18.0 2.0 %copy-start = (s32[2,2,3,8,8,128]{5,4,3,2,1,0:T(8,128)S(1)}, s32[2,2,3,8,8,128]{5,4,3,2,1,0:T(8,128)}, u32[]{:S(2)}) copy-start(s32[2,2,3,8,8,128]{5,4,3,2,1,0:T(8,128)} %cells_ref.7) | copy-start | bytes 1179652
  18.1 2.0 %copy-start.1 = (f32[2,2,3,8,8,128]{5,4,3,2,1,0:T(8,128)S(1)}, f32[2,2,3,8,8,128]{5,4,3,2,1,0:T(8,128)}, u32[]{:S(2)}) copy-start(f32[2,2,3,8,8,128]{5,4,3,2,1,0:T(8,128)} %fracs_ref.7) | copy-start | bytes 1179652
  24.3 3.8 %collective-permute-start.6 = (f32[4,8,128]{2,1,0:T(8,128)S(1)}, f32[4,8,128]{2,1,0:T(8,128)S(1)}, u32[]{:S(2)}, u32[]{:S(2)}) collective-permute-start(f32[4,8,128]{2,1,0:T(8,128)S(1)} %get-tuple-element.27), channel_id=1, source_target_pairs={{0,32},{32,64},{64,96},{96,0},{1,33},{33,65},{65,97},{97,1},{2,34}... | collective-permute-start | bytes 49160 | tf_op jit(solution)/shard_map/ppermute | solution.py:203
  24.6 4.9 %collective-permute-start.7 = (f32[4,8,128]{2,1,0:T(8,128)S(1)}, f32[4,8,128]{2,1,0:T(8,128)S(1)}, u32[]{:S(2)}, u32[]{:S(2)}) collective-permute-start(f32[4,8,128]{2,1,0:T(8,128)S(1)} %get-tuple-element.26), channel_id=1, source_target_pairs={{32,0},{64,32},{96,64},{0,96},{33,1},{65,33},{97,65},{1,97},{34,2}... | collective-permute-start | bytes 49160 | tf_op jit(solution)/shard_map/ppermute | solution.py:203
  29.6 4.0 %collective-permute-start.8 = (f32[16,4,128]{2,1,0:T(4,128)S(1)}, f32[16,4,128]{2,1,0:T(4,128)S(1)}, u32[]{:S(2)}, u32[]{:S(2)}) collective-permute-start(f32[16,4,128]{2,1,0:T(4,128)S(1)} %get-tuple-element.22), channel_id=1, source_target_pairs={{0,4},{4,8},{8,12},{12,16},{16,20},{20,24},{24,28},{28,0},{1,5},{5... | collective-permute-start | bytes 98312 | tf_op jit(solution)/shard_map/ppermute | solution.py:203
  29.7 7.6 %collective-permute-start.9 = (f32[16,4,128]{2,1,0:T(4,128)S(1)}, f32[16,4,128]{2,1,0:T(4,128)S(1)}, u32[]{:S(2)}, u32[]{:S(2)}) collective-permute-start(f32[16,4,128]{2,1,0:T(4,128)S(1)} %get-tuple-element.23), channel_id=1, source_target_pairs={{4,0},{8,4},{12,8},{16,12},{20,16},{24,20},{28,24},{0,28},{5,1},{9... | collective-permute-start | bytes 98312 | tf_op jit(solution)/shard_map/ppermute | solution.py:203
  37.5 4.4 %collective-permute-start.10 = (f32[8,128]{1,0:T(8,128)S(1)}, f32[8,128]{1,0:T(8,128)S(1)}, u32[]{:S(2)}, u32[]{:S(2)}) collective-permute-start(f32[8,128]{1,0:T(8,128)S(1)} %reshape.56), channel_id=1, source_target_pairs={{1,0},{2,1},{3,2},{0,3},{5,4},{6,5},{7,6},{4,7},{9,8},{10,9},{11,1... | collective-permute-start | bytes 12296 | tf_op jit(solution)/shard_map/ppermute | solution.py:201
  37.6 0.9 copy-start.2
  37.8 4.4 %collective-permute-start.11 = (f32[8,128]{1,0:T(8,128)S(1)}, f32[8,128]{1,0:T(8,128)S(1)}, u32[]{:S(2)}, u32[]{:S(2)}) collective-permute-start(f32[8,128]{1,0:T(8,128)S(1)} %reshape.58), channel_id=1, source_target_pairs={{0,1},{1,2},{2,3},{3,0},{4,5},{5,6},{6,7},{7,4},{8,9},{9,10},{10,1... | collective-permute-start | bytes 12296 | tf_op jit(solution)/shard_map/ppermute | solution.py:201
  56.5 3.2 %collective-permute-start.12 = (f32[32,128]{1,0:T(8,128)S(1)}, f32[32,128]{1,0:T(8,128)S(1)}, u32[]{:S(2)}, u32[]{:S(2)}) collective-permute-start(f32[32,128]{1,0:T(8,128)S(1)} %reshape.60), channel_id=1, source_target_pairs={{0,1},{1,2},{2,3},{3,0},{4,5},{5,6},{6,7},{7,4},{8,9},{9,10},{10,1... | collective-permute-start | bytes 49160 | tf_op jit(solution)/shard_map/ppermute | solution.py:201
  57.2 3.0 %collective-permute-start.13 = (f32[32,128]{1,0:T(8,128)S(1)}, f32[32,128]{1,0:T(8,128)S(1)}, u32[]{:S(2)}, u32[]{:S(2)}) collective-permute-start(f32[32,128]{1,0:T(8,128)S(1)} %reshape.62), channel_id=1, source_target_pairs={{1,0},{2,1},{3,2},{0,3},{5,4},{6,5},{7,6},{4,7},{9,8},{10,9},{11,1... | collective-permute-start | bytes 49160 | tf_op jit(solution)/shard_map/ppermute | solution.py:201
  61.1 6.1 %collective-permute-start.14 = (f32[4,16,4,128]{3,2,1,0:T(4,128)S(1)}, f32[4,16,4,128]{3,2,1,0:T(4,128)S(1)}, u32[]{:S(2)}, u32[]{:S(2)}) collective-permute-start(f32[4,16,4,128]{3,2,1,0:T(4,128)S(1)} %get-tuple-element.12), channel_id=1, source_target_pairs={{0,4},{4,8},{8,12},{12,16},{16,20},{20,24},{24,28},{28,0},{1,5},{5... | collective-permute-start | bytes 393224 | tf_op jit(solution)/shard_map/ppermute | solution.py:203
  61.2 9.8 %collective-permute-start.15 = (f32[4,16,4,128]{3,2,1,0:T(4,128)S(1)}, f32[4,16,4,128]{3,2,1,0:T(4,128)S(1)}, u32[]{:S(2)}, u32[]{:S(2)}) collective-permute-start(f32[4,16,4,128]{3,2,1,0:T(4,128)S(1)} %get-tuple-element.13), channel_id=1, source_target_pairs={{4,0},{8,4},{12,8},{16,12},{20,16},{24,20},{28,24},{0,28},{5,1},{9... | collective-permute-start | bytes 393224 | tf_op jit(solution)/shard_map/ppermute | solution.py:203
  71.1 4.3 %collective-permute-start.16 = (f32[4,4,8,128]{3,2,1,0:T(8,128)S(1)}, f32[4,4,8,128]{3,2,1,0:T(8,128)S(1)}, u32[]{:S(2)}, u32[]{:S(2)}) collective-permute-start(f32[4,4,8,128]{3,2,1,0:T(8,128)S(1)} %get-tuple-element.16), channel_id=1, source_target_pairs={{0,32},{32,64},{64,96},{96,0},{1,33},{33,65},{65,97},{97,1},{2,34}... | collective-permute-start | bytes 196616 | tf_op jit(solution)/shard_map/ppermute | solution.py:203
  71.4 5.5 %collective-permute-start.17 = (f32[4,4,8,128]{3,2,1,0:T(8,128)S(1)}, f32[4,4,8,128]{3,2,1,0:T(8,128)S(1)}, u32[]{:S(2)}, u32[]{:S(2)}) collective-permute-start(f32[4,4,8,128]{3,2,1,0:T(8,128)S(1)} %get-tuple-element.17), channel_id=1, source_target_pairs={{32,0},{64,32},{96,64},{0,96},{33,1},{65,33},{97,65},{1,97},{34,2}... | collective-permute-start | bytes 196616 | tf_op jit(solution)/shard_map/ppermute | solution.py:203
  90.2 3.5 %collective-permute-start.18 = (f32[32,128]{1,0:T(8,128)S(1)}, f32[32,128]{1,0:T(8,128)S(1)}, u32[]{:S(2)}, u32[]{:S(2)}) collective-permute-start(f32[32,128]{1,0:T(8,128)S(1)} %reshape.64), channel_id=1, source_target_pairs={{0,1},{1,2},{2,3},{3,0},{4,5},{5,6},{6,7},{7,4},{8,9},{9,10},{10,1... | collective-permute-start | bytes 49160 | tf_op jit(solution)/shard_map/ppermute | solution.py:201
  90.8 3.4 %collective-permute-start.19 = (f32[32,128]{1,0:T(8,128)S(1)}, f32[32,128]{1,0:T(8,128)S(1)}, u32[]{:S(2)}, u32[]{:S(2)}) collective-permute-start(f32[32,128]{1,0:T(8,128)S(1)} %reshape.66), channel_id=1, source_target_pairs={{1,0},{2,1},{3,2},{0,3},{5,4},{6,5},{7,6},{4,7},{9,8},{10,9},{11,1... | collective-permute-start | bytes 49160 | tf_op jit(solution)/shard_map/ppermute | solution.py:201
  95.0 6.0 %collective-permute-start.20 = (f32[4,16,4,128]{3,2,1,0:T(4,128)S(1)}, f32[4,16,4,128]{3,2,1,0:T(4,128)S(1)}, u32[]{:S(2)}, u32[]{:S(2)}) collective-permute-start(f32[4,16,4,128]{3,2,1,0:T(4,128)S(1)} %get-tuple-element.10), channel_id=1, source_target_pairs={{0,4},{4,8},{8,12},{12,16},{16,20},{20,24},{24,28},{28,0},{1,5},{5... | collective-permute-start | bytes 393224 | tf_op jit(solution)/shard_map/ppermute | solution.py:203
  95.1 9.6 %collective-permute-start.21 = (f32[4,16,4,128]{3,2,1,0:T(4,128)S(1)}, f32[4,16,4,128]{3,2,1,0:T(4,128)S(1)}, u32[]{:S(2)}, u32[]{:S(2)}) collective-permute-start(f32[4,16,4,128]{3,2,1,0:T(4,128)S(1)} %get-tuple-element.11), channel_id=1, source_target_pairs={{4,0},{8,4},{12,8},{16,12},{20,16},{24,20},{28,24},{0,28},{5,1},{9... | collective-permute-start | bytes 393224 | tf_op jit(solution)/shard_map/ppermute | solution.py:203
  104.8 4.3 %collective-permute-start.22 = (f32[4,4,8,128]{3,2,1,0:T(8,128)S(1)}, f32[4,4,8,128]{3,2,1,0:T(8,128)S(1)}, u32[]{:S(2)}, u32[]{:S(2)}) collective-permute-start(f32[4,4,8,128]{3,2,1,0:T(8,128)S(1)} %get-tuple-element.14), channel_id=1, source_target_pairs={{0,32},{32,64},{64,96},{96,0},{1,33},{33,65},{65,97},{97,1},{2,34}... | collective-permute-start | bytes 196616 | tf_op jit(solution)/shard_map/ppermute | solution.py:203
  104.9 5.5 %collective-permute-start.23 = (f32[4,4,8,128]{3,2,1,0:T(8,128)S(1)}, f32[4,4,8,128]{3,2,1,0:T(8,128)S(1)}, u32[]{:S(2)}, u32[]{:S(2)}) collective-permute-start(f32[4,4,8,128]{3,2,1,0:T(8,128)S(1)} %get-tuple-element.15), channel_id=1, source_target_pairs={{32,0},{64,32},{96,64},{0,96},{33,1},{65,33},{97,65},{1,97},{34,2}... | collective-permute-start | bytes 196616 | tf_op jit(solution)/shard_map/ppermute | solution.py:203
where the time goes:
time: 112 us
  waiting for transfers between devices  46.6 us (42%)
  Pallas kernels  34.1 us (30%)
  starting transfers between devices  22.1 us (20%)
  local copies, waits for them, and re-layouts  6.2 us (6%)
  other arithmetic  1.74 us (2%)
    ppermute x16, waiting for transfers between devices, shift_from(): return lax.ppermute(piece, axis, pairs)  42.2 us
    pallas_call x4, Pallas kernels, vmem_call(): pl.pallas_call(kernel, out_shape=out_shapes, in_specs=[pl.BlockSpec(memor...  34.1 us
    ppermute x16, starting transfers between devices, shift_from(): return lax.ppermute(piece, axis, pairs)  16.7 us
    ppermute x8, starting transfers between devices, shift_from(): flat = lax.ppermute(piece.reshape(-1, 128), axis, pairs)  5.42 us
    ppermute x8, waiting for transfers between devices, shift_from(): flat = lax.ppermute(piece.reshape(-1, 128), axis, pairs)  4.47 us
    reshape x8, local copies, waits for them, and re-layouts, shift_from(): return flat.reshape(shape)  2.64 us
  transfers between devices with their start and end apart: 24, of which 20 were waited for; matrix products, arithmetic and copies ran while one was open for 2% of the time, Pallas kernels for 3%

commit v1 on v0

--- a/solution.py
+++ b/solution.py
@@ -203,21 +203,83 @@
     return lax.ppermute(piece, axis, pairs)
 
 
+def neighbour_ids():
+    here = [lax.axis_index(axis) for axis, _ in AXES]
+    ids = []
+    for position, (axis, _) in enumerate(AXES):
+        count = lax.axis_size(axis)
+        for step in (1, count - 1):
+            target = list(here)
+            target[position] = lax.rem(here[position] + step, count)
+            ids.append(tuple(target))
+    return ids
+
+
+def widen_kernel(block_ref, out_ref, recv_x, recv_y, recv_z, wide_x, wide_y, send_sems,
+                 recv_sems):
+    nx, ny, nz = block_ref.shape
+    mesh = pl.DeviceIdType.MESH
+    ids = neighbour_ids()
+    barrier = pltpu.get_barrier_semaphore()
+    for target in ids:
+        pl.semaphore_signal(barrier, inc=1, device_id=target, device_id_type=mesh)
+    pl.semaphore_wait(barrier, len(ids))
+
+    def exchange(stage, source, landing):
+        copies = []
+        for side in range(2):
+            copy = pltpu.make_async_remote_copy(
+                src_ref=source,
+                dst_ref=landing.at[side],
+                send_sem=send_sems.at[2 * stage + side],
+                recv_sem=recv_sems.at[2 * stage + side],
+                device_id=ids[2 * stage + side],
+                device_id_type=mesh,
+            )
+            copy.start()
+            copies.append(copy)
+        for copy in copies:
+            copy.wait()
+
+    exchange(0, block_ref, recv_x)
+    wide_x[0:MARGIN] = recv_x[0, nx - MARGIN : nx]
+    wide_x[MARGIN : MARGIN + nx] = block_ref[...]
+    wide_x[MARGIN + nx :] = recv_x[1, 0:MARGIN]
+    exchange(1, wide_x, recv_y)
+    wide_y[:, 0:ny] = recv_y[0]
+    wide_y[:, ny : 2 * ny] = wide_x[...]
+    wide_y[:, 2 * ny :] = recv_y[1]
+    exchange(2, wide_y, recv_z)
+    rows = slice(ny - MARGIN, 2 * ny + MARGIN)
+    out_ref[:, :, 0:nz] = wide_y[:, rows, :]
+    lane = lax.broadcasted_iota(jnp.int32, out_ref.shape[:2] + (nz,), 2)
+    above = recv_z[1, :, rows, :]
+    below = recv_z[0, :, rows, :]
+    out_ref[:, :, nz:] = jnp.where(
+        lane < MARGIN, above, jnp.where(lane >= nz - MARGIN, below, 0.0)
+    )
+
+
 def widen(block, pz):
-    for axis, dim in AXES[:2]:
-        size = block.shape[dim]
-        head = lax.slice_in_dim(block, 0, MARGIN, axis=dim)
-        tail = lax.slice_in_dim(block, size - MARGIN, size, axis=dim)
-        block = jnp.concatenate(
-            [shift_from(tail, axis, True), block, shift_from(head, axis, False)], axis=dim
-        )
-    nz = block.shape[2]
-    head = block[:, :, :MARGIN]
-    tail = block[:, :, nz - MARGIN :]
-    gap = jnp.zeros(block.shape[:2] + (pz - nz - 2 * MARGIN,), jnp.float32)
-    return jnp.concatenate(
-        [block, shift_from(head, "gz", False), gap, shift_from(tail, "gz", True)], axis=2
-    )
+    nx, ny, nz = block.shape
+    px = nx + 2 * MARGIN
+    f32 = jnp.float32
+    return pl.pallas_call(
+        widen_kernel,
+        out_shape=jax.ShapeDtypeStruct((px, ny + 2 * MARGIN, pz), f32),
+        in_specs=[pl.BlockSpec(memory_space=pltpu.VMEM)],
+        out_specs=pl.BlockSpec(memory_space=pltpu.VMEM),
+        scratch_shapes=[
+            pltpu.VMEM((2, nx, ny, nz), f32),
+            pltpu.VMEM((2, px, ny, nz), f32),
+            pltpu.VMEM((2, px, 3 * ny, nz), f32),
+            pltpu.VMEM((px, ny, nz), f32),
+            pltpu.VMEM((px, 3 * ny, nz), f32),
+            pltpu.SemaphoreType.DMA((6,)),
+            pltpu.SemaphoreType.DMA((6,)),
+        ],
+        compiler_params=pltpu.CompilerParams(collective_id=0, has_side_effects=True),
+    )(block)
 
 
 def place_rim(rim, dim, start, size):

time: 112 us -> 120 us (1.071)
  Pallas kernels: 34.1 us -> 68.5 us
  waiting for transfers between devices: 46.6 us -> 27.8 us
  starting transfers between devices: 22.1 us -> 12.3 us
  local copies, waits for them, and re-layouts: 6.2 us -> 7.7 us
    pallas_call x0 -> x2, Pallas kernels: none -> 34.4 us  [widen(): pl.pallas_call(widen_kernel, out_shape=jax.ShapeDtypeStruct((px, ny + 2 *...]
    ppermute x16 -> x8, waiting for transfers between devices: 42.2 us -> 25.7 us  [shift_from(): return lax.ppermute(piece, axis, pairs)]
    ppermute x16 -> x8, starting transfers between devices: 16.7 us -> 8.37 us  [shift_from(): return lax.ppermute(piece, axis, pairs)]
    unnamed x12 -> x16, local copies, waits for them, and re-layouts: 0.03 us -> 3.56 us
    ppermute x8 -> x4, waiting for transfers between devices: 4.47 us -> 2.16 us  [shift_from(): flat = lax.ppermute(piece.reshape(-1, 128), axis, pairs)]
    ppermute x8 -> x4, starting transfers between devices: 5.42 us -> 3.93 us  [shift_from(): flat = lax.ppermute(piece.reshape(-1, 128), axis, pairs)]
    reshape x8 -> x4, local copies, waits for them, and re-layouts: 2.64 us -> 2.12 us  [shift_from(): return flat.reshape(shape)]
  transfers between devices with their start and end apart: 24 -> 12, of which waited for: 20 -> 10; matrix products, arithmetic and copies ran while one was open for 2% -> 1% of each run, Pallas kernels for 3% -> 0%
where the time goes in v1:
time: 120 us; the launch traced here: 119 us
  Pallas kernels  68.5 us (57%)
  waiting for transfers between devices  27.8 us (23%)
  starting transfers between devices  12.3 us (10%)
  local copies, waits for them, and re-layouts  7.7 us (6%)
  other arithmetic  1.47 us (1%)
    pallas_call x2, Pallas kernels, widen(): pl.pallas_call(widen_kernel, out_shape=jax.ShapeDtypeStruct((px, ny + 2 *...  34.4 us
    pallas_call x4, Pallas kernels, vmem_call(): pl.pallas_call(kernel, out_shape=out_shapes, in_specs=[pl.BlockSpec(memor...  34.1 us
    ppermute x8, waiting for transfers between devices, shift_from(): return lax.ppermute(piece, axis, pairs)  25.7 us
    ppermute x8, starting transfers between devices, shift_from(): return lax.ppermute(piece, axis, pairs)  8.37 us
    ppermute x4, starting transfers between devices, shift_from(): flat = lax.ppermute(piece.reshape(-1, 128), axis, pairs)  3.93 us
    unnamed x16, local copies, waits for them, and re-layouts  3.56 us
  transfers between devices with their start and end apart: 12, of which 10 were waited for; matrix products, arithmetic and copies ran while one was open for 1% of the time, Pallas kernels for 0%

profile of v1, /device:TPU:102, one launch (start us, length us, event | category | flops | bytes accessed | tf_op | source)
XLA Modules:
  0.0 118.7 jit_solution(15136365043914854949)
XLA Ops:
  0.6 15.5 %shard_map.60.wrapped_ref = f32[16,16,256]{2,1,0:T(8,128)} custom-call(f32[8,8,128]{2,1,0:T(8,128)} %block_ref.1), custom_call_target="tpu_custom_call" | custom-call | tf_op jit(solution)/shard_map/pallas_call | solution.py:267
  16.1 1.0 copy-done
  17.1 1.0 copy-done.2
  18.1 0.9 copy-done.5
  19.1 4.2 %shard_map.61 = (f32[8,8,128]{2,1,0:T(8,128)S(1)}, f32[3,8,8,128]{3,2,1,0:T(8,128)S(1)}) custom-call(f32[16,16,256]{2,1,0:T(8,128)S(1)} %copy-done.5, s32[2,2,3,8,8,128]{5,4,3,2,1,0:T(8,128)S(1)} %copy-done, f32[2,2,3,8,8,128]{5,4,3,2,1,0:T(8,128)S(1)} %copy-done.2), custom_call_target="tpu_custom_call" | custom-call | tf_op jit(solution)/shard_map/pallas_call | solution.py:183
  23.3 0.6 copy-done.7
  23.9 18.9 %shard_map.62.wrapped_ref = f32[16,16,256]{2,1,0:T(8,128)} custom-call(f32[8,8,128]{2,1,0:T(8,128)} %copy-done.7), custom_call_target="tpu_custom_call" | custom-call | tf_op jit(solution)/shard_map/pallas_call | solution.py:267
  42.9 3.5 %shard_map.59 = f32[16,16,256]{2,1,0:T(8,128)S(1)} custom-call(f32[8,8,128]{2,1,0:T(8,128)S(1)} %copy-done.6, s32[2,2,3,8,8,128]{5,4,3,2,1,0:T(8,128)S(1)} %copy-done.1, f32[2,2,3,8,8,128]{5,4,3,2,1,0:T(8,128)S(1)} %copy-done.3), custom_call_target="tpu_custom_call" | custom-call | tf_op jit(solution)/shard_map/pallas_call | solution.py:183
  46.3 13.6 %shard_map.63 = f32[3,16,16,256]{3,2,1,0:T(8,128)S(1)} custom-call(f32[16,16,256]{2,1,0:T(8,128)S(1)} %copy-done.4, f32[8,8,128]{2,1,0:T(8,128)S(1)} %copy-done.6, s32[2,2,3,8,8,128]{5,4,3,2,1,0:T(8,128)S(1)} %copy-done.1, f32[2,2,3,8,8,128]{5,4,3,2,1,0:T(8,128)S(1)} %copy-done.3), custom_call_target="tpu_custom_call" | custom-call | tf_op jit(solution)/shard_map/pallas_call | solution.py:183
  60.0 0.2 fusion
  60.2 0.3 reshape.28
  60.4 0.4 collective-permute-start
  60.8 0.3 reshape.30
  61.1 1.7 %collective-permute-start.1 = (f32[32,128]{1,0:T(8,128)S(1)}, f32[32,128]{1,0:T(8,128)S(1)}, u32[]{:S(2)}, u32[]{:S(2)}) collective-permute-start(f32[32,128]{1,0:T(8,128)S(1)} %reshape.30), channel_id=1, source_target_pairs={{1,0},{2,1},{3,2},{0,3},{5,4},{6,5},{7,6},{4,7},{9,8},{10,9},{11,1... | collective-permute-start | bytes 49160 | tf_op jit(solution)/shard_map/ppermute | solution.py:201
  62.8 1.1 collective-permute-done
  63.8 0.5 reshape.29
  64.4 0.5 reshape.31
  64.9 0.2 fusion.3
  65.2 1.7 %collective-permute-start.2 = (f32[4,16,4,128]{3,2,1,0:T(4,128)S(1)}, f32[4,16,4,128]{3,2,1,0:T(4,128)S(1)}, u32[]{:S(2)}, u32[]{:S(2)}) collective-permute-start(f32[4,16,4,128]{3,2,1,0:T(4,128)S(1)} %get-tuple-element.12), channel_id=1, source_target_pairs={{0,4},{4,8},{8,12},{12,16},{16,20},{20,24},{24,28},{28,0},{1,5},{5... | collective-permute-start | bytes 393224 | tf_op jit(solution)/shard_map/ppermute | solution.py:203
  66.9 0.4 collective-permute-start.3
  67.3 3.6 %collective-permute-done.2 = f32[4,16,4,128]{3,2,1,0:T(4,128)S(1)} collective-permute-done((f32[4,16,4,128]{3,2,1,0:T(4,128)S(1)}, f32[4,16,4,128]{3,2,1,0:T(4,128)S(1)}, u32[]{:S(2)}, u32[]{:S(2)}) %collective-permute-start.2) | collective-permute-done | bytes 131104 | tf_op jit(solution)/shard_map/ppermute | solution.py:203
  70.9 5.8 %collective-permute-done.3 = f32[4,16,4,128]{3,2,1,0:T(4,128)S(1)} collective-permute-done((f32[4,16,4,128]{3,2,1,0:T(4,128)S(1)}, f32[4,16,4,128]{3,2,1,0:T(4,128)S(1)}, u32[]{:S(2)}, u32[]{:S(2)}) %collective-permute-start.3) | collective-permute-done | bytes 131104 | tf_op jit(solution)/shard_map/ppermute | solution.py:203
  76.7 0.1 fusion.6
  76.8 1.2 %collective-permute-start.4 = (f32[4,4,8,128]{3,2,1,0:T(8,128)S(1)}, f32[4,4,8,128]{3,2,1,0:T(8,128)S(1)}, u32[]{:S(2)}, u32[]{:S(2)}) collective-permute-start(f32[4,4,8,128]{3,2,1,0:T(8,128)S(1)} %get-tuple-element.16), channel_id=1, source_target_pairs={{0,32},{32,64},{64,96},{96,0},{1,33},{33,65},{65,97},{97,1},{2,34}... | collective-permute-start | bytes 196616 | tf_op jit(solution)/shard_map/ppermute | solution.py:203
  78.1 0.9 collective-permute-start.5
  78.9 2.2 %collective-permute-done.4 = f32[4,4,8,128]{3,2,1,0:T(8,128)S(1)} collective-permute-done((f32[4,4,8,128]{3,2,1,0:T(8,128)S(1)}, f32[4,4,8,128]{3,2,1,0:T(8,128)S(1)}, u32[]{:S(2)}, u32[]{:S(2)}) %collective-permute-start.4) | collective-permute-done | bytes 65568 | tf_op jit(solution)/shard_map/ppermute | solution.py:203
  81.2 2.3 %collective-permute-done.5 = f32[4,4,8,128]{3,2,1,0:T(8,128)S(1)} collective-permute-done((f32[4,4,8,128]{3,2,1,0:T(8,128)S(1)}, f32[4,4,8,128]{3,2,1,0:T(8,128)S(1)}, u32[]{:S(2)}, u32[]{:S(2)}) %collective-permute-start.5) | collective-permute-done | bytes 65568 | tf_op jit(solution)/shard_map/ppermute | solution.py:203
  83.6 12.8 %shard_map.64 = f32[4,16,16,256]{3,2,1,0:T(8,128)S(1)} custom-call(f32[8,8,128]{2,1,0:T(8,128)S(1)} %slice_bitcast_fusion.1.adjoint_ref, f32[3,8,8,128]{3,2,1,0:T(8,128)S(1)} %get-tuple-element.5.grad_ref, s32[2,2,3,8,8,128]{5,4,3,2,1,0:T(8,128)S(1)} %copy-done.1, f32[2,2,3,8,8,128]{5,4,3,2,1,0:T(8,128)S(1)} %copy-done.3), custom_call_target="tpu_custom_call" | custom-call | tf_op jit(solution)/shard_map/pallas_call | solution.py:183
  96.4 0.2 fusion.9
  96.6 0.3 reshape.32
  96.8 0.1 collective-permute-start.6
  96.9 0.3 reshape.34
  97.2 1.8 %collective-permute-start.7 = (f32[32,128]{1,0:T(8,128)S(1)}, f32[32,128]{1,0:T(8,128)S(1)}, u32[]{:S(2)}, u32[]{:S(2)}) collective-permute-start(f32[32,128]{1,0:T(8,128)S(1)} %reshape.34), channel_id=1, source_target_pairs={{1,0},{2,1},{3,2},{0,3},{5,4},{6,5},{7,6},{4,7},{9,8},{10,9},{11,1... | collective-permute-start | bytes 49160 | tf_op jit(solution)/shard_map/ppermute | solution.py:201
  99.0 1.1 collective-permute-done.6
  100.1 0.5 reshape.33
  100.6 0.5 reshape.35
  101.2 0.2 fusion.4
  101.4 0.1 collective-permute-start.8
  101.5 2.0 %collective-permute-start.9 = (f32[4,16,4,128]{3,2,1,0:T(4,128)S(1)}, f32[4,16,4,128]{3,2,1,0:T(4,128)S(1)}, u32[]{:S(2)}, u32[]{:S(2)}) collective-permute-start(f32[4,16,4,128]{3,2,1,0:T(4,128)S(1)} %get-tuple-element.11), channel_id=1, source_target_pairs={{4,0},{8,4},{12,8},{16,12},{20,16},{24,20},{28,24},{0,28},{5,1},{9... | collective-permute-start | bytes 393224 | tf_op jit(solution)/shard_map/ppermute | solution.py:203
  103.5 4.0 %collective-permute-done.8 = f32[4,16,4,128]{3,2,1,0:T(4,128)S(1)} collective-permute-done((f32[4,16,4,128]{3,2,1,0:T(4,128)S(1)}, f32[4,16,4,128]{3,2,1,0:T(4,128)S(1)}, u32[]{:S(2)}, u32[]{:S(2)}) %collective-permute-start.8) | collective-permute-done | bytes 131104 | tf_op jit(solution)/shard_map/ppermute | solution.py:203
  107.5 3.9 %collective-permute-done.9 = f32[4,16,4,128]{3,2,1,0:T(4,128)S(1)} collective-permute-done((f32[4,16,4,128]{3,2,1,0:T(4,128)S(1)}, f32[4,16,4,128]{3,2,1,0:T(4,128)S(1)}, u32[]{:S(2)}, u32[]{:S(2)}) %collective-permute-start.9) | collective-permute-done | bytes 131104 | tf_op jit(solution)/shard_map/ppermute | solution.py:203
  111.4 0.1 fusion.5
  111.5 0.4 collective-permute-start.10
  111.9 1.7 %collective-permute-start.11 = (f32[4,4,8,128]{3,2,1,0:T(8,128)S(1)}, f32[4,4,8,128]{3,2,1,0:T(8,128)S(1)}, u32[]{:S(2)}, u32[]{:S(2)}) collective-permute-start(f32[4,4,8,128]{3,2,1,0:T(8,128)S(1)} %get-tuple-element.15), channel_id=1, source_target_pairs={{32,0},{64,32},{96,64},{0,96},{33,1},{65,33},{97,65},{1,97},{34,2}... | collective-permute-start | bytes 196616 | tf_op jit(solution)/shard_map/ppermute | solution.py:203
  113.6 2.2 %collective-permute-done.10 = f32[4,4,8,128]{3,2,1,0:T(8,128)S(1)} collective-permute-done((f32[4,4,8,128]{3,2,1,0:T(8,128)S(1)}, f32[4,4,8,128]{3,2,1,0:T(8,128)S(1)}, u32[]{:S(2)}, u32[]{:S(2)}) %collective-permute-start.10) | collective-permute-done | bytes 65568 | tf_op jit(solution)/shard_map/ppermute | solution.py:203
  115.8 1.5 %collective-permute-done.11 = f32[4,4,8,128]{3,2,1,0:T(8,128)S(1)} collective-permute-done((f32[4,4,8,128]{3,2,1,0:T(8,128)S(1)}, f32[4,4,8,128]{3,2,1,0:T(8,128)S(1)}, u32[]{:S(2)}, u32[]{:S(2)}) %collective-permute-start.11) | collective-permute-done | bytes 65568 | tf_op jit(solution)/shard_map/ppermute | solution.py:203
  117.4 0.7 slice_add_fusion.5
  118.1 0.6 slice_bitcast_fusion
  (21 shorter events, 0.2 us)
Async XLA Ops:
  16.1 1.0 copy-start
  17.1 1.0 copy-start.2
  18.1 0.9 copy-start.5
  19.1 23.8 %copy-start.1 = (s32[2,2,3,8,8,128]{5,4,3,2,1,0:T(8,128)S(1)}, s32[2,2,3,8,8,128]{5,4,3,2,1,0:T(8,128)}, u32[]{:S(2)}) copy-start(s32[2,2,3,8,8,128]{5,4,3,2,1,0:T(8,128)} %cells_ref.7) | copy-start | bytes 1179652
  19.1 23.8 %copy-start.3 = (f32[2,2,3,8,8,128]{5,4,3,2,1,0:T(8,128)S(1)}, f32[2,2,3,8,8,128]{5,4,3,2,1,0:T(8,128)}, u32[]{:S(2)}) copy-start(f32[2,2,3,8,8,128]{5,4,3,2,1,0:T(8,128)} %fracs_ref.7) | copy-start | bytes 1179652
  23.3 0.6 copy-start.7
  23.9 19.0 %copy-start.6 = (f32[8,8,128]{2,1,0:T(8,128)S(1)}, f32[8,8,128]{2,1,0:T(8,128)}, u32[]{:S(2)}) copy-start(f32[8,8,128]{2,1,0:T(8,128)} %cot_ref.3) | copy-start | bytes 98308
  42.8 3.5 %copy-start.4 = (f32[16,16,256]{2,1,0:T(8,128)S(1)}, f32[16,16,256]{2,1,0:T(8,128)}, u32[]{:S(2)}) copy-start(f32[16,16,256]{2,1,0:T(8,128)} %shard_map.62.wrapped_ref) | copy-start | bytes 786436
  60.4 3.4 %collective-permute-start = (f32[32,128]{1,0:T(8,128)S(1)}, f32[32,128]{1,0:T(8,128)S(1)}, u32[]{:S(2)}, u32[]{:S(2)}) collective-permute-start(f32[32,128]{1,0:T(8,128)S(1)} %reshape.28), channel_id=1, source_target_pairs={{0,1},{1,2},{2,3},{3,0},{4,5},{5,6},{6,7},{7,4},{8,9},{9,10},{10,1... | collective-permute-start | bytes 49160 | tf_op jit(solution)/shard_map/ppermute | solution.py:201
  61.1 3.3 %collective-permute-start.1 = (f32[32,128]{1,0:T(8,128)S(1)}, f32[32,128]{1,0:T(8,128)S(1)}, u32[]{:S(2)}, u32[]{:S(2)}) collective-permute-start(f32[32,128]{1,0:T(8,128)S(1)} %reshape.30), channel_id=1, source_target_pairs={{1,0},{2,1},{3,2},{0,3},{5,4},{6,5},{7,6},{4,7},{9,8},{10,9},{11,1... | collective-permute-start | bytes 49160 | tf_op jit(solution)/shard_map/ppermute | solution.py:201
  65.2 5.7 %collective-permute-start.2 = (f32[4,16,4,128]{3,2,1,0:T(4,128)S(1)}, f32[4,16,4,128]{3,2,1,0:T(4,128)S(1)}, u32[]{:S(2)}, u32[]{:S(2)}) collective-permute-start(f32[4,16,4,128]{3,2,1,0:T(4,128)S(1)} %get-tuple-element.12), channel_id=1, source_target_pairs={{0,4},{4,8},{8,12},{12,16},{16,20},{20,24},{24,28},{28,0},{1,5},{5... | collective-permute-start | bytes 393224 | tf_op jit(solution)/shard_map/ppermute | solution.py:203
  66.9 9.8 %collective-permute-start.3 = (f32[4,16,4,128]{3,2,1,0:T(4,128)S(1)}, f32[4,16,4,128]{3,2,1,0:T(4,128)S(1)}, u32[]{:S(2)}, u32[]{:S(2)}) collective-permute-start(f32[4,16,4,128]{3,2,1,0:T(4,128)S(1)} %get-tuple-element.13), channel_id=1, source_target_pairs={{4,0},{8,4},{12,8},{16,12},{20,16},{24,20},{28,24},{0,28},{5,1},{9... | collective-permute-start | bytes 393224 | tf_op jit(solution)/shard_map/ppermute | solution.py:203
  76.8 4.3 %collective-permute-start.4 = (f32[4,4,8,128]{3,2,1,0:T(8,128)S(1)}, f32[4,4,8,128]{3,2,1,0:T(8,128)S(1)}, u32[]{:S(2)}, u32[]{:S(2)}) collective-permute-start(f32[4,4,8,128]{3,2,1,0:T(8,128)S(1)} %get-tuple-element.16), channel_id=1, source_target_pairs={{0,32},{32,64},{64,96},{96,0},{1,33},{33,65},{65,97},{97,1},{2,34}... | collective-permute-start | bytes 196616 | tf_op jit(solution)/shard_map/ppermute | solution.py:203
  78.1 5.5 %collective-permute-start.5 = (f32[4,4,8,128]{3,2,1,0:T(8,128)S(1)}, f32[4,4,8,128]{3,2,1,0:T(8,128)S(1)}, u32[]{:S(2)}, u32[]{:S(2)}) collective-permute-start(f32[4,4,8,128]{3,2,1,0:T(8,128)S(1)} %get-tuple-element.17), channel_id=1, source_target_pairs={{32,0},{64,32},{96,64},{0,96},{33,1},{65,33},{97,65},{1,97},{34,2}... | collective-permute-start | bytes 196616 | tf_op jit(solution)/shard_map/ppermute | solution.py:203
  96.8 3.2 %collective-permute-start.6 = (f32[32,128]{1,0:T(8,128)S(1)}, f32[32,128]{1,0:T(8,128)S(1)}, u32[]{:S(2)}, u32[]{:S(2)}) collective-permute-start(f32[32,128]{1,0:T(8,128)S(1)} %reshape.32), channel_id=1, source_target_pairs={{0,1},{1,2},{2,3},{3,0},{4,5},{5,6},{6,7},{7,4},{8,9},{9,10},{10,1... | collective-permute-start | bytes 49160 | tf_op jit(solution)/shard_map/ppermute | solution.py:201
  97.2 3.4 %collective-permute-start.7 = (f32[32,128]{1,0:T(8,128)S(1)}, f32[32,128]{1,0:T(8,128)S(1)}, u32[]{:S(2)}, u32[]{:S(2)}) collective-permute-start(f32[32,128]{1,0:T(8,128)S(1)} %reshape.34), channel_id=1, source_target_pairs={{1,0},{2,1},{3,2},{0,3},{5,4},{6,5},{7,6},{4,7},{9,8},{10,9},{11,1... | collective-permute-start | bytes 49160 | tf_op jit(solution)/shard_map/ppermute | solution.py:201
  101.4 6.1 %collective-permute-start.8 = (f32[4,16,4,128]{3,2,1,0:T(4,128)S(1)}, f32[4,16,4,128]{3,2,1,0:T(4,128)S(1)}, u32[]{:S(2)}, u32[]{:S(2)}) collective-permute-start(f32[4,16,4,128]{3,2,1,0:T(4,128)S(1)} %get-tuple-element.10), channel_id=1, source_target_pairs={{0,4},{4,8},{8,12},{12,16},{16,20},{20,24},{24,28},{28,0},{1,5},{5... | collective-permute-start | bytes 393224 | tf_op jit(solution)/shard_map/ppermute | solution.py:203
  101.5 9.9 %collective-permute-start.9 = (f32[4,16,4,128]{3,2,1,0:T(4,128)S(1)}, f32[4,16,4,128]{3,2,1,0:T(4,128)S(1)}, u32[]{:S(2)}, u32[]{:S(2)}) collective-permute-start(f32[4,16,4,128]{3,2,1,0:T(4,128)S(1)} %get-tuple-element.11), channel_id=1, source_target_pairs={{4,0},{8,4},{12,8},{16,12},{20,16},{24,20},{28,24},{0,28},{5,1},{9... | collective-permute-start | bytes 393224 | tf_op jit(solution)/shard_map/ppermute | solution.py:203
  111.5 4.3 %collective-permute-start.10 = (f32[4,4,8,128]{3,2,1,0:T(8,128)S(1)}, f32[4,4,8,128]{3,2,1,0:T(8,128)S(1)}, u32[]{:S(2)}, u32[]{:S(2)}) collective-permute-start(f32[4,4,8,128]{3,2,1,0:T(8,128)S(1)} %get-tuple-element.14), channel_id=1, source_target_pairs={{0,32},{32,64},{64,96},{96,0},{1,33},{33,65},{65,97},{97,1},{2,34}... | collective-permute-start | bytes 196616 | tf_op jit(solution)/shard_map/ppermute | solution.py:203
  111.9 5.5 %collective-permute-start.11 = (f32[4,4,8,128]{3,2,1,0:T(8,128)S(1)}, f32[4,4,8,128]{3,2,1,0:T(8,128)S(1)}, u32[]{:S(2)}, u32[]{:S(2)}) collective-permute-start(f32[4,4,8,128]{3,2,1,0:T(8,128)S(1)} %get-tuple-element.15), channel_id=1, source_target_pairs={{32,0},{64,32},{96,64},{0,96},{33,1},{65,33},{97,65},{1,97},{34,2}... | collective-permute-start | bytes 196616 | tf_op jit(solution)/shard_map/ppermute | solution.py:203

commit v2 on v0

--- a/solution.py
+++ b/solution.py
@@ -203,21 +203,88 @@
     return lax.ppermute(piece, axis, pairs)
 
 
+def offsets_26():
+    return [
+        (a, b, c)
+        for a in (-1, 0, 1)
+        for b in (-1, 0, 1)
+        for c in (-1, 0, 1)
+        if (a, b, c) != (0, 0, 0)
+    ]
+
+
+def slot_of(offset):
+    return (offset[0] + 1) * 9 + (offset[1] + 1) * 3 + (offset[2] + 1)
+
+
+def device_at(offset):
+    target = []
+    for (axis, _), step in zip(AXES, offset):
+        count = lax.axis_size(axis)
+        target.append(lax.rem(lax.axis_index(axis) + (step + count), count))
+    return tuple(target)
+
+
+def widen_kernel(block_ref, out_ref, landed, planes, send_sems, recv_sems):
+    nx, ny, nz = block_ref.shape
+    mesh = pl.DeviceIdType.MESH
+    offsets = offsets_26()
+    barrier = pltpu.get_barrier_semaphore()
+    for offset in offsets:
+        pl.semaphore_signal(barrier, inc=1, device_id=device_at(offset), device_id_type=mesh)
+    pl.semaphore_wait(barrier, len(offsets))
+    copies = []
+    for offset in offsets:
+        back = slot_of(tuple(-step for step in offset))
+        copy = pltpu.make_async_remote_copy(
+            src_ref=block_ref,
+            dst_ref=landed.at[back],
+            send_sem=send_sems.at[slot_of(offset)],
+            recv_sem=recv_sems.at[back],
+            device_id=device_at(offset),
+            device_id_type=mesh,
+        )
+        copy.start()
+        copies.append(copy)
+    for copy in copies:
+        copy.wait()
+    row_ranges = {-1: (nx - MARGIN, nx, 0), 0: (0, nx, MARGIN), 1: (0, MARGIN, MARGIN + nx)}
+    for c in (-1, 0, 1):
+        for b in (-1, 0, 1):
+            for a in (-1, 0, 1):
+                first, last, at = row_ranges[a]
+                if (a, b, c) == (0, 0, 0):
+                    piece = block_ref[first:last]
+                else:
+                    piece = landed[slot_of((a, b, c)), first:last]
+                planes[c + 1, at : at + last - first, (b + 1) * ny : (b + 2) * ny, :] = piece
+    rows = slice(ny - MARGIN, 2 * ny + MARGIN)
+    out_ref[:, :, 0:nz] = planes[1, :, rows, :]
+    lane = lax.broadcasted_iota(jnp.int32, out_ref.shape[:2] + (nz,), 2)
+    above = planes[2, :, rows, :]
+    below = planes[0, :, rows, :]
+    out_ref[:, :, nz:] = jnp.where(
+        lane < MARGIN, above, jnp.where(lane >= nz - MARGIN, below, 0.0)
+    )
+
+
 def widen(block, pz):
-    for axis, dim in AXES[:2]:
-        size = block.shape[dim]
-        head = lax.slice_in_dim(block, 0, MARGIN, axis=dim)
-        tail = lax.slice_in_dim(block, size - MARGIN, size, axis=dim)
-        block = jnp.concatenate(
-            [shift_from(tail, axis, True), block, shift_from(head, axis, False)], axis=dim
-        )
-    nz = block.shape[2]
-    head = block[:, :, :MARGIN]
-    tail = block[:, :, nz - MARGIN :]
-    gap = jnp.zeros(block.shape[:2] + (pz - nz - 2 * MARGIN,), jnp.float32)
-    return jnp.concatenate(
-        [block, shift_from(head, "gz", False), gap, shift_from(tail, "gz", True)], axis=2
-    )
+    nx, ny, nz = block.shape
+    px = nx + 2 * MARGIN
+    f32 = jnp.float32
+    return pl.pallas_call(
+        widen_kernel,
+        out_shape=jax.ShapeDtypeStruct((px, ny + 2 * MARGIN, pz), f32),
+        in_specs=[pl.BlockSpec(memory_space=pltpu.VMEM)],
+        out_specs=pl.BlockSpec(memory_space=pltpu.VMEM),
+        scratch_shapes=[
+            pltpu.VMEM((27, nx, ny, nz), f32),
+            pltpu.VMEM((3, px, 3 * ny, nz), f32),
+            pltpu.SemaphoreType.DMA((27,)),
+            pltpu.SemaphoreType.DMA((27,)),
+        ],
+        compiler_params=pltpu.CompilerParams(collective_id=0, has_side_effects=True),
+    )(block)
 
 
 def place_rim(rim, dim, start, size):

time: 112 us -> 122 us (1.089)
  Pallas kernels: 34.1 us -> 68.6 us
  waiting for transfers between devices: 46.6 us -> 27.1 us
  starting transfers between devices: 22.1 us -> 15.8 us
  local copies, waits for them, and re-layouts: 6.2 us -> 7.7 us
    pallas_call x0 -> x2, Pallas kernels: none -> 34.5 us  [widen(): pl.pallas_call(widen_kernel, out_shape=jax.ShapeDtypeStruct((px, ny + 2 *...]
    ppermute x16 -> x8, waiting for transfers between devices: 42.2 us -> 24.9 us  [shift_from(): return lax.ppermute(piece, axis, pairs)]
    ppermute x16 -> x8, starting transfers between devices: 16.7 us -> 12.1 us  [shift_from(): return lax.ppermute(piece, axis, pairs)]
    unnamed x12 -> x16, local copies, waits for them, and re-layouts: 0.03 us -> 3.56 us
    ppermute x8 -> x4, waiting for transfers between devices: 4.47 us -> 2.17 us  [shift_from(): flat = lax.ppermute(piece.reshape(-1, 128), axis, pairs)]
    ppermute x8 -> x4, starting transfers between devices: 5.42 us -> 3.75 us  [shift_from(): flat = lax.ppermute(piece.reshape(-1, 128), axis, pairs)]
    reshape x8 -> x4, local copies, waits for them, and re-layouts: 2.64 us -> 2.12 us  [shift_from(): return flat.reshape(shape)]
  transfers between devices with their start and end apart: 24 -> 12, of which waited for: 20 -> 10; matrix products, arithmetic and copies ran while one was open for 2% -> 1% of each run, Pallas kernels for 3% -> 0%
where the time goes in v2:
time: 122 us
  Pallas kernels  68.6 us (56%)
  waiting for transfers between devices  27.1 us (22%)
  starting transfers between devices  15.8 us (13%)
  local copies, waits for them, and re-layouts  7.7 us (6%)
  other arithmetic  1.47 us (1%)
    pallas_call x2, Pallas kernels, widen(): pl.pallas_call(widen_kernel, out_shape=jax.ShapeDtypeStruct((px, ny + 2 *...  34.5 us
    pallas_call x4, Pallas kernels, vmem_call(): pl.pallas_call(kernel, out_shape=out_shapes, in_specs=[pl.BlockSpec(memor...  34.1 us
    ppermute x8, waiting for transfers between devices, shift_from(): return lax.ppermute(piece, axis, pairs)  24.9 us
    ppermute x8, starting transfers between devices, shift_from(): return lax.ppermute(piece, axis, pairs)  12.1 us
    ppermute x4, starting transfers between devices, shift_from(): flat = lax.ppermute(piece.reshape(-1, 128), axis, pairs)  3.75 us
    unnamed x16, local copies, waits for them, and re-layouts  3.56 us
  transfers between devices with their start and end apart: 12, of which 10 were waited for; matrix products, arithmetic and copies ran while one was open for 1% of the time, Pallas kernels for 0%

profile of v2, /device:TPU:102, one launch (start us, length us, event | category | flops | bytes accessed | tf_op | source)
XLA Modules:
  0.0 121.6 jit_solution(1138775156621953501)
XLA Ops:
  0.6 15.5 %shard_map.60.wrapped_ref = f32[16,16,256]{2,1,0:T(8,128)} custom-call(f32[8,8,128]{2,1,0:T(8,128)} %block_ref.1), custom_call_target="tpu_custom_call" | custom-call | tf_op jit(solution)/shard_map/pallas_call | solution.py:275
  16.1 0.0 copy-start
  16.1 1.0 copy-done
  17.1 1.0 copy-done.2
  18.1 0.9 copy-done.5
  19.1 4.2 %shard_map.61 = (f32[8,8,128]{2,1,0:T(8,128)S(1)}, f32[3,8,8,128]{3,2,1,0:T(8,128)S(1)}) custom-call(f32[16,16,256]{2,1,0:T(8,128)S(1)} %copy-done.5, s32[2,2,3,8,8,128]{5,4,3,2,1,0:T(8,128)S(1)} %copy-done, f32[2,2,3,8,8,128]{5,4,3,2,1,0:T(8,128)S(1)} %copy-done.2), custom_call_target="tpu_custom_call" | custom-call | tf_op jit(solution)/shard_map/pallas_call | solution.py:183
  23.3 0.6 copy-done.7
  23.9 19.0 %shard_map.62.wrapped_ref = f32[16,16,256]{2,1,0:T(8,128)} custom-call(f32[8,8,128]{2,1,0:T(8,128)} %copy-done.7), custom_call_target="tpu_custom_call" | custom-call | tf_op jit(solution)/shard_map/pallas_call | solution.py:275
  43.0 3.5 %shard_map.59 = f32[16,16,256]{2,1,0:T(8,128)S(1)} custom-call(f32[8,8,128]{2,1,0:T(8,128)S(1)} %copy-done.6, s32[2,2,3,8,8,128]{5,4,3,2,1,0:T(8,128)S(1)} %copy-done.1, f32[2,2,3,8,8,128]{5,4,3,2,1,0:T(8,128)S(1)} %copy-done.3), custom_call_target="tpu_custom_call" | custom-call | tf_op jit(solution)/shard_map/pallas_call | solution.py:183
  46.4 13.6 %shard_map.63 = f32[3,16,16,256]{3,2,1,0:T(8,128)S(1)} custom-call(f32[16,16,256]{2,1,0:T(8,128)S(1)} %copy-done.4, f32[8,8,128]{2,1,0:T(8,128)S(1)} %copy-done.6, s32[2,2,3,8,8,128]{5,4,3,2,1,0:T(8,128)S(1)} %copy-done.1, f32[2,2,3,8,8,128]{5,4,3,2,1,0:T(8,128)S(1)} %copy-done.3), custom_call_target="tpu_custom_call" | custom-call | tf_op jit(solution)/shard_map/pallas_call | solution.py:183
  60.1 0.2 fusion
  60.3 0.3 reshape.28
  60.6 0.5 collective-permute-start
  61.1 0.3 reshape.30
  61.3 1.4 %collective-permute-start.1 = (f32[32,128]{1,0:T(8,128)S(1)}, f32[32,128]{1,0:T(8,128)S(1)}, u32[]{:S(2)}, u32[]{:S(2)}) collective-permute-start(f32[32,128]{1,0:T(8,128)S(1)} %reshape.30), channel_id=1, source_target_pairs={{1,0},{2,1},{3,2},{0,3},{5,4},{6,5},{7,6},{4,7},{9,8},{10,9},{11,1... | collective-permute-start | bytes 49160 | tf_op jit(solution)/shard_map/ppermute | solution.py:201
  62.7 1.1 collective-permute-done
  63.8 0.5 reshape.29
  64.3 0.5 reshape.31
  64.9 0.2 fusion.3
  65.1 5.8 %collective-permute-start.2 = (f32[4,16,4,128]{3,2,1,0:T(4,128)S(1)}, f32[4,16,4,128]{3,2,1,0:T(4,128)S(1)}, u32[]{:S(2)}, u32[]{:S(2)}) collective-permute-start(f32[4,16,4,128]{3,2,1,0:T(4,128)S(1)} %get-tuple-element.12), channel_id=1, source_target_pairs={{0,4},{4,8},{8,12},{12,16},{16,20},{20,24},{24,28},{28,0},{1,5},{5... | collective-permute-start | bytes 393224 | tf_op jit(solution)/shard_map/ppermute | solution.py:203
  71.0 3.3 %collective-permute-done.2 = f32[4,16,4,128]{3,2,1,0:T(4,128)S(1)} collective-permute-done((f32[4,16,4,128]{3,2,1,0:T(4,128)S(1)}, f32[4,16,4,128]{3,2,1,0:T(4,128)S(1)}, u32[]{:S(2)}, u32[]{:S(2)}) %collective-permute-start.2) | collective-permute-done | bytes 131104 | tf_op jit(solution)/shard_map/ppermute | solution.py:203
  74.3 6.3 %collective-permute-done.3 = f32[4,16,4,128]{3,2,1,0:T(4,128)S(1)} collective-permute-done((f32[4,16,4,128]{3,2,1,0:T(4,128)S(1)}, f32[4,16,4,128]{3,2,1,0:T(4,128)S(1)}, u32[]{:S(2)}, u32[]{:S(2)}) %collective-permute-start.3) | collective-permute-done | bytes 131104 | tf_op jit(solution)/shard_map/ppermute | solution.py:203
  80.6 0.1 fusion.6
  80.7 0.5 collective-permute-start.4
  81.2 1.6 %collective-permute-start.5 = (f32[4,4,8,128]{3,2,1,0:T(8,128)S(1)}, f32[4,4,8,128]{3,2,1,0:T(8,128)S(1)}, u32[]{:S(2)}, u32[]{:S(2)}) collective-permute-start(f32[4,4,8,128]{3,2,1,0:T(8,128)S(1)} %get-tuple-element.17), channel_id=1, source_target_pairs={{32,0},{64,32},{96,64},{0,96},{33,1},{65,33},{97,65},{1,97},{34,2}... | collective-permute-start | bytes 196616 | tf_op jit(solution)/shard_map/ppermute | solution.py:203
  82.8 2.2 %collective-permute-done.4 = f32[4,4,8,128]{3,2,1,0:T(8,128)S(1)} collective-permute-done((f32[4,4,8,128]{3,2,1,0:T(8,128)S(1)}, f32[4,4,8,128]{3,2,1,0:T(8,128)S(1)}, u32[]{:S(2)}, u32[]{:S(2)}) %collective-permute-start.4) | collective-permute-done | bytes 65568 | tf_op jit(solution)/shard_map/ppermute | solution.py:203
  85.0 1.7 %collective-permute-done.5 = f32[4,4,8,128]{3,2,1,0:T(8,128)S(1)} collective-permute-done((f32[4,4,8,128]{3,2,1,0:T(8,128)S(1)}, f32[4,4,8,128]{3,2,1,0:T(8,128)S(1)}, u32[]{:S(2)}, u32[]{:S(2)}) %collective-permute-start.5) | collective-permute-done | bytes 65568 | tf_op jit(solution)/shard_map/ppermute | solution.py:203
  86.7 12.8 %shard_map.64 = f32[4,16,16,256]{3,2,1,0:T(8,128)S(1)} custom-call(f32[8,8,128]{2,1,0:T(8,128)S(1)} %slice_bitcast_fusion.1.adjoint_ref, f32[3,8,8,128]{3,2,1,0:T(8,128)S(1)} %get-tuple-element.5.grad_ref, s32[2,2,3,8,8,128]{5,4,3,2,1,0:T(8,128)S(1)} %copy-done.1, f32[2,2,3,8,8,128]{5,4,3,2,1,0:T(8,128)S(1)} %copy-done.3), custom_call_target="tpu_custom_call" | custom-call | tf_op jit(solution)/shard_map/pallas_call | solution.py:183
  99.5 0.2 fusion.9
  99.7 0.3 reshape.32
  100.0 0.1 collective-permute-start.6
  100.1 0.3 reshape.34
  100.4 1.8 %collective-permute-start.7 = (f32[32,128]{1,0:T(8,128)S(1)}, f32[32,128]{1,0:T(8,128)S(1)}, u32[]{:S(2)}, u32[]{:S(2)}) collective-permute-start(f32[32,128]{1,0:T(8,128)S(1)} %reshape.34), channel_id=1, source_target_pairs={{1,0},{2,1},{3,2},{0,3},{5,4},{6,5},{7,6},{4,7},{9,8},{10,9},{11,1... | collective-permute-start | bytes 49160 | tf_op jit(solution)/shard_map/ppermute | solution.py:201
  102.2 1.1 collective-permute-done.6
  103.2 0.5 reshape.33
  103.8 0.5 reshape.35
  104.3 0.2 fusion.4
  104.6 0.1 collective-permute-start.8
  104.7 2.0 %collective-permute-start.9 = (f32[4,16,4,128]{3,2,1,0:T(4,128)S(1)}, f32[4,16,4,128]{3,2,1,0:T(4,128)S(1)}, u32[]{:S(2)}, u32[]{:S(2)}) collective-permute-start(f32[4,16,4,128]{3,2,1,0:T(4,128)S(1)} %get-tuple-element.11), channel_id=1, source_target_pairs={{4,0},{8,4},{12,8},{16,12},{20,16},{24,20},{28,24},{0,28},{5,1},{9... | collective-permute-start | bytes 393224 | tf_op jit(solution)/shard_map/ppermute | solution.py:203
  106.7 3.5 %collective-permute-done.8 = f32[4,16,4,128]{3,2,1,0:T(4,128)S(1)} collective-permute-done((f32[4,16,4,128]{3,2,1,0:T(4,128)S(1)}, f32[4,16,4,128]{3,2,1,0:T(4,128)S(1)}, u32[]{:S(2)}, u32[]{:S(2)}) %collective-permute-start.8) | collective-permute-done | bytes 131104 | tf_op jit(solution)/shard_map/ppermute | solution.py:203
  110.2 4.2 %collective-permute-done.9 = f32[4,16,4,128]{3,2,1,0:T(4,128)S(1)} collective-permute-done((f32[4,16,4,128]{3,2,1,0:T(4,128)S(1)}, f32[4,16,4,128]{3,2,1,0:T(4,128)S(1)}, u32[]{:S(2)}, u32[]{:S(2)}) %collective-permute-start.9) | collective-permute-done | bytes 131104 | tf_op jit(solution)/shard_map/ppermute | solution.py:203
  114.4 0.1 fusion.5
  114.5 0.3 collective-permute-start.10
  114.8 1.8 %collective-permute-start.11 = (f32[4,4,8,128]{3,2,1,0:T(8,128)S(1)}, f32[4,4,8,128]{3,2,1,0:T(8,128)S(1)}, u32[]{:S(2)}, u32[]{:S(2)}) collective-permute-start(f32[4,4,8,128]{3,2,1,0:T(8,128)S(1)} %get-tuple-element.15), channel_id=1, source_target_pairs={{32,0},{64,32},{96,64},{0,96},{33,1},{65,33},{97,65},{1,97},{34,2}... | collective-permute-start | bytes 196616 | tf_op jit(solution)/shard_map/ppermute | solution.py:203
  116.6 2.2 %collective-permute-done.10 = f32[4,4,8,128]{3,2,1,0:T(8,128)S(1)} collective-permute-done((f32[4,4,8,128]{3,2,1,0:T(8,128)S(1)}, f32[4,4,8,128]{3,2,1,0:T(8,128)S(1)}, u32[]{:S(2)}, u32[]{:S(2)}) %collective-permute-start.10) | collective-permute-done | bytes 65568 | tf_op jit(solution)/shard_map/ppermute | solution.py:203
  118.9 1.4 %collective-permute-done.11 = f32[4,4,8,128]{3,2,1,0:T(8,128)S(1)} collective-permute-done((f32[4,4,8,128]{3,2,1,0:T(8,128)S(1)}, f32[4,4,8,128]{3,2,1,0:T(8,128)S(1)}, u32[]{:S(2)}, u32[]{:S(2)}) %collective-permute-start.11) | collective-permute-done | bytes 65568 | tf_op jit(solution)/shard_map/ppermute | solution.py:203
  120.3 0.7 slice_add_fusion.5
  121.0 0.6 slice_bitcast_fusion
  (21 shorter events, 0.2 us)
Async XLA Ops:
  16.1 1.0 copy-start
  17.1 1.0 copy-start.2
  18.1 0.9 copy-start.5
  19.1 23.9 %copy-start.1 = (s32[2,2,3,8,8,128]{5,4,3,2,1,0:T(8,128)S(1)}, s32[2,2,3,8,8,128]{5,4,3,2,1,0:T(8,128)}, u32[]{:S(2)}) copy-start(s32[2,2,3,8,8,128]{5,4,3,2,1,0:T(8,128)} %cells_ref.7) | copy-start | bytes 1179652
  19.1 23.9 %copy-start.3 = (f32[2,2,3,8,8,128]{5,4,3,2,1,0:T(8,128)S(1)}, f32[2,2,3,8,8,128]{5,4,3,2,1,0:T(8,128)}, u32[]{:S(2)}) copy-start(f32[2,2,3,8,8,128]{5,4,3,2,1,0:T(8,128)} %fracs_ref.7) | copy-start | bytes 1179652
  23.3 0.6 copy-start.7
  23.9 19.0 %copy-start.6 = (f32[8,8,128]{2,1,0:T(8,128)S(1)}, f32[8,8,128]{2,1,0:T(8,128)}, u32[]{:S(2)}) copy-start(f32[8,8,128]{2,1,0:T(8,128)} %cot_ref.3) | copy-start | bytes 98308
  42.9 3.5 %copy-start.4 = (f32[16,16,256]{2,1,0:T(8,128)S(1)}, f32[16,16,256]{2,1,0:T(8,128)}, u32[]{:S(2)}) copy-start(f32[16,16,256]{2,1,0:T(8,128)} %shard_map.62.wrapped_ref) | copy-start | bytes 786436
  60.6 3.2 %collective-permute-start = (f32[32,128]{1,0:T(8,128)S(1)}, f32[32,128]{1,0:T(8,128)S(1)}, u32[]{:S(2)}, u32[]{:S(2)}) collective-permute-start(f32[32,128]{1,0:T(8,128)S(1)} %reshape.28), channel_id=1, source_target_pairs={{0,1},{1,2},{2,3},{3,0},{4,5},{5,6},{6,7},{7,4},{8,9},{9,10},{10,1... | collective-permute-start | bytes 49160 | tf_op jit(solution)/shard_map/ppermute | solution.py:201
  61.3 3.0 %collective-permute-start.1 = (f32[32,128]{1,0:T(8,128)S(1)}, f32[32,128]{1,0:T(8,128)S(1)}, u32[]{:S(2)}, u32[]{:S(2)}) collective-permute-start(f32[32,128]{1,0:T(8,128)S(1)} %reshape.30), channel_id=1, source_target_pairs={{1,0},{2,1},{3,2},{0,3},{5,4},{6,5},{7,6},{4,7},{9,8},{10,9},{11,1... | collective-permute-start | bytes 49160 | tf_op jit(solution)/shard_map/ppermute | solution.py:201
  65.1 9.1 %collective-permute-start.2 = (f32[4,16,4,128]{3,2,1,0:T(4,128)S(1)}, f32[4,16,4,128]{3,2,1,0:T(4,128)S(1)}, u32[]{:S(2)}, u32[]{:S(2)}) collective-permute-start(f32[4,16,4,128]{3,2,1,0:T(4,128)S(1)} %get-tuple-element.12), channel_id=1, source_target_pairs={{0,4},{4,8},{8,12},{12,16},{16,20},{20,24},{24,28},{28,0},{1,5},{5... | collective-permute-start | bytes 393224 | tf_op jit(solution)/shard_map/ppermute | solution.py:203
  71.0 9.6 %collective-permute-start.3 = (f32[4,16,4,128]{3,2,1,0:T(4,128)S(1)}, f32[4,16,4,128]{3,2,1,0:T(4,128)S(1)}, u32[]{:S(2)}, u32[]{:S(2)}) collective-permute-start(f32[4,16,4,128]{3,2,1,0:T(4,128)S(1)} %get-tuple-element.13), channel_id=1, source_target_pairs={{4,0},{8,4},{12,8},{16,12},{20,16},{24,20},{28,24},{0,28},{5,1},{9... | collective-permute-start | bytes 393224 | tf_op jit(solution)/shard_map/ppermute | solution.py:203
  80.7 4.3 %collective-permute-start.4 = (f32[4,4,8,128]{3,2,1,0:T(8,128)S(1)}, f32[4,4,8,128]{3,2,1,0:T(8,128)S(1)}, u32[]{:S(2)}, u32[]{:S(2)}) collective-permute-start(f32[4,4,8,128]{3,2,1,0:T(8,128)S(1)} %get-tuple-element.16), channel_id=1, source_target_pairs={{0,32},{32,64},{64,96},{96,0},{1,33},{33,65},{65,97},{97,1},{2,34}... | collective-permute-start | bytes 196616 | tf_op jit(solution)/shard_map/ppermute | solution.py:203
  81.2 5.5 %collective-permute-start.5 = (f32[4,4,8,128]{3,2,1,0:T(8,128)S(1)}, f32[4,4,8,128]{3,2,1,0:T(8,128)S(1)}, u32[]{:S(2)}, u32[]{:S(2)}) collective-permute-start(f32[4,4,8,128]{3,2,1,0:T(8,128)S(1)} %get-tuple-element.17), channel_id=1, source_target_pairs={{32,0},{64,32},{96,64},{0,96},{33,1},{65,33},{97,65},{1,97},{34,2}... | collective-permute-start | bytes 196616 | tf_op jit(solution)/shard_map/ppermute | solution.py:203
  100.0 3.2 %collective-permute-start.6 = (f32[32,128]{1,0:T(8,128)S(1)}, f32[32,128]{1,0:T(8,128)S(1)}, u32[]{:S(2)}, u32[]{:S(2)}) collective-permute-start(f32[32,128]{1,0:T(8,128)S(1)} %reshape.32), channel_id=1, source_target_pairs={{0,1},{1,2},{2,3},{3,0},{4,5},{5,6},{6,7},{7,4},{8,9},{9,10},{10,1... | collective-permute-start | bytes 49160 | tf_op jit(solution)/shard_map/ppermute | solution.py:201
  100.4 3.4 %collective-permute-start.7 = (f32[32,128]{1,0:T(8,128)S(1)}, f32[32,128]{1,0:T(8,128)S(1)}, u32[]{:S(2)}, u32[]{:S(2)}) collective-permute-start(f32[32,128]{1,0:T(8,128)S(1)} %reshape.34), channel_id=1, source_target_pairs={{1,0},{2,1},{3,2},{0,3},{5,4},{6,5},{7,6},{4,7},{9,8},{10,9},{11,1... | collective-permute-start | bytes 49160 | tf_op jit(solution)/shard_map/ppermute | solution.py:201
  104.6 5.6 %collective-permute-start.8 = (f32[4,16,4,128]{3,2,1,0:T(4,128)S(1)}, f32[4,16,4,128]{3,2,1,0:T(4,128)S(1)}, u32[]{:S(2)}, u32[]{:S(2)}) collective-permute-start(f32[4,16,4,128]{3,2,1,0:T(4,128)S(1)} %get-tuple-element.10), channel_id=1, source_target_pairs={{0,4},{4,8},{8,12},{12,16},{16,20},{20,24},{24,28},{28,0},{1,5},{5... | collective-permute-start | bytes 393224 | tf_op jit(solution)/shard_map/ppermute | solution.py:203
  104.7 9.7 %collective-permute-start.9 = (f32[4,16,4,128]{3,2,1,0:T(4,128)S(1)}, f32[4,16,4,128]{3,2,1,0:T(4,128)S(1)}, u32[]{:S(2)}, u32[]{:S(2)}) collective-permute-start(f32[4,16,4,128]{3,2,1,0:T(4,128)S(1)} %get-tuple-element.11), channel_id=1, source_target_pairs={{4,0},{8,4},{12,8},{16,12},{20,16},{24,20},{28,24},{0,28},{5,1},{9... | collective-permute-start | bytes 393224 | tf_op jit(solution)/shard_map/ppermute | solution.py:203
  114.5 4.3 %collective-permute-start.10 = (f32[4,4,8,128]{3,2,1,0:T(8,128)S(1)}, f32[4,4,8,128]{3,2,1,0:T(8,128)S(1)}, u32[]{:S(2)}, u32[]{:S(2)}) collective-permute-start(f32[4,4,8,128]{3,2,1,0:T(8,128)S(1)} %get-tuple-element.14), channel_id=1, source_target_pairs={{0,32},{32,64},{64,96},{96,0},{1,33},{33,65},{65,97},{97,1},{2,34}... | collective-permute-start | bytes 196616 | tf_op jit(solution)/shard_map/ppermute | solution.py:203
  114.8 5.5 %collective-permute-start.11 = (f32[4,4,8,128]{3,2,1,0:T(8,128)S(1)}, f32[4,4,8,128]{3,2,1,0:T(8,128)S(1)}, u32[]{:S(2)}, u32[]{:S(2)}) collective-permute-start(f32[4,4,8,128]{3,2,1,0:T(8,128)S(1)} %get-tuple-element.15), channel_id=1, source_target_pairs={{32,0},{64,32},{96,64},{0,96},{33,1},{65,33},{97,65},{1,97},{34,2}... | collective-permute-start | bytes 196616 | tf_op jit(solution)/shard_map/ppermute | solution.py:203

commit v3 on v0

--- a/solution.py
+++ b/solution.py
@@ -187,6 +187,9 @@
         out_specs=jax.tree.map(lambda _: pl.BlockSpec(memory_space=pltpu.VMEM), out_shapes),
         scratch_shapes=scratch,
         compiler_params=pltpu.CompilerParams(vmem_limit_bytes=48 * 1024 * 1024),
+        cost_estimate=pl.CostEstimate(
+            flops=40_000_000, transcendentals=0, bytes_accessed=2_000_000
+        ),
     )(*args)
 
 
@@ -272,6 +275,13 @@
         [products, staged] + table_scratch(block, 3),
         cotangent, cells, fracs,
     )
+    adjoint_mid = fold(adjoint_padded[None], nz)[0]
+    early_padded = vmem_call(
+        early_spread_kernel,
+        jax.ShapeDtypeStruct((4, px, py, pz), f32),
+        [products, staged] + table_scratch(block, 6),
+        adjoint_mid, grad_raw, cells, fracs,
+    )
     wrapped_mid = widen(image_mid, pz)
     velocity_padded = vmem_call(
         late_velocity_kernel,
@@ -279,17 +289,9 @@
         [rolled, windows, products, staged] + table_scratch(block, 9),
         wrapped_mid, cotangent, cells, fracs,
     )
-    folded = fold(jnp.concatenate([adjoint_padded[None], velocity_padded]), nz)
-    adjoint_mid = folded[0]
-    velocity_late = folded[1:]
-    early_padded = vmem_call(
-        early_spread_kernel,
-        jax.ShapeDtypeStruct((4, px, py, pz), f32),
-        [products, staged] + table_scratch(block, 6),
-        adjoint_mid, grad_raw, cells, fracs,
-    )
-    folded = fold(early_padded, nz)
-    return (folded[0], velocity_late + folded[1:])
+    deposits = jnp.concatenate([early_padded[:1], early_padded[1:] + velocity_padded])
+    folded = fold(deposits, nz)
+    return (folded[0], folded[1:])
 
 
 def solution(mesh):

time: 112 us -> 104 us (0.929)
  waiting for transfers between devices: 46.6 us -> 32.3 us
  starting transfers between devices: 22.1 us -> 25.7 us
  local copies, waits for them, and re-layouts: 6.2 us -> 9.17 us
    ppermute x16, waiting for transfers between devices: 42.2 us -> 31.2 us  [shift_from(): return lax.ppermute(piece, axis, pairs)]
    unnamed x12 -> x16, local copies, waits for them, and re-layouts: 0.03 us -> 3.59 us
    ppermute x8, waiting for transfers between devices: 4.47 us -> 1.1 us  [shift_from(): flat = lax.ppermute(piece.reshape(-1, 128), axis, pairs)]
    ppermute x8, starting transfers between devices: 5.42 us -> 7.36 us  [shift_from(): flat = lax.ppermute(piece.reshape(-1, 128), axis, pairs)]
    ppermute x16, starting transfers between devices: 16.7 us -> 18.4 us  [shift_from(): return lax.ppermute(piece, axis, pairs)]
  transfers between devices with their start and end apart: 24 -> 24, of which waited for: 20 -> 11; matrix products, arithmetic and copies ran while one was open for 2% -> 2% of each run, Pallas kernels for 3% -> 20%
where the time goes in v3:
time: 104 us; the launch traced here: 103 us
  Pallas kernels  34.1 us (33%)
  waiting for transfers between devices  32.3 us (31%)
  starting transfers between devices  25.7 us (25%)
  local copies, waits for them, and re-layouts  9.17 us (9%)
  other arithmetic  1.04 us (1%)
    pallas_call x4, Pallas kernels, vmem_call(): pl.pallas_call(kernel, out_shape=out_shapes, in_specs=[pl.BlockSpec(memor...  34.1 us
    ppermute x16, waiting for transfers between devices, shift_from(): return lax.ppermute(piece, axis, pairs)  31.2 us
    ppermute x16, starting transfers between devices, shift_from(): return lax.ppermute(piece, axis, pairs)  18.4 us
    ppermute x8, starting transfers between devices, shift_from(): flat = lax.ppermute(piece.reshape(-1, 128), axis, pairs)  7.36 us
    unnamed x16, local copies, waits for them, and re-layouts  3.59 us
  transfers between devices with their start and end apart: 24, of which 11 were waited for; matrix products, arithmetic and copies ran while one was open for 2% of the time, Pallas kernels for 20%

profile of v3, /device:TPU:102, one launch (start us, length us, event | category | flops | bytes accessed | tf_op | source)
XLA Modules:
  0.0 103.3 jit_solution(3957539924136254851)
XLA Ops:
  0.6 0.7 fusion.20
  1.4 0.5 collective-permute-start.6
  1.9 1.0 copy-done
  2.9 1.0 copy-done.2
  3.9 3.5 %shard_map.59 = f32[16,16,256]{2,1,0:T(8,128)S(1)} custom-call(f32[8,8,128]{2,1,0:T(8,128)S(1)} %copy-done.4, s32[2,2,3,8,8,128]{5,4,3,2,1,0:T(8,128)S(1)} %copy-done, f32[2,2,3,8,8,128]{5,4,3,2,1,0:T(8,128)S(1)} %copy-done.2), custom_call_target="tpu_custom_call" | custom-call | flops 40000000 | bytes 2000000 | tf_op jit(solution)/shard_map/pallas_call | solution.py:183
  7.7 1.8 %collective-permute-start.1 = (f32[8,128]{1,0:T(8,128)S(1)}, f32[8,128]{1,0:T(8,128)S(1)}, u32[]{:S(2)}, u32[]{:S(2)}) collective-permute-start(f32[8,128]{1,0:T(8,128)S(1)} %reshape.54), channel_id=1, source_target_pairs={{1,0},{2,1},{3,2},{0,3},{5,4},{6,5},{7,6},{4,7},{9,8},{10,9},{11,1... | collective-permute-start | bytes 12296 | tf_op jit(solution)/shard_map/ppermute | solution.py:204
  9.5 1.5 %collective-permute-start.7 = (f32[4,8,128]{2,1,0:T(8,128)S(1)}, f32[4,8,128]{2,1,0:T(8,128)S(1)}, u32[]{:S(2)}, u32[]{:S(2)}) collective-permute-start(f32[4,8,128]{2,1,0:T(8,128)S(1)} %get-tuple-element.28), channel_id=1, source_target_pairs={{32,0},{64,32},{96,64},{0,96},{33,1},{65,33},{97,65},{1,97},{34,2}... | collective-permute-start | bytes 49160 | tf_op jit(solution)/shard_map/ppermute | solution.py:206
  11.5 0.7 copy-done.5
  12.2 2.3 %collective-permute-done.7 = f32[4,8,128]{2,1,0:T(8,128)S(1)} collective-permute-done((f32[4,8,128]{2,1,0:T(8,128)S(1)}, f32[4,8,128]{2,1,0:T(8,128)S(1)}, u32[]{:S(2)}, u32[]{:S(2)}) %collective-permute-start.7) | collective-permute-done | bytes 16416 | tf_op jit(solution)/shard_map/ppermute | solution.py:206
  14.5 1.9 %collective-permute-start.8 = (f32[16,4,128]{2,1,0:T(4,128)S(1)}, f32[16,4,128]{2,1,0:T(4,128)S(1)}, u32[]{:S(2)}, u32[]{:S(2)}) collective-permute-start(f32[16,4,128]{2,1,0:T(4,128)S(1)} %get-tuple-element.24), channel_id=1, source_target_pairs={{0,4},{4,8},{8,12},{12,16},{16,20},{20,24},{24,28},{28,0},{1,5},{5... | collective-permute-start | bytes 98312 | tf_op jit(solution)/shard_map/ppermute | solution.py:206
  16.4 0.2 collective-permute-start.9
  16.7 1.8 %collective-permute-done.8 = f32[16,4,128]{2,1,0:T(4,128)S(1)} collective-permute-done((f32[16,4,128]{2,1,0:T(4,128)S(1)}, f32[16,4,128]{2,1,0:T(4,128)S(1)}, u32[]{:S(2)}, u32[]{:S(2)}) %collective-permute-start.8) | collective-permute-done | bytes 32800 | tf_op jit(solution)/shard_map/ppermute | solution.py:206
  18.5 5.4 %collective-permute-done.9 = f32[16,4,128]{2,1,0:T(4,128)S(1)} collective-permute-done((f32[16,4,128]{2,1,0:T(4,128)S(1)}, f32[16,4,128]{2,1,0:T(4,128)S(1)}, u32[]{:S(2)}, u32[]{:S(2)}) %collective-permute-start.9) | collective-permute-done | bytes 32800 | tf_op jit(solution)/shard_map/ppermute | solution.py:206
  24.4 1.7 %collective-permute-start.10 = (f32[8,128]{1,0:T(8,128)S(1)}, f32[8,128]{1,0:T(8,128)S(1)}, u32[]{:S(2)}, u32[]{:S(2)}) collective-permute-start(f32[8,128]{1,0:T(8,128)S(1)} %reshape.56), channel_id=1, source_target_pairs={{1,0},{2,1},{3,2},{0,3},{5,4},{6,5},{7,6},{4,7},{9,8},{10,9},{11,1... | collective-permute-start | bytes 12296 | tf_op jit(solution)/shard_map/ppermute | solution.py:204
  26.2 2.0 %collective-permute-start.3 = (f32[1,16,4,128]{3,2,1,0:T(4,128)S(1)}, f32[1,16,4,128]{3,2,1,0:T(4,128)S(1)}, u32[]{:S(2)}, u32[]{:S(2)}) collective-permute-start(f32[1,16,4,128]{3,2,1,0:T(4,128)S(1)} %get-tuple-element.15), channel_id=1, source_target_pairs={{4,0},{8,4},{12,8},{16,12},{20,16},{24,20},{28,24},{0,28},{5,1},{9... | collective-permute-start | bytes 98312 | tf_op jit(solution)/shard_map/ppermute | solution.py:206
  28.2 0.1 reshape.57
  28.7 0.7 copy-done.1
  29.5 4.2 %shard_map.60 = (f32[8,8,128]{2,1,0:T(8,128)S(1)}, f32[3,8,8,128]{3,2,1,0:T(8,128)S(1)}) custom-call(f32[16,16,256]{2,1,0:T(8,128)S(1)} %pad_maximum_fusion.1.wrapped_ref, s32[2,2,3,8,8,128]{5,4,3,2,1,0:T(8,128)S(1)} %copy-done.1, f32[2,2,3,8,8,128]{5,4,3,2,1,0:T(8,128)S(1)} %copy-done.3), custom_call_target="tpu_custom_call" | custom-call | flops 40000000 | bytes 2000000 | tf_op jit(solution)/shard_map/pallas_call | solution.py:183
  33.7 0.3 collective-permute-start.12
  34.1 1.8 %collective-permute-start.13 = (f32[4,8,128]{2,1,0:T(8,128)S(1)}, f32[4,8,128]{2,1,0:T(8,128)S(1)}, u32[]{:S(2)}, u32[]{:S(2)}) collective-permute-start(f32[4,8,128]{2,1,0:T(8,128)S(1)} %get-tuple-element.26), channel_id=1, source_target_pairs={{32,0},{64,32},{96,64},{0,96},{33,1},{65,33},{97,65},{1,97},{34,2}... | collective-permute-start | bytes 49160 | tf_op jit(solution)/shard_map/ppermute | solution.py:206
  35.9 1.6 %collective-permute-done.12 = f32[4,8,128]{2,1,0:T(8,128)S(1)} collective-permute-done((f32[4,8,128]{2,1,0:T(8,128)S(1)}, f32[4,8,128]{2,1,0:T(8,128)S(1)}, u32[]{:S(2)}, u32[]{:S(2)}) %collective-permute-start.12) | collective-permute-done | bytes 16416 | tf_op jit(solution)/shard_map/ppermute | solution.py:206
  37.5 1.6 %collective-permute-done.13 = f32[4,8,128]{2,1,0:T(8,128)S(1)} collective-permute-done((f32[4,8,128]{2,1,0:T(8,128)S(1)}, f32[4,8,128]{2,1,0:T(8,128)S(1)}, u32[]{:S(2)}, u32[]{:S(2)}) %collective-permute-start.13) | collective-permute-done | bytes 16416 | tf_op jit(solution)/shard_map/ppermute | solution.py:206
  39.1 3.8 %collective-permute-start.14 = (f32[16,4,128]{2,1,0:T(4,128)S(1)}, f32[16,4,128]{2,1,0:T(4,128)S(1)}, u32[]{:S(2)}, u32[]{:S(2)}) collective-permute-start(f32[16,4,128]{2,1,0:T(4,128)S(1)} %get-tuple-element.22), channel_id=1, source_target_pairs={{0,4},{4,8},{8,12},{12,16},{16,20},{20,24},{24,28},{28,0},{1,5},{5... | collective-permute-start | bytes 98312 | tf_op jit(solution)/shard_map/ppermute | solution.py:206
  42.9 0.3 collective-permute-start.4
  43.2 1.7 %collective-permute-start.5 = (f32[1,4,8,128]{3,2,1,0:T(8,128)S(1)}, f32[1,4,8,128]{3,2,1,0:T(8,128)S(1)}, u32[]{:S(2)}, u32[]{:S(2)}) collective-permute-start(f32[1,4,8,128]{3,2,1,0:T(8,128)S(1)} %get-tuple-element.21), channel_id=1, source_target_pairs={{32,0},{64,32},{96,64},{0,96},{33,1},{65,33},{97,65},{1,97},{34,2}... | collective-permute-start | bytes 49160 | tf_op jit(solution)/shard_map/ppermute | solution.py:206
  44.9 5.5 %collective-permute-done.15 = f32[16,4,128]{2,1,0:T(4,128)S(1)} collective-permute-done((f32[16,4,128]{2,1,0:T(4,128)S(1)}, f32[16,4,128]{2,1,0:T(4,128)S(1)}, u32[]{:S(2)}, u32[]{:S(2)}) %collective-permute-start.15) | collective-permute-done | bytes 32800 | tf_op jit(solution)/shard_map/ppermute | solution.py:206
  50.9 1.7 %collective-permute-start.16 = (f32[8,128]{1,0:T(8,128)S(1)}, f32[8,128]{1,0:T(8,128)S(1)}, u32[]{:S(2)}, u32[]{:S(2)}) collective-permute-start(f32[8,128]{1,0:T(8,128)S(1)} %reshape.60), channel_id=1, source_target_pairs={{1,0},{2,1},{3,2},{0,3},{5,4},{6,5},{7,6},{4,7},{9,8},{10,9},{11,1... | collective-permute-start | bytes 12296 | tf_op jit(solution)/shard_map/ppermute | solution.py:204
  52.6 12.8 %shard_map.61 = f32[4,16,16,256]{3,2,1,0:T(8,128)S(1)} custom-call(f32[8,8,128]{2,1,0:T(8,128)S(1)} %fusion.9.adjoint_ref, f32[3,8,8,128]{3,2,1,0:T(8,128)S(1)} %get-tuple-element.4.grad_ref, s32[2,2,3,8,8,128]{5,4,3,2,1,0:T(8,128)S(1)} %copy-done.1, f32[2,2,3,8,8,128]{5,4,3,2,1,0:T(8,128)S(1)} %copy-done.3), custom_call_target="tpu_custom_call" | custom-call | flops 40000000 | bytes 2000000 | tf_op jit(solution)/shard_map/pallas_call | solution.py:183
  65.9 13.6 %shard_map.62 = f32[3,16,16,256]{3,2,1,0:T(8,128)S(1)} custom-call(f32[16,16,256]{2,1,0:T(8,128)S(1)} %pad_maximum_fusion.2.wrapped_ref, f32[8,8,128]{2,1,0:T(8,128)S(1)} %copy-done.4, s32[2,2,3,8,8,128]{5,4,3,2,1,0:T(8,128)S(1)} %copy-done.1, f32[2,2,3,8,8,128]{5,4,3,2,1,0:T(8,128)S(1)} %copy-done.3), custom_call_target="tpu_custom_call" | custom-call | flops 40000000 | bytes 2000000 | tf_op jit(solution)/shard_map/pallas_call | solution.py:183
  79.5 0.1 slice_add_fusion
  79.7 0.2 fusion
  79.9 0.3 reshape.64
  80.2 0.3 reshape.66
  80.5 1.8 %collective-permute-start.19 = (f32[32,128]{1,0:T(8,128)S(1)}, f32[32,128]{1,0:T(8,128)S(1)}, u32[]{:S(2)}, u32[]{:S(2)}) collective-permute-start(f32[32,128]{1,0:T(8,128)S(1)} %reshape.66), channel_id=1, source_target_pairs={{1,0},{2,1},{3,2},{0,3},{5,4},{6,5},{7,6},{4,7},{9,8},{10,9},{11,1... | collective-permute-start | bytes 49160 | tf_op jit(solution)/shard_map/ppermute | solution.py:204
  82.3 1.1 %collective-permute-done.18 = f32[32,128]{1,0:T(8,128)S(1)} collective-permute-done((f32[32,128]{1,0:T(8,128)S(1)}, f32[32,128]{1,0:T(8,128)S(1)}, u32[]{:S(2)}, u32[]{:S(2)}) %collective-permute-start.18) | collective-permute-done | bytes 16416 | tf_op jit(solution)/shard_map/ppermute | solution.py:204
  83.4 0.5 reshape.65
  83.9 0.5 reshape.67
  84.5 0.2 fusion.3
  84.7 1.2 %collective-permute-start.20 = (f32[4,16,4,128]{3,2,1,0:T(4,128)S(1)}, f32[4,16,4,128]{3,2,1,0:T(4,128)S(1)}, u32[]{:S(2)}, u32[]{:S(2)}) collective-permute-start(f32[4,16,4,128]{3,2,1,0:T(4,128)S(1)} %get-tuple-element.8), channel_id=1, source_target_pairs={{0,4},{4,8},{8,12},{12,16},{16,20},{20,24},{24,28},{28,0},{1,5},{5... | collective-permute-start | bytes 393224 | tf_op jit(solution)/shard_map/ppermute | solution.py:206
  86.0 0.9 collective-permute-start.21
  86.8 4.0 %collective-permute-done.20 = f32[4,16,4,128]{3,2,1,0:T(4,128)S(1)} collective-permute-done((f32[4,16,4,128]{3,2,1,0:T(4,128)S(1)}, f32[4,16,4,128]{3,2,1,0:T(4,128)S(1)}, u32[]{:S(2)}, u32[]{:S(2)}) %collective-permute-start.20) | collective-permute-done | bytes 131104 | tf_op jit(solution)/shard_map/ppermute | solution.py:206
  90.8 5.1 %collective-permute-done.21 = f32[4,16,4,128]{3,2,1,0:T(4,128)S(1)} collective-permute-done((f32[4,16,4,128]{3,2,1,0:T(4,128)S(1)}, f32[4,16,4,128]{3,2,1,0:T(4,128)S(1)}, u32[]{:S(2)}, u32[]{:S(2)}) %collective-permute-start.21) | collective-permute-done | bytes 131104 | tf_op jit(solution)/shard_map/ppermute | solution.py:206
  96.0 0.6 collective-permute-start.22
  96.5 1.5 %collective-permute-start.23 = (f32[4,4,8,128]{3,2,1,0:T(8,128)S(1)}, f32[4,4,8,128]{3,2,1,0:T(8,128)S(1)}, u32[]{:S(2)}, u32[]{:S(2)}) collective-permute-start(f32[4,4,8,128]{3,2,1,0:T(8,128)S(1)} %get-tuple-element.11), channel_id=1, source_target_pairs={{32,0},{64,32},{96,64},{0,96},{33,1},{65,33},{97,65},{1,97},{34,2}... | collective-permute-start | bytes 196616 | tf_op jit(solution)/shard_map/ppermute | solution.py:206
  98.1 2.2 %collective-permute-done.22 = f32[4,4,8,128]{3,2,1,0:T(8,128)S(1)} collective-permute-done((f32[4,4,8,128]{3,2,1,0:T(8,128)S(1)}, f32[4,4,8,128]{3,2,1,0:T(8,128)S(1)}, u32[]{:S(2)}, u32[]{:S(2)}) %collective-permute-start.22) | collective-permute-done | bytes 65568 | tf_op jit(solution)/shard_map/ppermute | solution.py:206
  100.3 1.7 %collective-permute-done.23 = f32[4,4,8,128]{3,2,1,0:T(8,128)S(1)} collective-permute-done((f32[4,4,8,128]{3,2,1,0:T(8,128)S(1)}, f32[4,4,8,128]{3,2,1,0:T(8,128)S(1)}, u32[]{:S(2)}, u32[]{:S(2)}) %collective-permute-start.23) | collective-permute-done | bytes 65568 | tf_op jit(solution)/shard_map/ppermute | solution.py:206
  102.0 0.6 slice_bitcast_fusion
  102.7 0.6 slice.166
  (66 shorter events, 2.9 us)
Async XLA Ops:
  0.6 1.2 %copy-start.4 = (f32[8,8,128]{2,1,0:T(8,128)S(1)}, f32[8,8,128]{2,1,0:T(8,128)}, u32[]{:S(2)}) copy-start(f32[8,8,128]{2,1,0:T(8,128)} %cot_ref.3) | copy-start | bytes 98308
  1.4 10.1 %collective-permute-start.6 = (f32[4,8,128]{2,1,0:T(8,128)S(1)}, f32[4,8,128]{2,1,0:T(8,128)S(1)}, u32[]{:S(2)}, u32[]{:S(2)}) collective-permute-start(f32[4,8,128]{2,1,0:T(8,128)S(1)} %get-tuple-element.29), channel_id=1, source_target_pairs={{0,32},{32,64},{64,96},{96,0},{1,33},{33,65},{65,97},{97,1},{2,34}... | collective-permute-start | bytes 49160 | tf_op jit(solution)/shard_map/ppermute | solution.py:206
  1.9 1.0 copy-start
  2.9 1.0 copy-start.2
  7.5 3.6 %collective-permute-start = (f32[8,128]{1,0:T(8,128)S(1)}, f32[8,128]{1,0:T(8,128)S(1)}, u32[]{:S(2)}, u32[]{:S(2)}) collective-permute-start(f32[8,128]{1,0:T(8,128)S(1)} %reshape.52), channel_id=1, source_target_pairs={{0,1},{1,2},{2,3},{3,0},{4,5},{5,6},{6,7},{7,4},{8,9},{9,10},{10,1... | collective-permute-start | bytes 12296 | tf_op jit(solution)/shard_map/ppermute | solution.py:204
  7.7 3.6 %collective-permute-start.1 = (f32[8,128]{1,0:T(8,128)S(1)}, f32[8,128]{1,0:T(8,128)S(1)}, u32[]{:S(2)}, u32[]{:S(2)}) collective-permute-start(f32[8,128]{1,0:T(8,128)S(1)} %reshape.54), channel_id=1, source_target_pairs={{1,0},{2,1},{3,2},{0,3},{5,4},{6,5},{7,6},{4,7},{9,8},{10,9},{11,1... | collective-permute-start | bytes 12296 | tf_op jit(solution)/shard_map/ppermute | solution.py:204
  9.5 4.9 %collective-permute-start.7 = (f32[4,8,128]{2,1,0:T(8,128)S(1)}, f32[4,8,128]{2,1,0:T(8,128)S(1)}, u32[]{:S(2)}, u32[]{:S(2)}) collective-permute-start(f32[4,8,128]{2,1,0:T(8,128)S(1)} %get-tuple-element.28), channel_id=1, source_target_pairs={{32,0},{64,32},{96,64},{0,96},{33,1},{65,33},{97,65},{1,97},{34,2}... | collective-permute-start | bytes 49160 | tf_op jit(solution)/shard_map/ppermute | solution.py:206
  11.5 0.8 copy-start.5
  14.5 4.0 %collective-permute-start.8 = (f32[16,4,128]{2,1,0:T(4,128)S(1)}, f32[16,4,128]{2,1,0:T(4,128)S(1)}, u32[]{:S(2)}, u32[]{:S(2)}) collective-permute-start(f32[16,4,128]{2,1,0:T(4,128)S(1)} %get-tuple-element.24), channel_id=1, source_target_pairs={{0,4},{4,8},{8,12},{12,16},{16,20},{20,24},{24,28},{28,0},{1,5},{5... | collective-permute-start | bytes 98312 | tf_op jit(solution)/shard_map/ppermute | solution.py:206
  16.4 7.5 %collective-permute-start.9 = (f32[16,4,128]{2,1,0:T(4,128)S(1)}, f32[16,4,128]{2,1,0:T(4,128)S(1)}, u32[]{:S(2)}, u32[]{:S(2)}) collective-permute-start(f32[16,4,128]{2,1,0:T(4,128)S(1)} %get-tuple-element.25), channel_id=1, source_target_pairs={{4,0},{8,4},{12,8},{16,12},{20,16},{24,20},{28,24},{0,28},{5,1},{9... | collective-permute-start | bytes 98312 | tf_op jit(solution)/shard_map/ppermute | solution.py:206
  24.3 4.1 %collective-permute-start.11 = (f32[8,128]{1,0:T(8,128)S(1)}, f32[8,128]{1,0:T(8,128)S(1)}, u32[]{:S(2)}, u32[]{:S(2)}) collective-permute-start(f32[8,128]{1,0:T(8,128)S(1)} %reshape.58), channel_id=1, source_target_pairs={{0,1},{1,2},{2,3},{3,0},{4,5},{5,6},{6,7},{7,4},{8,9},{9,10},{10,1... | collective-permute-start | bytes 12296 | tf_op jit(solution)/shard_map/ppermute | solution.py:204
  24.4 3.8 %collective-permute-start.10 = (f32[8,128]{1,0:T(8,128)S(1)}, f32[8,128]{1,0:T(8,128)S(1)}, u32[]{:S(2)}, u32[]{:S(2)}) collective-permute-start(f32[8,128]{1,0:T(8,128)S(1)} %reshape.56), channel_id=1, source_target_pairs={{1,0},{2,1},{3,2},{0,3},{5,4},{6,5},{7,6},{4,7},{9,8},{10,9},{11,1... | collective-permute-start | bytes 12296 | tf_op jit(solution)/shard_map/ppermute | solution.py:204
  26.1 7.9 %collective-permute-start.2 = (f32[1,16,4,128]{3,2,1,0:T(4,128)S(1)}, f32[1,16,4,128]{3,2,1,0:T(4,128)S(1)}, u32[]{:S(2)}, u32[]{:S(2)}) collective-permute-start(f32[1,16,4,128]{3,2,1,0:T(4,128)S(1)} %get-tuple-element.14), channel_id=1, source_target_pairs={{0,4},{4,8},{8,12},{12,16},{16,20},{20,24},{24,28},{28,0},{1,5},{5... | collective-permute-start | bytes 98312 | tf_op jit(solution)/shard_map/ppermute | solution.py:206
  26.2 7.9 %collective-permute-start.3 = (f32[1,16,4,128]{3,2,1,0:T(4,128)S(1)}, f32[1,16,4,128]{3,2,1,0:T(4,128)S(1)}, u32[]{:S(2)}, u32[]{:S(2)}) collective-permute-start(f32[1,16,4,128]{3,2,1,0:T(4,128)S(1)} %get-tuple-element.15), channel_id=1, source_target_pairs={{4,0},{8,4},{12,8},{16,12},{20,16},{24,20},{28,24},{0,28},{5,1},{9... | collective-permute-start | bytes 98312 | tf_op jit(solution)/shard_map/ppermute | solution.py:206
  28.4 1.0 copy-start.1
  28.4 1.1 %copy-start.3 = (f32[2,2,3,8,8,128]{5,4,3,2,1,0:T(8,128)S(1)}, f32[2,2,3,8,8,128]{5,4,3,2,1,0:T(8,128)}, u32[]{:S(2)}) copy-start(f32[2,2,3,8,8,128]{5,4,3,2,1,0:T(8,128)} %fracs_ref.7) | copy-start | bytes 1179652
  33.7 3.8 %collective-permute-start.12 = (f32[4,8,128]{2,1,0:T(8,128)S(1)}, f32[4,8,128]{2,1,0:T(8,128)S(1)}, u32[]{:S(2)}, u32[]{:S(2)}) collective-permute-start(f32[4,8,128]{2,1,0:T(8,128)S(1)} %get-tuple-element.27), channel_id=1, source_target_pairs={{0,32},{32,64},{64,96},{96,0},{1,33},{33,65},{65,97},{97,1},{2,34}... | collective-permute-start | bytes 49160 | tf_op jit(solution)/shard_map/ppermute | solution.py:206
  34.1 5.0 %collective-permute-start.13 = (f32[4,8,128]{2,1,0:T(8,128)S(1)}, f32[4,8,128]{2,1,0:T(8,128)S(1)}, u32[]{:S(2)}, u32[]{:S(2)}) collective-permute-start(f32[4,8,128]{2,1,0:T(8,128)S(1)} %get-tuple-element.26), channel_id=1, source_target_pairs={{32,0},{64,32},{96,64},{0,96},{33,1},{65,33},{97,65},{1,97},{34,2}... | collective-permute-start | bytes 49160 | tf_op jit(solution)/shard_map/ppermute | solution.py:206
  39.1 5.8 %collective-permute-start.14 = (f32[16,4,128]{2,1,0:T(4,128)S(1)}, f32[16,4,128]{2,1,0:T(4,128)S(1)}, u32[]{:S(2)}, u32[]{:S(2)}) collective-permute-start(f32[16,4,128]{2,1,0:T(4,128)S(1)} %get-tuple-element.22), channel_id=1, source_target_pairs={{0,4},{4,8},{8,12},{12,16},{16,20},{20,24},{24,28},{28,0},{1,5},{5... | collective-permute-start | bytes 98312 | tf_op jit(solution)/shard_map/ppermute | solution.py:206
  42.9 7.5 %collective-permute-start.15 = (f32[16,4,128]{2,1,0:T(4,128)S(1)}, f32[16,4,128]{2,1,0:T(4,128)S(1)}, u32[]{:S(2)}, u32[]{:S(2)}) collective-permute-start(f32[16,4,128]{2,1,0:T(4,128)S(1)} %get-tuple-element.23), channel_id=1, source_target_pairs={{4,0},{8,4},{12,8},{16,12},{20,16},{24,20},{28,24},{0,28},{5,1},{9... | collective-permute-start | bytes 98312 | tf_op jit(solution)/shard_map/ppermute | solution.py:206
  42.9 9.7 %collective-permute-start.4 = (f32[1,4,8,128]{3,2,1,0:T(8,128)S(1)}, f32[1,4,8,128]{3,2,1,0:T(8,128)S(1)}, u32[]{:S(2)}, u32[]{:S(2)}) collective-permute-start(f32[1,4,8,128]{3,2,1,0:T(8,128)S(1)} %get-tuple-element.20), channel_id=1, source_target_pairs={{0,32},{32,64},{64,96},{96,0},{1,33},{33,65},{65,97},{97,1},{2,34}... | collective-permute-start | bytes 49160 | tf_op jit(solution)/shard_map/ppermute | solution.py:206
  43.2 9.4 %collective-permute-start.5 = (f32[1,4,8,128]{3,2,1,0:T(8,128)S(1)}, f32[1,4,8,128]{3,2,1,0:T(8,128)S(1)}, u32[]{:S(2)}, u32[]{:S(2)}) collective-permute-start(f32[1,4,8,128]{3,2,1,0:T(8,128)S(1)} %get-tuple-element.21), channel_id=1, source_target_pairs={{32,0},{64,32},{96,64},{0,96},{33,1},{65,33},{97,65},{1,97},{34,2}... | collective-permute-start | bytes 49160 | tf_op jit(solution)/shard_map/ppermute | solution.py:206
  50.8 14.8 %collective-permute-start.17 = (f32[8,128]{1,0:T(8,128)S(1)}, f32[8,128]{1,0:T(8,128)S(1)}, u32[]{:S(2)}, u32[]{:S(2)}) collective-permute-start(f32[8,128]{1,0:T(8,128)S(1)} %reshape.62), channel_id=1, source_target_pairs={{0,1},{1,2},{2,3},{3,0},{4,5},{5,6},{6,7},{7,4},{8,9},{9,10},{10,1... | collective-permute-start | bytes 12296 | tf_op jit(solution)/shard_map/ppermute | solution.py:204
  50.9 14.6 %collective-permute-start.16 = (f32[8,128]{1,0:T(8,128)S(1)}, f32[8,128]{1,0:T(8,128)S(1)}, u32[]{:S(2)}, u32[]{:S(2)}) collective-permute-start(f32[8,128]{1,0:T(8,128)S(1)} %reshape.60), channel_id=1, source_target_pairs={{1,0},{2,1},{3,2},{0,3},{5,4},{6,5},{7,6},{4,7},{9,8},{10,9},{11,1... | collective-permute-start | bytes 12296 | tf_op jit(solution)/shard_map/ppermute | solution.py:204
  80.1 3.2 %collective-permute-start.18 = (f32[32,128]{1,0:T(8,128)S(1)}, f32[32,128]{1,0:T(8,128)S(1)}, u32[]{:S(2)}, u32[]{:S(2)}) collective-permute-start(f32[32,128]{1,0:T(8,128)S(1)} %reshape.64), channel_id=1, source_target_pairs={{0,1},{1,2},{2,3},{3,0},{4,5},{5,6},{6,7},{7,4},{8,9},{9,10},{10,1... | collective-permute-start | bytes 49160 | tf_op jit(solution)/shard_map/ppermute | solution.py:204
  80.5 3.4 %collective-permute-start.19 = (f32[32,128]{1,0:T(8,128)S(1)}, f32[32,128]{1,0:T(8,128)S(1)}, u32[]{:S(2)}, u32[]{:S(2)}) collective-permute-start(f32[32,128]{1,0:T(8,128)S(1)} %reshape.66), channel_id=1, source_target_pairs={{1,0},{2,1},{3,2},{0,3},{5,4},{6,5},{7,6},{4,7},{9,8},{10,9},{11,1... | collective-permute-start | bytes 49160 | tf_op jit(solution)/shard_map/ppermute | solution.py:204
  84.7 6.1 %collective-permute-start.20 = (f32[4,16,4,128]{3,2,1,0:T(4,128)S(1)}, f32[4,16,4,128]{3,2,1,0:T(4,128)S(1)}, u32[]{:S(2)}, u32[]{:S(2)}) collective-permute-start(f32[4,16,4,128]{3,2,1,0:T(4,128)S(1)} %get-tuple-element.8), channel_id=1, source_target_pairs={{0,4},{4,8},{8,12},{12,16},{16,20},{20,24},{24,28},{28,0},{1,5},{5... | collective-permute-start | bytes 393224 | tf_op jit(solution)/shard_map/ppermute | solution.py:206
  86.0 9.9 %collective-permute-start.21 = (f32[4,16,4,128]{3,2,1,0:T(4,128)S(1)}, f32[4,16,4,128]{3,2,1,0:T(4,128)S(1)}, u32[]{:S(2)}, u32[]{:S(2)}) collective-permute-start(f32[4,16,4,128]{3,2,1,0:T(4,128)S(1)} %get-tuple-element.9), channel_id=1, source_target_pairs={{4,0},{8,4},{12,8},{16,12},{20,16},{24,20},{28,24},{0,28},{5,1},{9... | collective-permute-start | bytes 393224 | tf_op jit(solution)/shard_map/ppermute | solution.py:206
  96.0 4.3 %collective-permute-start.22 = (f32[4,4,8,128]{3,2,1,0:T(8,128)S(1)}, f32[4,4,8,128]{3,2,1,0:T(8,128)S(1)}, u32[]{:S(2)}, u32[]{:S(2)}) collective-permute-start(f32[4,4,8,128]{3,2,1,0:T(8,128)S(1)} %get-tuple-element.10), channel_id=1, source_target_pairs={{0,32},{32,64},{64,96},{96,0},{1,33},{33,65},{65,97},{97,1},{2,34}... | collective-permute-start | bytes 196616 | tf_op jit(solution)/shard_map/ppermute | solution.py:206
  96.5 5.5 %collective-permute-start.23 = (f32[4,4,8,128]{3,2,1,0:T(8,128)S(1)}, f32[4,4,8,128]{3,2,1,0:T(8,128)S(1)}, u32[]{:S(2)}, u32[]{:S(2)}) collective-permute-start(f32[4,4,8,128]{3,2,1,0:T(8,128)S(1)} %get-tuple-element.11), channel_id=1, source_target_pairs={{32,0},{64,32},{96,64},{0,96},{33,1},{65,33},{97,65},{1,97},{34,2}... | collective-permute-start | bytes 196616 | tf_op jit(solution)/shard_map/ppermute | solution.py:206

commit v4 on v3

--- a/solution.py
+++ b/solution.py
@@ -97,7 +97,7 @@
     return value, (grad_x, grad_y, grad_z)
 
 
-def spread_block(field, weight_refs, product_ref, staged_ref, pz):
+def spread_block(field, weight_refs, product_ref, staged_ref, summed_ref, pz):
     table_x, table_y, table_z = weight_refs
     nx, ny, nz = field.shape
     px, py = nx + 2 * MARGIN, ny + 2 * MARGIN
@@ -105,7 +105,7 @@
         weighted = table_y[sy] * field
         for sx in range(SHIFTS):
             product_ref[sy, sx] = table_x[sx] * weighted
-    def along_z(sz, total):
+    def along_z(sz, carry):
         weight_z = table_z[sz]
         for sy in range(SHIFTS):
             rows = [None] * px
@@ -120,11 +120,15 @@
         summed = jnp.zeros((px, py, nz), jnp.float32)
         for sy in range(SHIFTS):
             summed = summed + staged_ref[sy, :, 7 - sy : 7 - sy + py, :]
-        padded = jnp.concatenate([summed, jnp.zeros((px, py, pz - nz), jnp.float32)], axis=2)
-        shift = lax.rem(sz + (pz - 3), pz)
-        return total + pltpu.roll(padded, shift, 2)
-
-    total = lax.fori_loop(0, SHIFTS, along_z, jnp.zeros((px, py, pz), jnp.float32))
+        summed_ref[sz] = summed
+        return carry
+
+    lax.fori_loop(0, SHIFTS, along_z, 0)
+    total = jnp.zeros((px, py, pz), jnp.float32)
+    gap = jnp.zeros((px, py, pz - nz), jnp.float32)
+    for sz in range(SHIFTS):
+        padded = jnp.concatenate([summed_ref[sz], gap], axis=2)
+        total = total + roll_lanes(padded, sz - 3)
     return total
 
 
@@ -146,14 +150,15 @@
         grad_ref[component] = grads[component]
 
 
-def late_spread_kernel(cot_ref, cells_ref, fracs_ref, out_ref, product_ref, staged_ref, *tables):
+def late_spread_kernel(cot_ref, cells_ref, fracs_ref, out_ref, product_ref, staged_ref, summed_ref, *tables):
     build_tables(cells_ref, fracs_ref, 1, 1, tables, None)
     clear_rims(staged_ref)
-    out_ref[...] = spread_block(cot_ref[...], tables, product_ref, staged_ref, out_ref.shape[-1])
+    out_ref[...] = spread_block(cot_ref[...], tables, product_ref, staged_ref, summed_ref,
+                                out_ref.shape[-1])
 
 
 def late_velocity_kernel(wrapped_ref, cot_ref, cells_ref, fracs_ref, out_ref,
-                         rolled_ref, window_ref, product_ref, staged_ref, *tables):
+                         rolled_ref, window_ref, product_ref, staged_ref, summed_ref, *tables):
     weights, slopes, mid = tables[:3], tables[3:6], tables[6:]
     build_tables(cells_ref, fracs_ref, 1, 1, weights, slopes)
     build_tables(cells_ref, fracs_ref, 1, 0, mid, None)
@@ -161,22 +166,22 @@
     cot = cot_ref[...]
     clear_rims(staged_ref)
     for component in range(3):
-        out_ref[component] = spread_block(cot * grads[component], mid, product_ref, staged_ref,
+        out_ref[component] = spread_block(cot * grads[component], mid, product_ref, staged_ref, summed_ref,
                                           out_ref.shape[-1])
 
 
 def early_spread_kernel(adjoint_ref, grad_ref, cells_ref, fracs_ref, out_ref,
-                        product_ref, staged_ref, *tables):
+                        product_ref, staged_ref, summed_ref, *tables):
     dep, mid = tables[:3], tables[3:]
     build_tables(cells_ref, fracs_ref, 0, 1, dep, None)
     build_tables(cells_ref, fracs_ref, 0, 0, mid, None)
     adjoint = adjoint_ref[...]
     clear_rims(staged_ref)
     pz = out_ref.shape[-1]
-    out_ref[0] = spread_block(adjoint, dep, product_ref, staged_ref, pz)
+    out_ref[0] = spread_block(adjoint, dep, product_ref, staged_ref, summed_ref, pz)
     for component in range(3):
         out_ref[1 + component] = spread_block(adjoint * grad_ref[component], mid, product_ref,
-                                              staged_ref, pz)
+                                              staged_ref, summed_ref, pz)
 
 
 def vmem_call(kernel, out_shapes, scratch, *args):
@@ -261,6 +266,7 @@
     windows = pltpu.VMEM((SHIFTS, SHIFTS, px, ny, nz), f32)
     products = pltpu.VMEM((SHIFTS, SHIFTS) + block, f32)
     staged = pltpu.VMEM((SHIFTS, px, ny + 16, nz), f32)
+    summed = pltpu.VMEM((SHIFTS, px, py, nz), f32)
 
     wrapped = widen(intensity, pz)
     image_mid, grad_raw = vmem_call(
@@ -272,21 +278,21 @@
     adjoint_padded = vmem_call(
         late_spread_kernel,
         jax.ShapeDtypeStruct((px, py, pz), f32),
-        [products, staged] + table_scratch(block, 3),
+        [products, staged, summed] + table_scratch(block, 3),
         cotangent, cells, fracs,
     )
     adjoint_mid = fold(adjoint_padded[None], nz)[0]
     early_padded = vmem_call(
         early_spread_kernel,
         jax.ShapeDtypeStruct((4, px, py, pz), f32),
-        [products, staged] + table_scratch(block, 6),
+        [products, staged, summed] + table_scratch(block, 6),
         adjoint_mid, grad_raw, cells, fracs,
     )
     wrapped_mid = widen(image_mid, pz)
     velocity_padded = vmem_call(
         late_velocity_kernel,
         jax.ShapeDtypeStruct((3, px, py, pz), f32),
-        [rolled, windows, products, staged] + table_scratch(block, 9),
+        [rolled, windows, products, staged, summed] + table_scratch(block, 9),
         wrapped_mid, cotangent, cells, fracs,
     )
     deposits = jnp.concatenate([early_padded[:1], early_padded[1:] + velocity_padded])

time: 104 us -> 95.1 us (0.914)
  Pallas kernels: 34.1 us -> 25.6 us
    pallas_call x4, Pallas kernels: 34.1 us -> 25.6 us  [vmem_call(): pl.pallas_call(kernel, out_shape=out_shapes, in_specs=[pl.BlockSpec(memor...]
  transfers between devices with their start and end apart: 24 -> 24, of which waited for: 11 -> 11; matrix products, arithmetic and copies ran while one was open for 2% -> 3% of each run, Pallas kernels for 20% -> 16%
where the time goes in v4:
time: 95.1 us; the launch traced here: 94.8 us
  waiting for transfers between devices  32.3 us (34%)
  starting transfers between devices  25.7 us (27%)
  Pallas kernels  25.6 us (27%)
  local copies, waits for them, and re-layouts  9.17 us (10%)
  other arithmetic  1.04 us (1%)
  between operations  1.01 us (1%)
    ppermute x16, waiting for transfers between devices, shift_from(): return lax.ppermute(piece, axis, pairs)  31.2 us
    pallas_call x4, Pallas kernels, vmem_call(): pl.pallas_call(kernel, out_shape=out_shapes, in_specs=[pl.BlockSpec(memor...  25.6 us
    ppermute x16, starting transfers between devices, shift_from(): return lax.ppermute(piece, axis, pairs)  18.4 us
    ppermute x8, starting transfers between devices, shift_from(): flat = lax.ppermute(piece.reshape(-1, 128), axis, pairs)  7.36 us
    unnamed x16, local copies, waits for them, and re-layouts  3.59 us
  transfers between devices with their start and end apart: 24, of which 11 were waited for; matrix products, arithmetic and copies ran while one was open for 3% of the time, Pallas kernels for 16%

profile of v4, /device:TPU:102, one launch (start us, length us, event | category | flops | bytes accessed | tf_op | source)
XLA Modules:
  0.0 94.8 jit_solution(5671659249117789822)
XLA Ops:
  0.6 0.7 fusion.20
  1.4 0.5 collective-permute-start.6
  1.9 1.0 %copy-done = s32[2,2,3,8,8,128]{5,4,3,2,1,0:T(8,128)S(1)} copy-done((s32[2,2,3,8,8,128]{5,4,3,2,1,0:T(8,128)S(1)}, s32[2,2,3,8,8,128]{5,4,3,2,1,0:T(8,128)}, u32[]{:S(2)}) %copy-start) | copy-done | bytes 393240
  2.9 1.0 %copy-done.2 = f32[2,2,3,8,8,128]{5,4,3,2,1,0:T(8,128)S(1)} copy-done((f32[2,2,3,8,8,128]{5,4,3,2,1,0:T(8,128)S(1)}, f32[2,2,3,8,8,128]{5,4,3,2,1,0:T(8,128)}, u32[]{:S(2)}) %copy-start.2) | copy-done | bytes 393240
  3.9 2.4 %shard_map.59 = f32[16,16,256]{2,1,0:T(8,128)S(1)} custom-call(f32[8,8,128]{2,1,0:T(8,128)S(1)} %copy-done.4, s32[2,2,3,8,8,128]{5,4,3,2,1,0:T(8,128)S(1)} %copy-done, f32[2,2,3,8,8,128]{5,4,3,2,1,0:T(8,128)S(1)} %copy-done.2), custom_call_target="tpu_custom_call" | custom-call | flops 40000000 | bytes 2000000 | tf_op jit(solution)/shard_map/pallas_call | solution.py:188
  6.7 1.8 %collective-permute-start.1 = (f32[8,128]{1,0:T(8,128)S(1)}, f32[8,128]{1,0:T(8,128)S(1)}, u32[]{:S(2)}, u32[]{:S(2)}) collective-permute-start(f32[8,128]{1,0:T(8,128)S(1)} %reshape.54), channel_id=1, source_target_pairs={{1,0},{2,1},{3,2},{0,3},{5,4},{6,5},{7,6},{4,7},{9,8},{10,9},{11,1... | collective-permute-start | bytes 12296 | tf_op jit(solution)/shard_map/ppermute | solution.py:209
  8.5 1.5 %collective-permute-start.7 = (f32[4,8,128]{2,1,0:T(8,128)S(1)}, f32[4,8,128]{2,1,0:T(8,128)S(1)}, u32[]{:S(2)}, u32[]{:S(2)}) collective-permute-start(f32[4,8,128]{2,1,0:T(8,128)S(1)} %get-tuple-element.28), channel_id=1, source_target_pairs={{32,0},{64,32},{96,64},{0,96},{33,1},{65,33},{97,65},{1,97},{34,2}... | collective-permute-start | bytes 49160 | tf_op jit(solution)/shard_map/ppermute | solution.py:211
  10.5 0.7 copy-done.5
  11.2 2.3 %collective-permute-done.7 = f32[4,8,128]{2,1,0:T(8,128)S(1)} collective-permute-done((f32[4,8,128]{2,1,0:T(8,128)S(1)}, f32[4,8,128]{2,1,0:T(8,128)S(1)}, u32[]{:S(2)}, u32[]{:S(2)}) %collective-permute-start.7) | collective-permute-done | bytes 16416 | tf_op jit(solution)/shard_map/ppermute | solution.py:211
  13.5 1.9 %collective-permute-start.8 = (f32[16,4,128]{2,1,0:T(4,128)S(1)}, f32[16,4,128]{2,1,0:T(4,128)S(1)}, u32[]{:S(2)}, u32[]{:S(2)}) collective-permute-start(f32[16,4,128]{2,1,0:T(4,128)S(1)} %get-tuple-element.24), channel_id=1, source_target_pairs={{0,4},{4,8},{8,12},{12,16},{16,20},{20,24},{24,28},{28,0},{1,5},{5... | collective-permute-start | bytes 98312 | tf_op jit(solution)/shard_map/ppermute | solution.py:211
  15.4 0.2 collective-permute-start.9
  15.7 1.8 %collective-permute-done.8 = f32[16,4,128]{2,1,0:T(4,128)S(1)} collective-permute-done((f32[16,4,128]{2,1,0:T(4,128)S(1)}, f32[16,4,128]{2,1,0:T(4,128)S(1)}, u32[]{:S(2)}, u32[]{:S(2)}) %collective-permute-start.8) | collective-permute-done | bytes 32800 | tf_op jit(solution)/shard_map/ppermute | solution.py:211
  17.5 5.4 %collective-permute-done.9 = f32[16,4,128]{2,1,0:T(4,128)S(1)} collective-permute-done((f32[16,4,128]{2,1,0:T(4,128)S(1)}, f32[16,4,128]{2,1,0:T(4,128)S(1)}, u32[]{:S(2)}, u32[]{:S(2)}) %collective-permute-start.9) | collective-permute-done | bytes 32800 | tf_op jit(solution)/shard_map/ppermute | solution.py:211
  23.3 1.7 %collective-permute-start.10 = (f32[8,128]{1,0:T(8,128)S(1)}, f32[8,128]{1,0:T(8,128)S(1)}, u32[]{:S(2)}, u32[]{:S(2)}) collective-permute-start(f32[8,128]{1,0:T(8,128)S(1)} %reshape.56), channel_id=1, source_target_pairs={{1,0},{2,1},{3,2},{0,3},{5,4},{6,5},{7,6},{4,7},{9,8},{10,9},{11,1... | collective-permute-start | bytes 12296 | tf_op jit(solution)/shard_map/ppermute | solution.py:209
  25.2 2.0 %collective-permute-start.3 = (f32[1,16,4,128]{3,2,1,0:T(4,128)S(1)}, f32[1,16,4,128]{3,2,1,0:T(4,128)S(1)}, u32[]{:S(2)}, u32[]{:S(2)}) collective-permute-start(f32[1,16,4,128]{3,2,1,0:T(4,128)S(1)} %get-tuple-element.15), channel_id=1, source_target_pairs={{4,0},{8,4},{12,8},{16,12},{20,16},{24,20},{28,24},{0,28},{5,1},{9... | collective-permute-start | bytes 98312 | tf_op jit(solution)/shard_map/ppermute | solution.py:211
  27.2 0.1 reshape.57
  27.6 0.7 copy-done.1
  28.5 4.2 %shard_map.60 = (f32[8,8,128]{2,1,0:T(8,128)S(1)}, f32[3,8,8,128]{3,2,1,0:T(8,128)S(1)}) custom-call(f32[16,16,256]{2,1,0:T(8,128)S(1)} %pad_maximum_fusion.1.wrapped_ref, s32[2,2,3,8,8,128]{5,4,3,2,1,0:T(8,128)S(1)} %copy-done.1, f32[2,2,3,8,8,128]{5,4,3,2,1,0:T(8,128)S(1)} %copy-done.3), custom_call_target="tpu_custom_call" | custom-call | flops 40000000 | bytes 2000000 | tf_op jit(solution)/shard_map/pallas_call | solution.py:188
  32.7 0.3 collective-permute-start.12
  33.1 1.8 %collective-permute-start.13 = (f32[4,8,128]{2,1,0:T(8,128)S(1)}, f32[4,8,128]{2,1,0:T(8,128)S(1)}, u32[]{:S(2)}, u32[]{:S(2)}) collective-permute-start(f32[4,8,128]{2,1,0:T(8,128)S(1)} %get-tuple-element.26), channel_id=1, source_target_pairs={{32,0},{64,32},{96,64},{0,96},{33,1},{65,33},{97,65},{1,97},{34,2}... | collective-permute-start | bytes 49160 | tf_op jit(solution)/shard_map/ppermute | solution.py:211
  34.9 1.6 %collective-permute-done.12 = f32[4,8,128]{2,1,0:T(8,128)S(1)} collective-permute-done((f32[4,8,128]{2,1,0:T(8,128)S(1)}, f32[4,8,128]{2,1,0:T(8,128)S(1)}, u32[]{:S(2)}, u32[]{:S(2)}) %collective-permute-start.12) | collective-permute-done | bytes 16416 | tf_op jit(solution)/shard_map/ppermute | solution.py:211
  36.5 1.6 %collective-permute-done.13 = f32[4,8,128]{2,1,0:T(8,128)S(1)} collective-permute-done((f32[4,8,128]{2,1,0:T(8,128)S(1)}, f32[4,8,128]{2,1,0:T(8,128)S(1)}, u32[]{:S(2)}, u32[]{:S(2)}) %collective-permute-start.13) | collective-permute-done | bytes 16416 | tf_op jit(solution)/shard_map/ppermute | solution.py:211
  38.1 3.8 %collective-permute-start.14 = (f32[16,4,128]{2,1,0:T(4,128)S(1)}, f32[16,4,128]{2,1,0:T(4,128)S(1)}, u32[]{:S(2)}, u32[]{:S(2)}) collective-permute-start(f32[16,4,128]{2,1,0:T(4,128)S(1)} %get-tuple-element.22), channel_id=1, source_target_pairs={{0,4},{4,8},{8,12},{12,16},{16,20},{20,24},{24,28},{28,0},{1,5},{5... | collective-permute-start | bytes 98312 | tf_op jit(solution)/shard_map/ppermute | solution.py:211
  41.9 0.3 collective-permute-start.4
  42.1 1.7 %collective-permute-start.5 = (f32[1,4,8,128]{3,2,1,0:T(8,128)S(1)}, f32[1,4,8,128]{3,2,1,0:T(8,128)S(1)}, u32[]{:S(2)}, u32[]{:S(2)}) collective-permute-start(f32[1,4,8,128]{3,2,1,0:T(8,128)S(1)} %get-tuple-element.21), channel_id=1, source_target_pairs={{32,0},{64,32},{96,64},{0,96},{33,1},{65,33},{97,65},{1,97},{34,2}... | collective-permute-start | bytes 49160 | tf_op jit(solution)/shard_map/ppermute | solution.py:211
  43.9 5.5 %collective-permute-done.15 = f32[16,4,128]{2,1,0:T(4,128)S(1)} collective-permute-done((f32[16,4,128]{2,1,0:T(4,128)S(1)}, f32[16,4,128]{2,1,0:T(4,128)S(1)}, u32[]{:S(2)}, u32[]{:S(2)}) %collective-permute-start.15) | collective-permute-done | bytes 32800 | tf_op jit(solution)/shard_map/ppermute | solution.py:211
  49.8 1.7 %collective-permute-start.16 = (f32[8,128]{1,0:T(8,128)S(1)}, f32[8,128]{1,0:T(8,128)S(1)}, u32[]{:S(2)}, u32[]{:S(2)}) collective-permute-start(f32[8,128]{1,0:T(8,128)S(1)} %reshape.60), channel_id=1, source_target_pairs={{1,0},{2,1},{3,2},{0,3},{5,4},{6,5},{7,6},{4,7},{9,8},{10,9},{11,1... | collective-permute-start | bytes 12296 | tf_op jit(solution)/shard_map/ppermute | solution.py:209
  51.6 8.4 %shard_map.61 = f32[4,16,16,256]{3,2,1,0:T(8,128)S(1)} custom-call(f32[8,8,128]{2,1,0:T(8,128)S(1)} %fusion.9.adjoint_ref, f32[3,8,8,128]{3,2,1,0:T(8,128)S(1)} %get-tuple-element.4.grad_ref, s32[2,2,3,8,8,128]{5,4,3,2,1,0:T(8,128)S(1)} %copy-done.1, f32[2,2,3,8,8,128]{5,4,3,2,1,0:T(8,128)S(1)} %copy-done.3), custom_call_target="tpu_custom_call" | custom-call | flops 40000000 | bytes 2000000 | tf_op jit(solution)/shard_map/pallas_call | solution.py:188
  60.4 10.6 %shard_map.62 = f32[3,16,16,256]{3,2,1,0:T(8,128)S(1)} custom-call(f32[16,16,256]{2,1,0:T(8,128)S(1)} %pad_maximum_fusion.2.wrapped_ref, f32[8,8,128]{2,1,0:T(8,128)S(1)} %copy-done.4, s32[2,2,3,8,8,128]{5,4,3,2,1,0:T(8,128)S(1)} %copy-done.1, f32[2,2,3,8,8,128]{5,4,3,2,1,0:T(8,128)S(1)} %copy-done.3), custom_call_target="tpu_custom_call" | custom-call | flops 40000000 | bytes 2000000 | tf_op jit(solution)/shard_map/pallas_call | solution.py:188
  71.0 0.1 slice_add_fusion
  71.2 0.2 fusion
  71.4 0.3 reshape.64
  71.7 0.3 reshape.66
  72.0 1.8 %collective-permute-start.19 = (f32[32,128]{1,0:T(8,128)S(1)}, f32[32,128]{1,0:T(8,128)S(1)}, u32[]{:S(2)}, u32[]{:S(2)}) collective-permute-start(f32[32,128]{1,0:T(8,128)S(1)} %reshape.66), channel_id=1, source_target_pairs={{1,0},{2,1},{3,2},{0,3},{5,4},{6,5},{7,6},{4,7},{9,8},{10,9},{11,1... | collective-permute-start | bytes 49160 | tf_op jit(solution)/shard_map/ppermute | solution.py:209
  73.8 1.1 %collective-permute-done.18 = f32[32,128]{1,0:T(8,128)S(1)} collective-permute-done((f32[32,128]{1,0:T(8,128)S(1)}, f32[32,128]{1,0:T(8,128)S(1)}, u32[]{:S(2)}, u32[]{:S(2)}) %collective-permute-start.18) | collective-permute-done | bytes 16416 | tf_op jit(solution)/shard_map/ppermute | solution.py:209
  74.9 0.5 reshape.65
  75.4 0.5 reshape.67
  76.0 0.2 fusion.3
  76.2 1.2 %collective-permute-start.20 = (f32[4,16,4,128]{3,2,1,0:T(4,128)S(1)}, f32[4,16,4,128]{3,2,1,0:T(4,128)S(1)}, u32[]{:S(2)}, u32[]{:S(2)}) collective-permute-start(f32[4,16,4,128]{3,2,1,0:T(4,128)S(1)} %get-tuple-element.8), channel_id=1, source_target_pairs={{0,4},{4,8},{8,12},{12,16},{16,20},{20,24},{24,28},{28,0},{1,5},{5... | collective-permute-start | bytes 393224 | tf_op jit(solution)/shard_map/ppermute | solution.py:211
  77.4 0.9 collective-permute-start.21
  78.3 4.0 %collective-permute-done.20 = f32[4,16,4,128]{3,2,1,0:T(4,128)S(1)} collective-permute-done((f32[4,16,4,128]{3,2,1,0:T(4,128)S(1)}, f32[4,16,4,128]{3,2,1,0:T(4,128)S(1)}, u32[]{:S(2)}, u32[]{:S(2)}) %collective-permute-start.20) | collective-permute-done | bytes 131104 | tf_op jit(solution)/shard_map/ppermute | solution.py:211
  82.3 5.1 %collective-permute-done.21 = f32[4,16,4,128]{3,2,1,0:T(4,128)S(1)} collective-permute-done((f32[4,16,4,128]{3,2,1,0:T(4,128)S(1)}, f32[4,16,4,128]{3,2,1,0:T(4,128)S(1)}, u32[]{:S(2)}, u32[]{:S(2)}) %collective-permute-start.21) | collective-permute-done | bytes 131104 | tf_op jit(solution)/shard_map/ppermute | solution.py:211
  87.5 0.6 collective-permute-start.22
  88.0 1.5 %collective-permute-start.23 = (f32[4,4,8,128]{3,2,1,0:T(8,128)S(1)}, f32[4,4,8,128]{3,2,1,0:T(8,128)S(1)}, u32[]{:S(2)}, u32[]{:S(2)}) collective-permute-start(f32[4,4,8,128]{3,2,1,0:T(8,128)S(1)} %get-tuple-element.11), channel_id=1, source_target_pairs={{32,0},{64,32},{96,64},{0,96},{33,1},{65,33},{97,65},{1,97},{34,2}... | collective-permute-start | bytes 196616 | tf_op jit(solution)/shard_map/ppermute | solution.py:211
  89.6 2.2 %collective-permute-done.22 = f32[4,4,8,128]{3,2,1,0:T(8,128)S(1)} collective-permute-done((f32[4,4,8,128]{3,2,1,0:T(8,128)S(1)}, f32[4,4,8,128]{3,2,1,0:T(8,128)S(1)}, u32[]{:S(2)}, u32[]{:S(2)}) %collective-permute-start.22) | collective-permute-done | bytes 65568 | tf_op jit(solution)/shard_map/ppermute | solution.py:211
  91.8 1.7 %collective-permute-done.23 = f32[4,4,8,128]{3,2,1,0:T(8,128)S(1)} collective-permute-done((f32[4,4,8,128]{3,2,1,0:T(8,128)S(1)}, f32[4,4,8,128]{3,2,1,0:T(8,128)S(1)}, u32[]{:S(2)}, u32[]{:S(2)}) %collective-permute-start.23) | collective-permute-done | bytes 65568 | tf_op jit(solution)/shard_map/ppermute | solution.py:211
  93.5 0.6 slice_bitcast_fusion
  94.1 0.6 slice.166
  (66 shorter events, 2.9 us)
Async XLA Ops:
  0.6 1.2 %copy-start.4 = (f32[8,8,128]{2,1,0:T(8,128)S(1)}, f32[8,8,128]{2,1,0:T(8,128)}, u32[]{:S(2)}) copy-start(f32[8,8,128]{2,1,0:T(8,128)} %cot_ref.3) | copy-start | bytes 98308
  1.4 9.1 %collective-permute-start.6 = (f32[4,8,128]{2,1,0:T(8,128)S(1)}, f32[4,8,128]{2,1,0:T(8,128)S(1)}, u32[]{:S(2)}, u32[]{:S(2)}) collective-permute-start(f32[4,8,128]{2,1,0:T(8,128)S(1)} %get-tuple-element.29), channel_id=1, source_target_pairs={{0,32},{32,64},{64,96},{96,0},{1,33},{33,65},{65,97},{97,1},{2,34}... | collective-permute-start | bytes 49160 | tf_op jit(solution)/shard_map/ppermute | solution.py:211
  1.9 1.0 %copy-start = (s32[2,2,3,8,8,128]{5,4,3,2,1,0:T(8,128)S(1)}, s32[2,2,3,8,8,128]{5,4,3,2,1,0:T(8,128)}, u32[]{:S(2)}) copy-start(s32[2,2,3,8,8,128]{5,4,3,2,1,0:T(8,128)} %cells_ref.7) | copy-start | bytes 1179652
  2.9 1.0 %copy-start.2 = (f32[2,2,3,8,8,128]{5,4,3,2,1,0:T(8,128)S(1)}, f32[2,2,3,8,8,128]{5,4,3,2,1,0:T(8,128)}, u32[]{:S(2)}) copy-start(f32[2,2,3,8,8,128]{5,4,3,2,1,0:T(8,128)} %fracs_ref.7) | copy-start | bytes 1179652
  6.5 3.6 %collective-permute-start = (f32[8,128]{1,0:T(8,128)S(1)}, f32[8,128]{1,0:T(8,128)S(1)}, u32[]{:S(2)}, u32[]{:S(2)}) collective-permute-start(f32[8,128]{1,0:T(8,128)S(1)} %reshape.52), channel_id=1, source_target_pairs={{0,1},{1,2},{2,3},{3,0},{4,5},{5,6},{6,7},{7,4},{8,9},{9,10},{10,1... | collective-permute-start | bytes 12296 | tf_op jit(solution)/shard_map/ppermute | solution.py:209
  6.7 3.6 %collective-permute-start.1 = (f32[8,128]{1,0:T(8,128)S(1)}, f32[8,128]{1,0:T(8,128)S(1)}, u32[]{:S(2)}, u32[]{:S(2)}) collective-permute-start(f32[8,128]{1,0:T(8,128)S(1)} %reshape.54), channel_id=1, source_target_pairs={{1,0},{2,1},{3,2},{0,3},{5,4},{6,5},{7,6},{4,7},{9,8},{10,9},{11,1... | collective-permute-start | bytes 12296 | tf_op jit(solution)/shard_map/ppermute | solution.py:209
  8.5 4.9 %collective-permute-start.7 = (f32[4,8,128]{2,1,0:T(8,128)S(1)}, f32[4,8,128]{2,1,0:T(8,128)S(1)}, u32[]{:S(2)}, u32[]{:S(2)}) collective-permute-start(f32[4,8,128]{2,1,0:T(8,128)S(1)} %get-tuple-element.28), channel_id=1, source_target_pairs={{32,0},{64,32},{96,64},{0,96},{33,1},{65,33},{97,65},{1,97},{34,2}... | collective-permute-start | bytes 49160 | tf_op jit(solution)/shard_map/ppermute | solution.py:211
  10.4 0.8 copy-start.5
  13.5 4.0 %collective-permute-start.8 = (f32[16,4,128]{2,1,0:T(4,128)S(1)}, f32[16,4,128]{2,1,0:T(4,128)S(1)}, u32[]{:S(2)}, u32[]{:S(2)}) collective-permute-start(f32[16,4,128]{2,1,0:T(4,128)S(1)} %get-tuple-element.24), channel_id=1, source_target_pairs={{0,4},{4,8},{8,12},{12,16},{16,20},{20,24},{24,28},{28,0},{1,5},{5... | collective-permute-start | bytes 98312 | tf_op jit(solution)/shard_map/ppermute | solution.py:211
  15.4 7.5 %collective-permute-start.9 = (f32[16,4,128]{2,1,0:T(4,128)S(1)}, f32[16,4,128]{2,1,0:T(4,128)S(1)}, u32[]{:S(2)}, u32[]{:S(2)}) collective-permute-start(f32[16,4,128]{2,1,0:T(4,128)S(1)} %get-tuple-element.25), channel_id=1, source_target_pairs={{4,0},{8,4},{12,8},{16,12},{20,16},{24,20},{28,24},{0,28},{5,1},{9... | collective-permute-start | bytes 98312 | tf_op jit(solution)/shard_map/ppermute | solution.py:211
  23.3 4.1 %collective-permute-start.11 = (f32[8,128]{1,0:T(8,128)S(1)}, f32[8,128]{1,0:T(8,128)S(1)}, u32[]{:S(2)}, u32[]{:S(2)}) collective-permute-start(f32[8,128]{1,0:T(8,128)S(1)} %reshape.58), channel_id=1, source_target_pairs={{0,1},{1,2},{2,3},{3,0},{4,5},{5,6},{6,7},{7,4},{8,9},{9,10},{10,1... | collective-permute-start | bytes 12296 | tf_op jit(solution)/shard_map/ppermute | solution.py:209
  23.3 3.8 %collective-permute-start.10 = (f32[8,128]{1,0:T(8,128)S(1)}, f32[8,128]{1,0:T(8,128)S(1)}, u32[]{:S(2)}, u32[]{:S(2)}) collective-permute-start(f32[8,128]{1,0:T(8,128)S(1)} %reshape.56), channel_id=1, source_target_pairs={{1,0},{2,1},{3,2},{0,3},{5,4},{6,5},{7,6},{4,7},{9,8},{10,9},{11,1... | collective-permute-start | bytes 12296 | tf_op jit(solution)/shard_map/ppermute | solution.py:209
  25.1 7.9 %collective-permute-start.2 = (f32[1,16,4,128]{3,2,1,0:T(4,128)S(1)}, f32[1,16,4,128]{3,2,1,0:T(4,128)S(1)}, u32[]{:S(2)}, u32[]{:S(2)}) collective-permute-start(f32[1,16,4,128]{3,2,1,0:T(4,128)S(1)} %get-tuple-element.14), channel_id=1, source_target_pairs={{0,4},{4,8},{8,12},{12,16},{16,20},{20,24},{24,28},{28,0},{1,5},{5... | collective-permute-start | bytes 98312 | tf_op jit(solution)/shard_map/ppermute | solution.py:211
  25.2 7.9 %collective-permute-start.3 = (f32[1,16,4,128]{3,2,1,0:T(4,128)S(1)}, f32[1,16,4,128]{3,2,1,0:T(4,128)S(1)}, u32[]{:S(2)}, u32[]{:S(2)}) collective-permute-start(f32[1,16,4,128]{3,2,1,0:T(4,128)S(1)} %get-tuple-element.15), channel_id=1, source_target_pairs={{4,0},{8,4},{12,8},{16,12},{20,16},{24,20},{28,24},{0,28},{5,1},{9... | collective-permute-start | bytes 98312 | tf_op jit(solution)/shard_map/ppermute | solution.py:211
  27.3 1.0 %copy-start.1 = (s32[2,2,3,8,8,128]{5,4,3,2,1,0:T(8,128)S(1)}, s32[2,2,3,8,8,128]{5,4,3,2,1,0:T(8,128)}, u32[]{:S(2)}) copy-start(s32[2,2,3,8,8,128]{5,4,3,2,1,0:T(8,128)} %cells_ref.7) | copy-start | bytes 1179652
  27.3 1.1 %copy-start.3 = (f32[2,2,3,8,8,128]{5,4,3,2,1,0:T(8,128)S(1)}, f32[2,2,3,8,8,128]{5,4,3,2,1,0:T(8,128)}, u32[]{:S(2)}) copy-start(f32[2,2,3,8,8,128]{5,4,3,2,1,0:T(8,128)} %fracs_ref.7) | copy-start | bytes 1179652
  32.7 3.8 %collective-permute-start.12 = (f32[4,8,128]{2,1,0:T(8,128)S(1)}, f32[4,8,128]{2,1,0:T(8,128)S(1)}, u32[]{:S(2)}, u32[]{:S(2)}) collective-permute-start(f32[4,8,128]{2,1,0:T(8,128)S(1)} %get-tuple-element.27), channel_id=1, source_target_pairs={{0,32},{32,64},{64,96},{96,0},{1,33},{33,65},{65,97},{97,1},{2,34}... | collective-permute-start | bytes 49160 | tf_op jit(solution)/shard_map/ppermute | solution.py:211
  33.1 5.0 %collective-permute-start.13 = (f32[4,8,128]{2,1,0:T(8,128)S(1)}, f32[4,8,128]{2,1,0:T(8,128)S(1)}, u32[]{:S(2)}, u32[]{:S(2)}) collective-permute-start(f32[4,8,128]{2,1,0:T(8,128)S(1)} %get-tuple-element.26), channel_id=1, source_target_pairs={{32,0},{64,32},{96,64},{0,96},{33,1},{65,33},{97,65},{1,97},{34,2}... | collective-permute-start | bytes 49160 | tf_op jit(solution)/shard_map/ppermute | solution.py:211
  38.1 5.8 %collective-permute-start.14 = (f32[16,4,128]{2,1,0:T(4,128)S(1)}, f32[16,4,128]{2,1,0:T(4,128)S(1)}, u32[]{:S(2)}, u32[]{:S(2)}) collective-permute-start(f32[16,4,128]{2,1,0:T(4,128)S(1)} %get-tuple-element.22), channel_id=1, source_target_pairs={{0,4},{4,8},{8,12},{12,16},{16,20},{20,24},{24,28},{28,0},{1,5},{5... | collective-permute-start | bytes 98312 | tf_op jit(solution)/shard_map/ppermute | solution.py:211
  41.9 7.5 %collective-permute-start.15 = (f32[16,4,128]{2,1,0:T(4,128)S(1)}, f32[16,4,128]{2,1,0:T(4,128)S(1)}, u32[]{:S(2)}, u32[]{:S(2)}) collective-permute-start(f32[16,4,128]{2,1,0:T(4,128)S(1)} %get-tuple-element.23), channel_id=1, source_target_pairs={{4,0},{8,4},{12,8},{16,12},{20,16},{24,20},{28,24},{0,28},{5,1},{9... | collective-permute-start | bytes 98312 | tf_op jit(solution)/shard_map/ppermute | solution.py:211
  41.9 9.7 %collective-permute-start.4 = (f32[1,4,8,128]{3,2,1,0:T(8,128)S(1)}, f32[1,4,8,128]{3,2,1,0:T(8,128)S(1)}, u32[]{:S(2)}, u32[]{:S(2)}) collective-permute-start(f32[1,4,8,128]{3,2,1,0:T(8,128)S(1)} %get-tuple-element.20), channel_id=1, source_target_pairs={{0,32},{32,64},{64,96},{96,0},{1,33},{33,65},{65,97},{97,1},{2,34}... | collective-permute-start | bytes 49160 | tf_op jit(solution)/shard_map/ppermute | solution.py:211
  42.1 9.4 %collective-permute-start.5 = (f32[1,4,8,128]{3,2,1,0:T(8,128)S(1)}, f32[1,4,8,128]{3,2,1,0:T(8,128)S(1)}, u32[]{:S(2)}, u32[]{:S(2)}) collective-permute-start(f32[1,4,8,128]{3,2,1,0:T(8,128)S(1)} %get-tuple-element.21), channel_id=1, source_target_pairs={{32,0},{64,32},{96,64},{0,96},{33,1},{65,33},{97,65},{1,97},{34,2}... | collective-permute-start | bytes 49160 | tf_op jit(solution)/shard_map/ppermute | solution.py:211
  49.8 10.4 %collective-permute-start.17 = (f32[8,128]{1,0:T(8,128)S(1)}, f32[8,128]{1,0:T(8,128)S(1)}, u32[]{:S(2)}, u32[]{:S(2)}) collective-permute-start(f32[8,128]{1,0:T(8,128)S(1)} %reshape.62), channel_id=1, source_target_pairs={{0,1},{1,2},{2,3},{3,0},{4,5},{5,6},{6,7},{7,4},{8,9},{9,10},{10,1... | collective-permute-start | bytes 12296 | tf_op jit(solution)/shard_map/ppermute | solution.py:209
  49.8 10.2 %collective-permute-start.16 = (f32[8,128]{1,0:T(8,128)S(1)}, f32[8,128]{1,0:T(8,128)S(1)}, u32[]{:S(2)}, u32[]{:S(2)}) collective-permute-start(f32[8,128]{1,0:T(8,128)S(1)} %reshape.60), channel_id=1, source_target_pairs={{1,0},{2,1},{3,2},{0,3},{5,4},{6,5},{7,6},{4,7},{9,8},{10,9},{11,1... | collective-permute-start | bytes 12296 | tf_op jit(solution)/shard_map/ppermute | solution.py:209
  71.6 3.2 %collective-permute-start.18 = (f32[32,128]{1,0:T(8,128)S(1)}, f32[32,128]{1,0:T(8,128)S(1)}, u32[]{:S(2)}, u32[]{:S(2)}) collective-permute-start(f32[32,128]{1,0:T(8,128)S(1)} %reshape.64), channel_id=1, source_target_pairs={{0,1},{1,2},{2,3},{3,0},{4,5},{5,6},{6,7},{7,4},{8,9},{9,10},{10,1... | collective-permute-start | bytes 49160 | tf_op jit(solution)/shard_map/ppermute | solution.py:209
  72.0 3.4 %collective-permute-start.19 = (f32[32,128]{1,0:T(8,128)S(1)}, f32[32,128]{1,0:T(8,128)S(1)}, u32[]{:S(2)}, u32[]{:S(2)}) collective-permute-start(f32[32,128]{1,0:T(8,128)S(1)} %reshape.66), channel_id=1, source_target_pairs={{1,0},{2,1},{3,2},{0,3},{5,4},{6,5},{7,6},{4,7},{9,8},{10,9},{11,1... | collective-permute-start | bytes 49160 | tf_op jit(solution)/shard_map/ppermute | solution.py:209
  76.2 6.1 %collective-permute-start.20 = (f32[4,16,4,128]{3,2,1,0:T(4,128)S(1)}, f32[4,16,4,128]{3,2,1,0:T(4,128)S(1)}, u32[]{:S(2)}, u32[]{:S(2)}) collective-permute-start(f32[4,16,4,128]{3,2,1,0:T(4,128)S(1)} %get-tuple-element.8), channel_id=1, source_target_pairs={{0,4},{4,8},{8,12},{12,16},{16,20},{20,24},{24,28},{28,0},{1,5},{5... | collective-permute-start | bytes 393224 | tf_op jit(solution)/shard_map/ppermute | solution.py:211
  77.4 9.9 %collective-permute-start.21 = (f32[4,16,4,128]{3,2,1,0:T(4,128)S(1)}, f32[4,16,4,128]{3,2,1,0:T(4,128)S(1)}, u32[]{:S(2)}, u32[]{:S(2)}) collective-permute-start(f32[4,16,4,128]{3,2,1,0:T(4,128)S(1)} %get-tuple-element.9), channel_id=1, source_target_pairs={{4,0},{8,4},{12,8},{16,12},{20,16},{24,20},{28,24},{0,28},{5,1},{9... | collective-permute-start | bytes 393224 | tf_op jit(solution)/shard_map/ppermute | solution.py:211
  87.5 4.3 %collective-permute-start.22 = (f32[4,4,8,128]{3,2,1,0:T(8,128)S(1)}, f32[4,4,8,128]{3,2,1,0:T(8,128)S(1)}, u32[]{:S(2)}, u32[]{:S(2)}) collective-permute-start(f32[4,4,8,128]{3,2,1,0:T(8,128)S(1)} %get-tuple-element.10), channel_id=1, source_target_pairs={{0,32},{32,64},{64,96},{96,0},{1,33},{33,65},{65,97},{97,1},{2,34}... | collective-permute-start | bytes 196616 | tf_op jit(solution)/shard_map/ppermute | solution.py:211
  88.0 5.5 %collective-permute-start.23 = (f32[4,4,8,128]{3,2,1,0:T(8,128)S(1)}, f32[4,4,8,128]{3,2,1,0:T(8,128)S(1)}, u32[]{:S(2)}, u32[]{:S(2)}) collective-permute-start(f32[4,4,8,128]{3,2,1,0:T(8,128)S(1)} %get-tuple-element.11), channel_id=1, source_target_pairs={{32,0},{64,32},{96,64},{0,96},{33,1},{65,33},{97,65},{1,97},{34,2}... | collective-permute-start | bytes 196616 | tf_op jit(solution)/shard_map/ppermute | solution.py:211

commit v5 on v4

--- a/solution.py
+++ b/solution.py
@@ -255,6 +255,50 @@
     return block
 
 
+def joint_exchange(block, deposit, pz):
+    nz = block.shape[2]
+
+    def trade(axis, up_pieces, down_pieces):
+        results = []
+        for pieces, upward in ((up_pieces, True), (down_pieces, False)):
+            flat = jnp.concatenate([piece.reshape(-1, 128) for piece in pieces])
+            got = lax.ppermute(flat, axis, [
+                ((i, (i + 1) % lax.axis_size(axis)) if upward
+                 else ((i + 1) % lax.axis_size(axis), i))
+                for i in range(lax.axis_size(axis))
+            ])
+            parts, start = [], 0
+            for piece in pieces:
+                rows = piece.size // 128
+                parts.append(got[start : start + rows].reshape(piece.shape))
+                start += rows
+            results.append(parts)
+        return results
+
+    for axis, dim in AXES[:2]:
+        size = block.shape[dim]
+        head = lax.slice_in_dim(block, 0, MARGIN, axis=dim)
+        tail = lax.slice_in_dim(block, size - MARGIN, size, axis=dim)
+        low = lax.slice_in_dim(deposit, 0, MARGIN, axis=dim)
+        high = lax.slice_in_dim(deposit, size + MARGIN, size + 2 * MARGIN, axis=dim)
+        (below, got_low), (above, got_high) = trade(axis, [tail, high], [head, low])
+        block = jnp.concatenate([below, block, above], axis=dim)
+        deposit = lax.slice_in_dim(deposit, MARGIN, size + MARGIN, axis=dim)
+        deposit = deposit + place_rim(got_low, dim, 0, size)
+        deposit = deposit + place_rim(got_high, dim, size - MARGIN, size)
+    head = block[:, :, :MARGIN]
+    tail = block[:, :, nz - MARGIN :]
+    upper = deposit[..., nz : nz + MARGIN]
+    lower = deposit[..., pz - MARGIN :]
+    (below, from_below), (above, from_above) = trade("gz", [tail, upper], [head, lower])
+    gap = jnp.zeros(block.shape[:2] + (pz - nz - 2 * MARGIN,), jnp.float32)
+    wrapped = jnp.concatenate([block, above, gap, below], axis=2)
+    folded = deposit[..., :nz]
+    folded = folded + place_rim(from_below, 2, 0, nz)
+    folded = folded + place_rim(from_above, 2, nz - MARGIN, nz)
+    return wrapped, folded
+
+
 def body(intensity, cotangent, departure_cells, departure_fracs):
     cells = departure_cells
     fracs = departure_fracs
@@ -268,20 +312,19 @@
     staged = pltpu.VMEM((SHIFTS, px, ny + 16, nz), f32)
     summed = pltpu.VMEM((SHIFTS, px, py, nz), f32)
 
-    wrapped = widen(intensity, pz)
+    adjoint_padded = vmem_call(
+        late_spread_kernel,
+        jax.ShapeDtypeStruct((px, py, pz), f32),
+        [products, staged, summed] + table_scratch(block, 3),
+        cotangent, cells, fracs,
+    )
+    wrapped, adjoint_mid = joint_exchange(intensity, adjoint_padded, pz)
     image_mid, grad_raw = vmem_call(
         early_sample_kernel,
         (jax.ShapeDtypeStruct(block, f32), jax.ShapeDtypeStruct((3,) + block, f32)),
         [rolled, windows] + table_scratch(block, 6),
         wrapped, cells, fracs,
     )
-    adjoint_padded = vmem_call(
-        late_spread_kernel,
-        jax.ShapeDtypeStruct((px, py, pz), f32),
-        [products, staged, summed] + table_scratch(block, 3),
-        cotangent, cells, fracs,
-    )
-    adjoint_mid = fold(adjoint_padded[None], nz)[0]
     early_padded = vmem_call(
         early_spread_kernel,
         jax.ShapeDtypeStruct((4, px, py, pz), f32),

time: 95.1 us -> 96.7 us (1.017)
  starting transfers between devices: 25.7 us -> 26.9 us
    ppermute x0 -> x6, starting transfers between devices: none -> 9.65 us  [trade(): lax.ppermute(flat, axis, [(i, (i + 1) % lax.axis_size(axis)) if upward el...]
    ppermute x16 -> x8, waiting for transfers between devices: 31.2 us -> 23.5 us  [shift_from(): return lax.ppermute(piece, axis, pairs)]
    ppermute x0 -> x6, waiting for transfers between devices: none -> 7.05 us  [trade(): lax.ppermute(flat, axis, [(i, (i + 1) % lax.axis_size(axis)) if upward el...]
    ppermute x16 -> x8, starting transfers between devices: 18.4 us -> 13.6 us  [shift_from(): return lax.ppermute(piece, axis, pairs)]
    ppermute x8 -> x4, starting transfers between devices: 7.36 us -> 3.68 us  [shift_from(): flat = lax.ppermute(piece.reshape(-1, 128), axis, pairs)]
    reshape x0 -> x19, local copies, waits for them, and re-layouts: none -> 1.79 us  [the longest x9 1.24 us: trade(): flat = jnp.concatenate([piece.reshape(-1, 128) for piece in pieces])]
    unnamed x16 -> x14, local copies, waits for them, and re-layouts: 3.59 us -> 3.6 us
  transfers between devices with their start and end apart: 24 -> 18, of which waited for: 11 -> 13; matrix products, arithmetic and copies ran while one was open for 3% -> 2% of each run, Pallas kernels for 16% -> 9%
where the time goes in v5:
time: 96.7 us; the launch traced here: 95.6 us
  waiting for transfers between devices  31.6 us (33%)
  starting transfers between devices  26.9 us (28%)
  Pallas kernels  25.6 us (26%)
  local copies, waits for them, and re-layouts  9.25 us (10%)
  between operations  1.09 us (1%)
  other arithmetic  1.08 us (1%)
    pallas_call x4, Pallas kernels, vmem_call(): pl.pallas_call(kernel, out_shape=out_shapes, in_specs=[pl.BlockSpec(memor...  25.6 us
    ppermute x8, waiting for transfers between devices, shift_from(): return lax.ppermute(piece, axis, pairs)  23.5 us
    ppermute x8, starting transfers between devices, shift_from(): return lax.ppermute(piece, axis, pairs)  13.6 us
    ppermute x6, starting transfers between devices, trade(): lax.ppermute(flat, axis, [(i, (i + 1) % lax.axis_size(axis)) if upward el...  9.65 us
    ppermute x6, waiting for transfers between devices, trade(): lax.ppermute(flat, axis, [(i, (i + 1) % lax.axis_size(axis)) if upward el...  7.05 us
    ppermute x4, starting transfers between devices, shift_from(): flat = lax.ppermute(piece.reshape(-1, 128), axis, pairs)  3.68 us
    unnamed x14, local copies, waits for them, and re-layouts  3.6 us
  transfers between devices with their start and end apart: 18, of which 13 were waited for; matrix products, arithmetic and copies ran while one was open for 2% of the time, Pallas kernels for 9%

profile of v5, /device:TPU:102, one launch (start us, length us, event | category | flops | bytes accessed | tf_op | source)
XLA Modules:
  0.0 95.6 jit_solution(2261145184412782516)
XLA Ops:
  0.6 0.7 slice_bitcast_fusion.4
  1.4 1.0 %copy-done = s32[2,2,3,8,8,128]{5,4,3,2,1,0:T(8,128)S(1)} copy-done((s32[2,2,3,8,8,128]{5,4,3,2,1,0:T(8,128)S(1)}, s32[2,2,3,8,8,128]{5,4,3,2,1,0:T(8,128)}, u32[]{:S(2)}) %copy-start) | copy-done | bytes 393240
  2.4 1.0 %copy-done.2 = f32[2,2,3,8,8,128]{5,4,3,2,1,0:T(8,128)S(1)} copy-done((f32[2,2,3,8,8,128]{5,4,3,2,1,0:T(8,128)S(1)}, f32[2,2,3,8,8,128]{5,4,3,2,1,0:T(8,128)}, u32[]{:S(2)}) %copy-start.2) | copy-done | bytes 393240
  3.4 2.4 %shard_map.59 = f32[16,16,256]{2,1,0:T(8,128)S(1)} custom-call(f32[8,8,128]{2,1,0:T(8,128)S(1)} %copy-done.4, s32[2,2,3,8,8,128]{5,4,3,2,1,0:T(8,128)S(1)} %copy-done, f32[2,2,3,8,8,128]{5,4,3,2,1,0:T(8,128)S(1)} %copy-done.2), custom_call_target="tpu_custom_call" | custom-call | flops 40000000 | bytes 2000000 | tf_op jit(solution)/shard_map/pallas_call | solution.py:188
  5.9 0.9 collective-permute-start.1
  6.8 2.5 %collective-permute-start = (f32[160,128]{1,0:T(8,128)S(1)}, f32[160,128]{1,0:T(8,128)S(1)}, u32[]{:S(2)}, u32[]{:S(2)}) collective-permute-start(f32[160,128]{1,0:T(8,128)S(1)} %pad_maximum_fusion.5), channel_id=1, source_target_pairs={{0,32},{32,64},{64,96},{96,0},{1,33},{33,65},{65,97},{97,1},{2,34}... | collective-permute-start | bytes 245768 | tf_op jit(solution)/shard_map/ppermute | solution.py:265
  9.2 2.3 %collective-permute-done.1 = f32[160,128]{1,0:T(8,128)S(1)} collective-permute-done((f32[160,128]{1,0:T(8,128)S(1)}, f32[160,128]{1,0:T(8,128)S(1)}, u32[]{:S(2)}, u32[]{:S(2)}) %collective-permute-start.1) | collective-permute-done | bytes 81952 | tf_op jit(solution)/shard_map/ppermute | solution.py:265
  11.7 0.7 copy-done.5
  12.5 0.5 collective-permute-start.3
  13.0 5.2 %collective-permute-start.2 = (f32[128,128]{1,0:T(8,128)S(1)}, f32[128,128]{1,0:T(8,128)S(1)}, u32[]{:S(2)}, u32[]{:S(2)}) collective-permute-start(f32[128,128]{1,0:T(8,128)S(1)} %pad_maximum_fusion.8), channel_id=1, source_target_pairs={{0,4},{4,8},{8,12},{12,16},{16,20},{20,24},{24,28},{28,0},{1,5},{5... | collective-permute-start | bytes 196616 | tf_op jit(solution)/shard_map/ppermute | solution.py:265
  18.3 2.2 %collective-permute-done.3 = f32[128,128]{1,0:T(8,128)S(1)} collective-permute-done((f32[128,128]{1,0:T(8,128)S(1)}, f32[128,128]{1,0:T(8,128)S(1)}, u32[]{:S(2)}, u32[]{:S(2)}) %collective-permute-start.3) | collective-permute-done | bytes 65568 | tf_op jit(solution)/shard_map/ppermute | solution.py:265
  21.0 0.1 reshape.119
  21.4 0.5 collective-permute-start.4
  22.0 0.8 collective-permute-done.5
  22.7 0.1 reshape.122
  22.9 1.7 %collective-permute-done.4 = f32[10,128]{1,0:T(8,128)S(1)} collective-permute-done((f32[10,128]{1,0:T(8,128)S(1)}, f32[10,128]{1,0:T(8,128)S(1)}, u32[]{:S(2)}, u32[]{:S(2)}) %collective-permute-start.4) | collective-permute-done | bytes 5152 | tf_op jit(solution)/shard_map/ppermute | solution.py:265
  24.6 0.1 reshape.123
  24.8 0.7 copy-done.1
  25.7 4.2 %shard_map.60 = (f32[8,8,128]{2,1,0:T(8,128)S(1)}, f32[3,8,8,128]{3,2,1,0:T(8,128)S(1)}) custom-call(f32[16,16,256]{2,1,0:T(8,128)S(1)} %pad_maximum_fusion.1.wrapped_ref, s32[2,2,3,8,8,128]{5,4,3,2,1,0:T(8,128)S(1)} %copy-done.1, f32[2,2,3,8,8,128]{5,4,3,2,1,0:T(8,128)S(1)} %copy-done.3), custom_call_target="tpu_custom_call" | custom-call | flops 40000000 | bytes 2000000 | tf_op jit(solution)/shard_map/pallas_call | solution.py:188
  29.9 3.3 %collective-permute-start.6 = (f32[4,8,128]{2,1,0:T(8,128)S(1)}, f32[4,8,128]{2,1,0:T(8,128)S(1)}, u32[]{:S(2)}, u32[]{:S(2)}) collective-permute-start(f32[4,8,128]{2,1,0:T(8,128)S(1)} %get-tuple-element.31), channel_id=1, source_target_pairs={{0,32},{32,64},{64,96},{96,0},{1,33},{33,65},{65,97},{97,1},{2,34}... | collective-permute-start | bytes 49160 | tf_op jit(solution)/shard_map/ppermute | solution.py:211
  33.3 1.4 %collective-permute-done.6 = f32[4,8,128]{2,1,0:T(8,128)S(1)} collective-permute-done((f32[4,8,128]{2,1,0:T(8,128)S(1)}, f32[4,8,128]{2,1,0:T(8,128)S(1)}, u32[]{:S(2)}, u32[]{:S(2)}) %collective-permute-start.6) | collective-permute-done | bytes 16416 | tf_op jit(solution)/shard_map/ppermute | solution.py:211
  34.7 3.5 %collective-permute-done.7 = f32[4,8,128]{2,1,0:T(8,128)S(1)} collective-permute-done((f32[4,8,128]{2,1,0:T(8,128)S(1)}, f32[4,8,128]{2,1,0:T(8,128)S(1)}, u32[]{:S(2)}, u32[]{:S(2)}) %collective-permute-start.7) | collective-permute-done | bytes 16416 | tf_op jit(solution)/shard_map/ppermute | solution.py:211
  38.2 6.1 %collective-permute-start.8 = (f32[16,4,128]{2,1,0:T(4,128)S(1)}, f32[16,4,128]{2,1,0:T(4,128)S(1)}, u32[]{:S(2)}, u32[]{:S(2)}) collective-permute-start(f32[16,4,128]{2,1,0:T(4,128)S(1)} %get-tuple-element.20), channel_id=1, source_target_pairs={{0,4},{4,8},{8,12},{12,16},{16,20},{20,24},{24,28},{28,0},{1,5},{5... | collective-permute-start | bytes 98312 | tf_op jit(solution)/shard_map/ppermute | solution.py:211
  44.5 1.4 %collective-permute-done.8 = f32[16,4,128]{2,1,0:T(4,128)S(1)} collective-permute-done((f32[16,4,128]{2,1,0:T(4,128)S(1)}, f32[16,4,128]{2,1,0:T(4,128)S(1)}, u32[]{:S(2)}, u32[]{:S(2)}) %collective-permute-start.8) | collective-permute-done | bytes 32800 | tf_op jit(solution)/shard_map/ppermute | solution.py:211
  45.9 5.9 %collective-permute-done.9 = f32[16,4,128]{2,1,0:T(4,128)S(1)} collective-permute-done((f32[16,4,128]{2,1,0:T(4,128)S(1)}, f32[16,4,128]{2,1,0:T(4,128)S(1)}, u32[]{:S(2)}, u32[]{:S(2)}) %collective-permute-start.9) | collective-permute-done | bytes 32800 | tf_op jit(solution)/shard_map/ppermute | solution.py:211
  52.0 0.1 reshape.124
  52.3 1.7 %collective-permute-start.10 = (f32[8,128]{1,0:T(8,128)S(1)}, f32[8,128]{1,0:T(8,128)S(1)}, u32[]{:S(2)}, u32[]{:S(2)}) collective-permute-start(f32[8,128]{1,0:T(8,128)S(1)} %reshape.124), channel_id=1, source_target_pairs={{1,0},{2,1},{3,2},{0,3},{5,4},{6,5},{7,6},{4,7},{9,8},{10,9},{11,1... | collective-permute-start | bytes 12296 | tf_op jit(solution)/shard_map/ppermute | solution.py:209
  54.1 8.4 %shard_map.61 = f32[4,16,16,256]{3,2,1,0:T(8,128)S(1)} custom-call(f32[8,8,128]{2,1,0:T(8,128)S(1)} %fusion.8.adjoint_ref, f32[3,8,8,128]{3,2,1,0:T(8,128)S(1)} %get-tuple-element.4.grad_ref, s32[2,2,3,8,8,128]{5,4,3,2,1,0:T(8,128)S(1)} %copy-done.1, f32[2,2,3,8,8,128]{5,4,3,2,1,0:T(8,128)S(1)} %copy-done.3), custom_call_target="tpu_custom_call" | custom-call | flops 40000000 | bytes 2000000 | tf_op jit(solution)/shard_map/pallas_call | solution.py:188
  62.5 0.1 reshape.125
  62.7 0.1 reshape.127
  62.9 10.6 %shard_map.62 = f32[3,16,16,256]{3,2,1,0:T(8,128)S(1)} custom-call(f32[16,16,256]{2,1,0:T(8,128)S(1)} %pad_maximum_fusion.2.wrapped_ref, f32[8,8,128]{2,1,0:T(8,128)S(1)} %copy-done.4, s32[2,2,3,8,8,128]{5,4,3,2,1,0:T(8,128)S(1)} %copy-done.1, f32[2,2,3,8,8,128]{5,4,3,2,1,0:T(8,128)S(1)} %copy-done.3), custom_call_target="tpu_custom_call" | custom-call | flops 40000000 | bytes 2000000 | tf_op jit(solution)/shard_map/pallas_call | solution.py:188
  73.5 0.1 slice_add_fusion
  73.7 0.2 fusion
  73.9 0.3 reshape.128
  74.2 0.3 reshape.130
  74.5 1.8 %collective-permute-start.13 = (f32[32,128]{1,0:T(8,128)S(1)}, f32[32,128]{1,0:T(8,128)S(1)}, u32[]{:S(2)}, u32[]{:S(2)}) collective-permute-start(f32[32,128]{1,0:T(8,128)S(1)} %reshape.130), channel_id=1, source_target_pairs={{1,0},{2,1},{3,2},{0,3},{5,4},{6,5},{7,6},{4,7},{9,8},{10,9},{11,1... | collective-permute-start | bytes 49160 | tf_op jit(solution)/shard_map/ppermute | solution.py:209
  76.3 1.1 %collective-permute-done.12 = f32[32,128]{1,0:T(8,128)S(1)} collective-permute-done((f32[32,128]{1,0:T(8,128)S(1)}, f32[32,128]{1,0:T(8,128)S(1)}, u32[]{:S(2)}, u32[]{:S(2)}) %collective-permute-start.12) | collective-permute-done | bytes 16416 | tf_op jit(solution)/shard_map/ppermute | solution.py:209
  77.4 0.5 reshape.129
  77.9 0.5 reshape.131
  78.5 0.2 fusion.3
  78.8 2.0 %collective-permute-start.15 = (f32[4,16,4,128]{3,2,1,0:T(4,128)S(1)}, f32[4,16,4,128]{3,2,1,0:T(4,128)S(1)}, u32[]{:S(2)}, u32[]{:S(2)}) collective-permute-start(f32[4,16,4,128]{3,2,1,0:T(4,128)S(1)} %get-tuple-element.9), channel_id=1, source_target_pairs={{4,0},{8,4},{12,8},{16,12},{20,16},{24,20},{28,24},{0,28},{5,1},{9... | collective-permute-start | bytes 393224 | tf_op jit(solution)/shard_map/ppermute | solution.py:211
  80.8 4.3 %collective-permute-done.14 = f32[4,16,4,128]{3,2,1,0:T(4,128)S(1)} collective-permute-done((f32[4,16,4,128]{3,2,1,0:T(4,128)S(1)}, f32[4,16,4,128]{3,2,1,0:T(4,128)S(1)}, u32[]{:S(2)}, u32[]{:S(2)}) %collective-permute-start.14) | collective-permute-done | bytes 131104 | tf_op jit(solution)/shard_map/ppermute | solution.py:211
  85.1 3.4 %collective-permute-done.15 = f32[4,16,4,128]{3,2,1,0:T(4,128)S(1)} collective-permute-done((f32[4,16,4,128]{3,2,1,0:T(4,128)S(1)}, f32[4,16,4,128]{3,2,1,0:T(4,128)S(1)}, u32[]{:S(2)}, u32[]{:S(2)}) %collective-permute-start.15) | collective-permute-done | bytes 131104 | tf_op jit(solution)/shard_map/ppermute | solution.py:211
  88.8 2.0 %collective-permute-start.17 = (f32[4,4,8,128]{3,2,1,0:T(8,128)S(1)}, f32[4,4,8,128]{3,2,1,0:T(8,128)S(1)}, u32[]{:S(2)}, u32[]{:S(2)}) collective-permute-start(f32[4,4,8,128]{3,2,1,0:T(8,128)S(1)} %get-tuple-element.11), channel_id=1, source_target_pairs={{32,0},{64,32},{96,64},{0,96},{33,1},{65,33},{97,65},{1,97},{34,2}... | collective-permute-start | bytes 196616 | tf_op jit(solution)/shard_map/ppermute | solution.py:211
  90.8 2.2 %collective-permute-done.16 = f32[4,4,8,128]{3,2,1,0:T(8,128)S(1)} collective-permute-done((f32[4,4,8,128]{3,2,1,0:T(8,128)S(1)}, f32[4,4,8,128]{3,2,1,0:T(8,128)S(1)}, u32[]{:S(2)}, u32[]{:S(2)}) %collective-permute-start.16) | collective-permute-done | bytes 65568 | tf_op jit(solution)/shard_map/ppermute | solution.py:211
  93.0 1.3 %collective-permute-done.17 = f32[4,4,8,128]{3,2,1,0:T(8,128)S(1)} collective-permute-done((f32[4,4,8,128]{3,2,1,0:T(8,128)S(1)}, f32[4,4,8,128]{3,2,1,0:T(8,128)S(1)}, u32[]{:S(2)}, u32[]{:S(2)}) %collective-permute-start.17) | collective-permute-done | bytes 65568 | tf_op jit(solution)/shard_map/ppermute | solution.py:211
  94.3 0.6 slice_bitcast_fusion
  94.9 0.6 slice.226
  (76 shorter events, 2.4 us)
Async XLA Ops:
  0.6 0.8 copy-start.4
  1.4 1.0 %copy-start = (s32[2,2,3,8,8,128]{5,4,3,2,1,0:T(8,128)S(1)}, s32[2,2,3,8,8,128]{5,4,3,2,1,0:T(8,128)}, u32[]{:S(2)}) copy-start(s32[2,2,3,8,8,128]{5,4,3,2,1,0:T(8,128)} %cells_ref.7) | copy-start | bytes 1179652
  2.4 1.0 %copy-start.2 = (f32[2,2,3,8,8,128]{5,4,3,2,1,0:T(8,128)S(1)}, f32[2,2,3,8,8,128]{5,4,3,2,1,0:T(8,128)}, u32[]{:S(2)}) copy-start(f32[2,2,3,8,8,128]{5,4,3,2,1,0:T(8,128)} %fracs_ref.7) | copy-start | bytes 1179652
  5.9 5.7 %collective-permute-start.1 = (f32[160,128]{1,0:T(8,128)S(1)}, f32[160,128]{1,0:T(8,128)S(1)}, u32[]{:S(2)}, u32[]{:S(2)}) collective-permute-start(f32[160,128]{1,0:T(8,128)S(1)} %pad_maximum_fusion.6), channel_id=1, source_target_pairs={{32,0},{64,32},{96,64},{0,96},{33,1},{65,33},{97,65},{1,97},{34,2}... | collective-permute-start | bytes 245768 | tf_op jit(solution)/shard_map/ppermute | solution.py:265
  6.8 4.8 %collective-permute-start = (f32[160,128]{1,0:T(8,128)S(1)}, f32[160,128]{1,0:T(8,128)S(1)}, u32[]{:S(2)}, u32[]{:S(2)}) collective-permute-start(f32[160,128]{1,0:T(8,128)S(1)} %pad_maximum_fusion.5), channel_id=1, source_target_pairs={{0,32},{32,64},{64,96},{96,0},{1,33},{33,65},{65,97},{97,1},{2,34}... | collective-permute-start | bytes 245768 | tf_op jit(solution)/shard_map/ppermute | solution.py:265
  11.7 0.8 copy-start.5
  12.5 7.9 %collective-permute-start.3 = (f32[128,128]{1,0:T(8,128)S(1)}, f32[128,128]{1,0:T(8,128)S(1)}, u32[]{:S(2)}, u32[]{:S(2)}) collective-permute-start(f32[128,128]{1,0:T(8,128)S(1)} %pad_maximum_fusion.9), channel_id=1, source_target_pairs={{4,0},{8,4},{12,8},{16,12},{20,16},{24,20},{28,24},{0,28},{5,1},{9... | collective-permute-start | bytes 196616 | tf_op jit(solution)/shard_map/ppermute | solution.py:265
  13.0 7.5 %collective-permute-start.2 = (f32[128,128]{1,0:T(8,128)S(1)}, f32[128,128]{1,0:T(8,128)S(1)}, u32[]{:S(2)}, u32[]{:S(2)}) collective-permute-start(f32[128,128]{1,0:T(8,128)S(1)} %pad_maximum_fusion.8), channel_id=1, source_target_pairs={{0,4},{4,8},{8,12},{12,16},{16,20},{20,24},{24,28},{28,0},{1,5},{5... | collective-permute-start | bytes 196616 | tf_op jit(solution)/shard_map/ppermute | solution.py:265
  21.3 1.4 %collective-permute-start.5 = (f32[10,128]{1,0:T(8,128)S(1)}, f32[10,128]{1,0:T(8,128)S(1)}, u32[]{:S(2)}, u32[]{:S(2)}) collective-permute-start(f32[10,128]{1,0:T(8,128)S(1)} %pad_maximum_fusion.11), channel_id=1, source_target_pairs={{1,0},{2,1},{3,2},{0,3},{5,4},{6,5},{7,6},{4,7},{9,8},{10,9},{11,1... | collective-permute-start | bytes 15368 | tf_op jit(solution)/shard_map/ppermute | solution.py:265
  21.4 3.2 %collective-permute-start.4 = (f32[10,128]{1,0:T(8,128)S(1)}, f32[10,128]{1,0:T(8,128)S(1)}, u32[]{:S(2)}, u32[]{:S(2)}) collective-permute-start(f32[10,128]{1,0:T(8,128)S(1)} %pad_maximum_fusion.10), channel_id=1, source_target_pairs={{0,1},{1,2},{2,3},{3,0},{4,5},{5,6},{6,7},{7,4},{8,9},{9,10},{10,1... | collective-permute-start | bytes 15368 | tf_op jit(solution)/shard_map/ppermute | solution.py:265
  24.6 1.0 %copy-start.1 = (s32[2,2,3,8,8,128]{5,4,3,2,1,0:T(8,128)S(1)}, s32[2,2,3,8,8,128]{5,4,3,2,1,0:T(8,128)}, u32[]{:S(2)}) copy-start(s32[2,2,3,8,8,128]{5,4,3,2,1,0:T(8,128)} %cells_ref.7) | copy-start | bytes 1179652
  24.6 1.1 %copy-start.3 = (f32[2,2,3,8,8,128]{5,4,3,2,1,0:T(8,128)S(1)}, f32[2,2,3,8,8,128]{5,4,3,2,1,0:T(8,128)}, u32[]{:S(2)}) copy-start(f32[2,2,3,8,8,128]{5,4,3,2,1,0:T(8,128)} %fracs_ref.7) | copy-start | bytes 1179652
  29.9 4.8 %collective-permute-start.6 = (f32[4,8,128]{2,1,0:T(8,128)S(1)}, f32[4,8,128]{2,1,0:T(8,128)S(1)}, u32[]{:S(2)}, u32[]{:S(2)}) collective-permute-start(f32[4,8,128]{2,1,0:T(8,128)S(1)} %get-tuple-element.31), channel_id=1, source_target_pairs={{0,32},{32,64},{64,96},{96,0},{1,33},{33,65},{65,97},{97,1},{2,34}... | collective-permute-start | bytes 49160 | tf_op jit(solution)/shard_map/ppermute | solution.py:211
  33.3 4.9 %collective-permute-start.7 = (f32[4,8,128]{2,1,0:T(8,128)S(1)}, f32[4,8,128]{2,1,0:T(8,128)S(1)}, u32[]{:S(2)}, u32[]{:S(2)}) collective-permute-start(f32[4,8,128]{2,1,0:T(8,128)S(1)} %get-tuple-element.30), channel_id=1, source_target_pairs={{32,0},{64,32},{96,64},{0,96},{33,1},{65,33},{97,65},{1,97},{34,2}... | collective-permute-start | bytes 49160 | tf_op jit(solution)/shard_map/ppermute | solution.py:211
  38.2 7.7 %collective-permute-start.8 = (f32[16,4,128]{2,1,0:T(4,128)S(1)}, f32[16,4,128]{2,1,0:T(4,128)S(1)}, u32[]{:S(2)}, u32[]{:S(2)}) collective-permute-start(f32[16,4,128]{2,1,0:T(4,128)S(1)} %get-tuple-element.20), channel_id=1, source_target_pairs={{0,4},{4,8},{8,12},{12,16},{16,20},{20,24},{24,28},{28,0},{1,5},{5... | collective-permute-start | bytes 98312 | tf_op jit(solution)/shard_map/ppermute | solution.py:211
  44.3 7.5 %collective-permute-start.9 = (f32[16,4,128]{2,1,0:T(4,128)S(1)}, f32[16,4,128]{2,1,0:T(4,128)S(1)}, u32[]{:S(2)}, u32[]{:S(2)}) collective-permute-start(f32[16,4,128]{2,1,0:T(4,128)S(1)} %get-tuple-element.21), channel_id=1, source_target_pairs={{4,0},{8,4},{12,8},{16,12},{20,16},{24,20},{28,24},{0,28},{5,1},{9... | collective-permute-start | bytes 98312 | tf_op jit(solution)/shard_map/ppermute | solution.py:211
  52.2 10.4 %collective-permute-start.11 = (f32[8,128]{1,0:T(8,128)S(1)}, f32[8,128]{1,0:T(8,128)S(1)}, u32[]{:S(2)}, u32[]{:S(2)}) collective-permute-start(f32[8,128]{1,0:T(8,128)S(1)} %reshape.126), channel_id=1, source_target_pairs={{0,1},{1,2},{2,3},{3,0},{4,5},{5,6},{6,7},{7,4},{8,9},{9,10},{10,1... | collective-permute-start | bytes 12296 | tf_op jit(solution)/shard_map/ppermute | solution.py:209
  52.3 10.2 %collective-permute-start.10 = (f32[8,128]{1,0:T(8,128)S(1)}, f32[8,128]{1,0:T(8,128)S(1)}, u32[]{:S(2)}, u32[]{:S(2)}) collective-permute-start(f32[8,128]{1,0:T(8,128)S(1)} %reshape.124), channel_id=1, source_target_pairs={{1,0},{2,1},{3,2},{0,3},{5,4},{6,5},{7,6},{4,7},{9,8},{10,9},{11,1... | collective-permute-start | bytes 12296 | tf_op jit(solution)/shard_map/ppermute | solution.py:209
  74.1 3.2 %collective-permute-start.12 = (f32[32,128]{1,0:T(8,128)S(1)}, f32[32,128]{1,0:T(8,128)S(1)}, u32[]{:S(2)}, u32[]{:S(2)}) collective-permute-start(f32[32,128]{1,0:T(8,128)S(1)} %reshape.128), channel_id=1, source_target_pairs={{0,1},{1,2},{2,3},{3,0},{4,5},{5,6},{6,7},{7,4},{8,9},{9,10},{10,1... | collective-permute-start | bytes 49160 | tf_op jit(solution)/shard_map/ppermute | solution.py:209
  74.5 3.4 %collective-permute-start.13 = (f32[32,128]{1,0:T(8,128)S(1)}, f32[32,128]{1,0:T(8,128)S(1)}, u32[]{:S(2)}, u32[]{:S(2)}) collective-permute-start(f32[32,128]{1,0:T(8,128)S(1)} %reshape.130), channel_id=1, source_target_pairs={{1,0},{2,1},{3,2},{0,3},{5,4},{6,5},{7,6},{4,7},{9,8},{10,9},{11,1... | collective-permute-start | bytes 49160 | tf_op jit(solution)/shard_map/ppermute | solution.py:209
  78.7 6.4 %collective-permute-start.14 = (f32[4,16,4,128]{3,2,1,0:T(4,128)S(1)}, f32[4,16,4,128]{3,2,1,0:T(4,128)S(1)}, u32[]{:S(2)}, u32[]{:S(2)}) collective-permute-start(f32[4,16,4,128]{3,2,1,0:T(4,128)S(1)} %get-tuple-element.8), channel_id=1, source_target_pairs={{0,4},{4,8},{8,12},{12,16},{16,20},{20,24},{24,28},{28,0},{1,5},{5... | collective-permute-start | bytes 393224 | tf_op jit(solution)/shard_map/ppermute | solution.py:211
  78.8 9.8 %collective-permute-start.15 = (f32[4,16,4,128]{3,2,1,0:T(4,128)S(1)}, f32[4,16,4,128]{3,2,1,0:T(4,128)S(1)}, u32[]{:S(2)}, u32[]{:S(2)}) collective-permute-start(f32[4,16,4,128]{3,2,1,0:T(4,128)S(1)} %get-tuple-element.9), channel_id=1, source_target_pairs={{4,0},{8,4},{12,8},{16,12},{20,16},{24,20},{28,24},{0,28},{5,1},{9... | collective-permute-start | bytes 393224 | tf_op jit(solution)/shard_map/ppermute | solution.py:211
  88.7 4.3 %collective-permute-start.16 = (f32[4,4,8,128]{3,2,1,0:T(8,128)S(1)}, f32[4,4,8,128]{3,2,1,0:T(8,128)S(1)}, u32[]{:S(2)}, u32[]{:S(2)}) collective-permute-start(f32[4,4,8,128]{3,2,1,0:T(8,128)S(1)} %get-tuple-element.10), channel_id=1, source_target_pairs={{0,32},{32,64},{64,96},{96,0},{1,33},{33,65},{65,97},{97,1},{2,34}... | collective-permute-start | bytes 196616 | tf_op jit(solution)/shard_map/ppermute | solution.py:211
  88.8 5.5 %collective-permute-start.17 = (f32[4,4,8,128]{3,2,1,0:T(8,128)S(1)}, f32[4,4,8,128]{3,2,1,0:T(8,128)S(1)}, u32[]{:S(2)}, u32[]{:S(2)}) collective-permute-start(f32[4,4,8,128]{3,2,1,0:T(8,128)S(1)} %get-tuple-element.11), channel_id=1, source_target_pairs={{32,0},{64,32},{96,64},{0,96},{33,1},{65,33},{97,65},{1,97},{34,2}... | collective-permute-start | bytes 196616 | tf_op jit(solution)/shard_map/ppermute | solution.py:211

commit v6 on v5

--- a/solution.py
+++ b/solution.py
@@ -193,7 +193,7 @@
         scratch_shapes=scratch,
         compiler_params=pltpu.CompilerParams(vmem_limit_bytes=48 * 1024 * 1024),
         cost_estimate=pl.CostEstimate(
-            flops=40_000_000, transcendentals=0, bytes_accessed=2_000_000
+            flops=4_000_000_000, transcendentals=0, bytes_accessed=2_000_000
         ),
     )(*args)
 

time: 96.7 us -> 97 us (level)
  no operation moved by 1% of the time
where the time goes in v6:
time: 97 us; the launch traced here: 95.8 us
  waiting for transfers between devices  31.8 us (33%)
  starting transfers between devices  27 us (28%)
  Pallas kernels  25.6 us (26%)
  local copies, waits for them, and re-layouts  9.25 us (10%)
  between operations  1.1 us (1%)
  other arithmetic  1.08 us (1%)
    pallas_call x4, Pallas kernels, vmem_call(): pl.pallas_call(kernel, out_shape=out_shapes, in_specs=[pl.BlockSpec(memor...  25.6 us
    ppermute x8, waiting for transfers between devices, shift_from(): return lax.ppermute(piece, axis, pairs)  23.7 us
    ppermute x8, starting transfers between devices, shift_from(): return lax.ppermute(piece, axis, pairs)  13.7 us
    ppermute x6, starting transfers between devices, trade(): lax.ppermute(flat, axis, [(i, (i + 1) % lax.axis_size(axis)) if upward el...  9.65 us
    ppermute x6, waiting for transfers between devices, trade(): lax.ppermute(flat, axis, [(i, (i + 1) % lax.axis_size(axis)) if upward el...  7.05 us
    ppermute x4, starting transfers between devices, shift_from(): flat = lax.ppermute(piece.reshape(-1, 128), axis, pairs)  3.68 us
    unnamed x14, local copies, waits for them, and re-layouts  3.6 us
  transfers between devices with their start and end apart: 18, of which 13 were waited for; matrix products, arithmetic and copies ran while one was open for 2% of the time, Pallas kernels for 9%

profile of v6, /device:TPU:102, one launch (start us, length us, event | category | flops | bytes accessed | tf_op | source)
XLA Modules:
  0.0 95.8 jit_solution(2729590798883792352)
XLA Ops:
  0.6 0.7 slice_bitcast_fusion.4
  1.4 1.0 %copy-done = s32[2,2,3,8,8,128]{5,4,3,2,1,0:T(8,128)S(1)} copy-done((s32[2,2,3,8,8,128]{5,4,3,2,1,0:T(8,128)S(1)}, s32[2,2,3,8,8,128]{5,4,3,2,1,0:T(8,128)}, u32[]{:S(2)}) %copy-start) | copy-done | bytes 393240
  2.4 1.0 %copy-done.2 = f32[2,2,3,8,8,128]{5,4,3,2,1,0:T(8,128)S(1)} copy-done((f32[2,2,3,8,8,128]{5,4,3,2,1,0:T(8,128)S(1)}, f32[2,2,3,8,8,128]{5,4,3,2,1,0:T(8,128)}, u32[]{:S(2)}) %copy-start.2) | copy-done | bytes 393240
  3.4 2.4 %shard_map.59 = f32[16,16,256]{2,1,0:T(8,128)S(1)} custom-call(f32[8,8,128]{2,1,0:T(8,128)S(1)} %copy-done.4, s32[2,2,3,8,8,128]{5,4,3,2,1,0:T(8,128)S(1)} %copy-done, f32[2,2,3,8,8,128]{5,4,3,2,1,0:T(8,128)S(1)} %copy-done.2), custom_call_target="tpu_custom_call" | custom-call | flops 4000000000 | bytes 2000000 | tf_op jit(solution)/shard_map/pallas_call | solution.py:188
  5.9 0.9 collective-permute-start.1
  6.8 2.5 %collective-permute-start = (f32[160,128]{1,0:T(8,128)S(1)}, f32[160,128]{1,0:T(8,128)S(1)}, u32[]{:S(2)}, u32[]{:S(2)}) collective-permute-start(f32[160,128]{1,0:T(8,128)S(1)} %pad_maximum_fusion.5), channel_id=1, source_target_pairs={{0,32},{32,64},{64,96},{96,0},{1,33},{33,65},{65,97},{97,1},{2,34}... | collective-permute-start | bytes 245768 | tf_op jit(solution)/shard_map/ppermute | solution.py:265
  9.2 2.3 %collective-permute-done.1 = f32[160,128]{1,0:T(8,128)S(1)} collective-permute-done((f32[160,128]{1,0:T(8,128)S(1)}, f32[160,128]{1,0:T(8,128)S(1)}, u32[]{:S(2)}, u32[]{:S(2)}) %collective-permute-start.1) | collective-permute-done | bytes 81952 | tf_op jit(solution)/shard_map/ppermute | solution.py:265
  11.7 0.7 copy-done.5
  12.5 0.5 collective-permute-start.3
  13.0 5.2 %collective-permute-start.2 = (f32[128,128]{1,0:T(8,128)S(1)}, f32[128,128]{1,0:T(8,128)S(1)}, u32[]{:S(2)}, u32[]{:S(2)}) collective-permute-start(f32[128,128]{1,0:T(8,128)S(1)} %pad_maximum_fusion.8), channel_id=1, source_target_pairs={{0,4},{4,8},{8,12},{12,16},{16,20},{20,24},{24,28},{28,0},{1,5},{5... | collective-permute-start | bytes 196616 | tf_op jit(solution)/shard_map/ppermute | solution.py:265
  18.3 2.2 %collective-permute-done.3 = f32[128,128]{1,0:T(8,128)S(1)} collective-permute-done((f32[128,128]{1,0:T(8,128)S(1)}, f32[128,128]{1,0:T(8,128)S(1)}, u32[]{:S(2)}, u32[]{:S(2)}) %collective-permute-start.3) | collective-permute-done | bytes 65568 | tf_op jit(solution)/shard_map/ppermute | solution.py:265
  21.0 0.1 reshape.119
  21.4 0.5 collective-permute-start.4
  22.0 0.8 collective-permute-done.5
  22.7 0.1 reshape.122
  22.9 1.7 %collective-permute-done.4 = f32[10,128]{1,0:T(8,128)S(1)} collective-permute-done((f32[10,128]{1,0:T(8,128)S(1)}, f32[10,128]{1,0:T(8,128)S(1)}, u32[]{:S(2)}, u32[]{:S(2)}) %collective-permute-start.4) | collective-permute-done | bytes 5152 | tf_op jit(solution)/shard_map/ppermute | solution.py:265
  24.6 0.1 reshape.123
  24.8 0.7 copy-done.1
  25.7 4.2 %shard_map.60 = (f32[8,8,128]{2,1,0:T(8,128)S(1)}, f32[3,8,8,128]{3,2,1,0:T(8,128)S(1)}) custom-call(f32[16,16,256]{2,1,0:T(8,128)S(1)} %pad_maximum_fusion.1.wrapped_ref, s32[2,2,3,8,8,128]{5,4,3,2,1,0:T(8,128)S(1)} %copy-done.1, f32[2,2,3,8,8,128]{5,4,3,2,1,0:T(8,128)S(1)} %copy-done.3), custom_call_target="tpu_custom_call" | custom-call | flops 4000000000 | bytes 2000000 | tf_op jit(solution)/shard_map/pallas_call | solution.py:188
  29.9 3.3 %collective-permute-start.6 = (f32[4,8,128]{2,1,0:T(8,128)S(1)}, f32[4,8,128]{2,1,0:T(8,128)S(1)}, u32[]{:S(2)}, u32[]{:S(2)}) collective-permute-start(f32[4,8,128]{2,1,0:T(8,128)S(1)} %get-tuple-element.31), channel_id=1, source_target_pairs={{0,32},{32,64},{64,96},{96,0},{1,33},{33,65},{65,97},{97,1},{2,34}... | collective-permute-start | bytes 49160 | tf_op jit(solution)/shard_map/ppermute | solution.py:211
  33.6 1.1 %collective-permute-done.6 = f32[4,8,128]{2,1,0:T(8,128)S(1)} collective-permute-done((f32[4,8,128]{2,1,0:T(8,128)S(1)}, f32[4,8,128]{2,1,0:T(8,128)S(1)}, u32[]{:S(2)}, u32[]{:S(2)}) %collective-permute-start.6) | collective-permute-done | bytes 16416 | tf_op jit(solution)/shard_map/ppermute | solution.py:211
  34.7 3.8 %collective-permute-done.7 = f32[4,8,128]{2,1,0:T(8,128)S(1)} collective-permute-done((f32[4,8,128]{2,1,0:T(8,128)S(1)}, f32[4,8,128]{2,1,0:T(8,128)S(1)}, u32[]{:S(2)}, u32[]{:S(2)}) %collective-permute-start.7) | collective-permute-done | bytes 16416 | tf_op jit(solution)/shard_map/ppermute | solution.py:211
  38.5 6.1 %collective-permute-start.8 = (f32[16,4,128]{2,1,0:T(4,128)S(1)}, f32[16,4,128]{2,1,0:T(4,128)S(1)}, u32[]{:S(2)}, u32[]{:S(2)}) collective-permute-start(f32[16,4,128]{2,1,0:T(4,128)S(1)} %get-tuple-element.20), channel_id=1, source_target_pairs={{0,4},{4,8},{8,12},{12,16},{16,20},{20,24},{24,28},{28,0},{1,5},{5... | collective-permute-start | bytes 98312 | tf_op jit(solution)/shard_map/ppermute | solution.py:211
  44.7 1.5 %collective-permute-done.8 = f32[16,4,128]{2,1,0:T(4,128)S(1)} collective-permute-done((f32[16,4,128]{2,1,0:T(4,128)S(1)}, f32[16,4,128]{2,1,0:T(4,128)S(1)}, u32[]{:S(2)}, u32[]{:S(2)}) %collective-permute-start.8) | collective-permute-done | bytes 32800 | tf_op jit(solution)/shard_map/ppermute | solution.py:211
  46.2 5.9 %collective-permute-done.9 = f32[16,4,128]{2,1,0:T(4,128)S(1)} collective-permute-done((f32[16,4,128]{2,1,0:T(4,128)S(1)}, f32[16,4,128]{2,1,0:T(4,128)S(1)}, u32[]{:S(2)}, u32[]{:S(2)}) %collective-permute-start.9) | collective-permute-done | bytes 32800 | tf_op jit(solution)/shard_map/ppermute | solution.py:211
  52.3 0.1 reshape.124
  52.6 1.7 %collective-permute-start.10 = (f32[8,128]{1,0:T(8,128)S(1)}, f32[8,128]{1,0:T(8,128)S(1)}, u32[]{:S(2)}, u32[]{:S(2)}) collective-permute-start(f32[8,128]{1,0:T(8,128)S(1)} %reshape.124), channel_id=1, source_target_pairs={{1,0},{2,1},{3,2},{0,3},{5,4},{6,5},{7,6},{4,7},{9,8},{10,9},{11,1... | collective-permute-start | bytes 12296 | tf_op jit(solution)/shard_map/ppermute | solution.py:209
  54.3 8.4 %shard_map.61 = f32[4,16,16,256]{3,2,1,0:T(8,128)S(1)} custom-call(f32[8,8,128]{2,1,0:T(8,128)S(1)} %fusion.8.adjoint_ref, f32[3,8,8,128]{3,2,1,0:T(8,128)S(1)} %get-tuple-element.4.grad_ref, s32[2,2,3,8,8,128]{5,4,3,2,1,0:T(8,128)S(1)} %copy-done.1, f32[2,2,3,8,8,128]{5,4,3,2,1,0:T(8,128)S(1)} %copy-done.3), custom_call_target="tpu_custom_call" | custom-call | flops 4000000000 | bytes 2000000 | tf_op jit(solution)/shard_map/pallas_call | solution.py:188
  62.7 0.1 reshape.125
  62.9 0.1 reshape.127
  63.1 10.6 %shard_map.62 = f32[3,16,16,256]{3,2,1,0:T(8,128)S(1)} custom-call(f32[16,16,256]{2,1,0:T(8,128)S(1)} %pad_maximum_fusion.2.wrapped_ref, f32[8,8,128]{2,1,0:T(8,128)S(1)} %copy-done.4, s32[2,2,3,8,8,128]{5,4,3,2,1,0:T(8,128)S(1)} %copy-done.1, f32[2,2,3,8,8,128]{5,4,3,2,1,0:T(8,128)S(1)} %copy-done.3), custom_call_target="tpu_custom_call" | custom-call | flops 4000000000 | bytes 2000000 | tf_op jit(solution)/shard_map/pallas_call | solution.py:188
  73.7 0.1 slice_add_fusion
  73.9 0.2 fusion
  74.1 0.3 reshape.128
  74.4 0.3 reshape.130
  74.7 1.8 %collective-permute-start.13 = (f32[32,128]{1,0:T(8,128)S(1)}, f32[32,128]{1,0:T(8,128)S(1)}, u32[]{:S(2)}, u32[]{:S(2)}) collective-permute-start(f32[32,128]{1,0:T(8,128)S(1)} %reshape.130), channel_id=1, source_target_pairs={{1,0},{2,1},{3,2},{0,3},{5,4},{6,5},{7,6},{4,7},{9,8},{10,9},{11,1... | collective-permute-start | bytes 49160 | tf_op jit(solution)/shard_map/ppermute | solution.py:209
  76.5 1.1 %collective-permute-done.12 = f32[32,128]{1,0:T(8,128)S(1)} collective-permute-done((f32[32,128]{1,0:T(8,128)S(1)}, f32[32,128]{1,0:T(8,128)S(1)}, u32[]{:S(2)}, u32[]{:S(2)}) %collective-permute-start.12) | collective-permute-done | bytes 16416 | tf_op jit(solution)/shard_map/ppermute | solution.py:209
  77.6 0.5 reshape.129
  78.1 0.5 reshape.131
  78.7 0.2 fusion.3
  79.0 2.0 %collective-permute-start.15 = (f32[4,16,4,128]{3,2,1,0:T(4,128)S(1)}, f32[4,16,4,128]{3,2,1,0:T(4,128)S(1)}, u32[]{:S(2)}, u32[]{:S(2)}) collective-permute-start(f32[4,16,4,128]{3,2,1,0:T(4,128)S(1)} %get-tuple-element.9), channel_id=1, source_target_pairs={{4,0},{8,4},{12,8},{16,12},{20,16},{24,20},{28,24},{0,28},{5,1},{9... | collective-permute-start | bytes 393224 | tf_op jit(solution)/shard_map/ppermute | solution.py:211
  81.0 4.3 %collective-permute-done.14 = f32[4,16,4,128]{3,2,1,0:T(4,128)S(1)} collective-permute-done((f32[4,16,4,128]{3,2,1,0:T(4,128)S(1)}, f32[4,16,4,128]{3,2,1,0:T(4,128)S(1)}, u32[]{:S(2)}, u32[]{:S(2)}) %collective-permute-start.14) | collective-permute-done | bytes 131104 | tf_op jit(solution)/shard_map/ppermute | solution.py:211
  85.3 3.4 %collective-permute-done.15 = f32[4,16,4,128]{3,2,1,0:T(4,128)S(1)} collective-permute-done((f32[4,16,4,128]{3,2,1,0:T(4,128)S(1)}, f32[4,16,4,128]{3,2,1,0:T(4,128)S(1)}, u32[]{:S(2)}, u32[]{:S(2)}) %collective-permute-start.15) | collective-permute-done | bytes 131104 | tf_op jit(solution)/shard_map/ppermute | solution.py:211
  89.0 2.0 %collective-permute-start.17 = (f32[4,4,8,128]{3,2,1,0:T(8,128)S(1)}, f32[4,4,8,128]{3,2,1,0:T(8,128)S(1)}, u32[]{:S(2)}, u32[]{:S(2)}) collective-permute-start(f32[4,4,8,128]{3,2,1,0:T(8,128)S(1)} %get-tuple-element.11), channel_id=1, source_target_pairs={{32,0},{64,32},{96,64},{0,96},{33,1},{65,33},{97,65},{1,97},{34,2}... | collective-permute-start | bytes 196616 | tf_op jit(solution)/shard_map/ppermute | solution.py:211
  91.0 2.2 %collective-permute-done.16 = f32[4,4,8,128]{3,2,1,0:T(8,128)S(1)} collective-permute-done((f32[4,4,8,128]{3,2,1,0:T(8,128)S(1)}, f32[4,4,8,128]{3,2,1,0:T(8,128)S(1)}, u32[]{:S(2)}, u32[]{:S(2)}) %collective-permute-start.16) | collective-permute-done | bytes 65568 | tf_op jit(solution)/shard_map/ppermute | solution.py:211
  93.2 1.3 %collective-permute-done.17 = f32[4,4,8,128]{3,2,1,0:T(8,128)S(1)} collective-permute-done((f32[4,4,8,128]{3,2,1,0:T(8,128)S(1)}, f32[4,4,8,128]{3,2,1,0:T(8,128)S(1)}, u32[]{:S(2)}, u32[]{:S(2)}) %collective-permute-start.17) | collective-permute-done | bytes 65568 | tf_op jit(solution)/shard_map/ppermute | solution.py:211
  94.5 0.6 slice_bitcast_fusion
  95.2 0.6 slice.226
  (76 shorter events, 2.4 us)
Async XLA Ops:
  0.6 0.8 copy-start.4
  1.4 1.0 %copy-start = (s32[2,2,3,8,8,128]{5,4,3,2,1,0:T(8,128)S(1)}, s32[2,2,3,8,8,128]{5,4,3,2,1,0:T(8,128)}, u32[]{:S(2)}) copy-start(s32[2,2,3,8,8,128]{5,4,3,2,1,0:T(8,128)} %cells_ref.7) | copy-start | bytes 1179652
  2.4 1.0 %copy-start.2 = (f32[2,2,3,8,8,128]{5,4,3,2,1,0:T(8,128)S(1)}, f32[2,2,3,8,8,128]{5,4,3,2,1,0:T(8,128)}, u32[]{:S(2)}) copy-start(f32[2,2,3,8,8,128]{5,4,3,2,1,0:T(8,128)} %fracs_ref.7) | copy-start | bytes 1179652
  5.9 5.7 %collective-permute-start.1 = (f32[160,128]{1,0:T(8,128)S(1)}, f32[160,128]{1,0:T(8,128)S(1)}, u32[]{:S(2)}, u32[]{:S(2)}) collective-permute-start(f32[160,128]{1,0:T(8,128)S(1)} %pad_maximum_fusion.6), channel_id=1, source_target_pairs={{32,0},{64,32},{96,64},{0,96},{33,1},{65,33},{97,65},{1,97},{34,2}... | collective-permute-start | bytes 245768 | tf_op jit(solution)/shard_map/ppermute | solution.py:265
  6.8 4.8 %collective-permute-start = (f32[160,128]{1,0:T(8,128)S(1)}, f32[160,128]{1,0:T(8,128)S(1)}, u32[]{:S(2)}, u32[]{:S(2)}) collective-permute-start(f32[160,128]{1,0:T(8,128)S(1)} %pad_maximum_fusion.5), channel_id=1, source_target_pairs={{0,32},{32,64},{64,96},{96,0},{1,33},{33,65},{65,97},{97,1},{2,34}... | collective-permute-start | bytes 245768 | tf_op jit(solution)/shard_map/ppermute | solution.py:265
  11.7 0.8 copy-start.5
  12.5 7.9 %collective-permute-start.3 = (f32[128,128]{1,0:T(8,128)S(1)}, f32[128,128]{1,0:T(8,128)S(1)}, u32[]{:S(2)}, u32[]{:S(2)}) collective-permute-start(f32[128,128]{1,0:T(8,128)S(1)} %pad_maximum_fusion.9), channel_id=1, source_target_pairs={{4,0},{8,4},{12,8},{16,12},{20,16},{24,20},{28,24},{0,28},{5,1},{9... | collective-permute-start | bytes 196616 | tf_op jit(solution)/shard_map/ppermute | solution.py:265
  13.0 7.5 %collective-permute-start.2 = (f32[128,128]{1,0:T(8,128)S(1)}, f32[128,128]{1,0:T(8,128)S(1)}, u32[]{:S(2)}, u32[]{:S(2)}) collective-permute-start(f32[128,128]{1,0:T(8,128)S(1)} %pad_maximum_fusion.8), channel_id=1, source_target_pairs={{0,4},{4,8},{8,12},{12,16},{16,20},{20,24},{24,28},{28,0},{1,5},{5... | collective-permute-start | bytes 196616 | tf_op jit(solution)/shard_map/ppermute | solution.py:265
  21.3 1.4 %collective-permute-start.5 = (f32[10,128]{1,0:T(8,128)S(1)}, f32[10,128]{1,0:T(8,128)S(1)}, u32[]{:S(2)}, u32[]{:S(2)}) collective-permute-start(f32[10,128]{1,0:T(8,128)S(1)} %pad_maximum_fusion.11), channel_id=1, source_target_pairs={{1,0},{2,1},{3,2},{0,3},{5,4},{6,5},{7,6},{4,7},{9,8},{10,9},{11,1... | collective-permute-start | bytes 15368 | tf_op jit(solution)/shard_map/ppermute | solution.py:265
  21.4 3.2 %collective-permute-start.4 = (f32[10,128]{1,0:T(8,128)S(1)}, f32[10,128]{1,0:T(8,128)S(1)}, u32[]{:S(2)}, u32[]{:S(2)}) collective-permute-start(f32[10,128]{1,0:T(8,128)S(1)} %pad_maximum_fusion.10), channel_id=1, source_target_pairs={{0,1},{1,2},{2,3},{3,0},{4,5},{5,6},{6,7},{7,4},{8,9},{9,10},{10,1... | collective-permute-start | bytes 15368 | tf_op jit(solution)/shard_map/ppermute | solution.py:265
  24.6 1.0 %copy-start.1 = (s32[2,2,3,8,8,128]{5,4,3,2,1,0:T(8,128)S(1)}, s32[2,2,3,8,8,128]{5,4,3,2,1,0:T(8,128)}, u32[]{:S(2)}) copy-start(s32[2,2,3,8,8,128]{5,4,3,2,1,0:T(8,128)} %cells_ref.7) | copy-start | bytes 1179652
  24.6 1.1 %copy-start.3 = (f32[2,2,3,8,8,128]{5,4,3,2,1,0:T(8,128)S(1)}, f32[2,2,3,8,8,128]{5,4,3,2,1,0:T(8,128)}, u32[]{:S(2)}) copy-start(f32[2,2,3,8,8,128]{5,4,3,2,1,0:T(8,128)} %fracs_ref.7) | copy-start | bytes 1179652
  29.9 4.8 %collective-permute-start.6 = (f32[4,8,128]{2,1,0:T(8,128)S(1)}, f32[4,8,128]{2,1,0:T(8,128)S(1)}, u32[]{:S(2)}, u32[]{:S(2)}) collective-permute-start(f32[4,8,128]{2,1,0:T(8,128)S(1)} %get-tuple-element.31), channel_id=1, source_target_pairs={{0,32},{32,64},{64,96},{96,0},{1,33},{33,65},{65,97},{97,1},{2,34}... | collective-permute-start | bytes 49160 | tf_op jit(solution)/shard_map/ppermute | solution.py:211
  33.5 5.0 %collective-permute-start.7 = (f32[4,8,128]{2,1,0:T(8,128)S(1)}, f32[4,8,128]{2,1,0:T(8,128)S(1)}, u32[]{:S(2)}, u32[]{:S(2)}) collective-permute-start(f32[4,8,128]{2,1,0:T(8,128)S(1)} %get-tuple-element.30), channel_id=1, source_target_pairs={{32,0},{64,32},{96,64},{0,96},{33,1},{65,33},{97,65},{1,97},{34,2}... | collective-permute-start | bytes 49160 | tf_op jit(solution)/shard_map/ppermute | solution.py:211
  38.5 7.7 %collective-permute-start.8 = (f32[16,4,128]{2,1,0:T(4,128)S(1)}, f32[16,4,128]{2,1,0:T(4,128)S(1)}, u32[]{:S(2)}, u32[]{:S(2)}) collective-permute-start(f32[16,4,128]{2,1,0:T(4,128)S(1)} %get-tuple-element.20), channel_id=1, source_target_pairs={{0,4},{4,8},{8,12},{12,16},{16,20},{20,24},{24,28},{28,0},{1,5},{5... | collective-permute-start | bytes 98312 | tf_op jit(solution)/shard_map/ppermute | solution.py:211
  44.6 7.5 %collective-permute-start.9 = (f32[16,4,128]{2,1,0:T(4,128)S(1)}, f32[16,4,128]{2,1,0:T(4,128)S(1)}, u32[]{:S(2)}, u32[]{:S(2)}) collective-permute-start(f32[16,4,128]{2,1,0:T(4,128)S(1)} %get-tuple-element.21), channel_id=1, source_target_pairs={{4,0},{8,4},{12,8},{16,12},{20,16},{24,20},{28,24},{0,28},{5,1},{9... | collective-permute-start | bytes 98312 | tf_op jit(solution)/shard_map/ppermute | solution.py:211
  52.5 10.4 %collective-permute-start.11 = (f32[8,128]{1,0:T(8,128)S(1)}, f32[8,128]{1,0:T(8,128)S(1)}, u32[]{:S(2)}, u32[]{:S(2)}) collective-permute-start(f32[8,128]{1,0:T(8,128)S(1)} %reshape.126), channel_id=1, source_target_pairs={{0,1},{1,2},{2,3},{3,0},{4,5},{5,6},{6,7},{7,4},{8,9},{9,10},{10,1... | collective-permute-start | bytes 12296 | tf_op jit(solution)/shard_map/ppermute | solution.py:209
  52.6 10.1 %collective-permute-start.10 = (f32[8,128]{1,0:T(8,128)S(1)}, f32[8,128]{1,0:T(8,128)S(1)}, u32[]{:S(2)}, u32[]{:S(2)}) collective-permute-start(f32[8,128]{1,0:T(8,128)S(1)} %reshape.124), channel_id=1, source_target_pairs={{1,0},{2,1},{3,2},{0,3},{5,4},{6,5},{7,6},{4,7},{9,8},{10,9},{11,1... | collective-permute-start | bytes 12296 | tf_op jit(solution)/shard_map/ppermute | solution.py:209
  74.4 3.2 %collective-permute-start.12 = (f32[32,128]{1,0:T(8,128)S(1)}, f32[32,128]{1,0:T(8,128)S(1)}, u32[]{:S(2)}, u32[]{:S(2)}) collective-permute-start(f32[32,128]{1,0:T(8,128)S(1)} %reshape.128), channel_id=1, source_target_pairs={{0,1},{1,2},{2,3},{3,0},{4,5},{5,6},{6,7},{7,4},{8,9},{9,10},{10,1... | collective-permute-start | bytes 49160 | tf_op jit(solution)/shard_map/ppermute | solution.py:209
  74.7 3.4 %collective-permute-start.13 = (f32[32,128]{1,0:T(8,128)S(1)}, f32[32,128]{1,0:T(8,128)S(1)}, u32[]{:S(2)}, u32[]{:S(2)}) collective-permute-start(f32[32,128]{1,0:T(8,128)S(1)} %reshape.130), channel_id=1, source_target_pairs={{1,0},{2,1},{3,2},{0,3},{5,4},{6,5},{7,6},{4,7},{9,8},{10,9},{11,1... | collective-permute-start | bytes 49160 | tf_op jit(solution)/shard_map/ppermute | solution.py:209
  78.9 6.4 %collective-permute-start.14 = (f32[4,16,4,128]{3,2,1,0:T(4,128)S(1)}, f32[4,16,4,128]{3,2,1,0:T(4,128)S(1)}, u32[]{:S(2)}, u32[]{:S(2)}) collective-permute-start(f32[4,16,4,128]{3,2,1,0:T(4,128)S(1)} %get-tuple-element.8), channel_id=1, source_target_pairs={{0,4},{4,8},{8,12},{12,16},{16,20},{20,24},{24,28},{28,0},{1,5},{5... | collective-permute-start | bytes 393224 | tf_op jit(solution)/shard_map/ppermute | solution.py:211
  79.0 9.8 %collective-permute-start.15 = (f32[4,16,4,128]{3,2,1,0:T(4,128)S(1)}, f32[4,16,4,128]{3,2,1,0:T(4,128)S(1)}, u32[]{:S(2)}, u32[]{:S(2)}) collective-permute-start(f32[4,16,4,128]{3,2,1,0:T(4,128)S(1)} %get-tuple-element.9), channel_id=1, source_target_pairs={{4,0},{8,4},{12,8},{16,12},{20,16},{24,20},{28,24},{0,28},{5,1},{9... | collective-permute-start | bytes 393224 | tf_op jit(solution)/shard_map/ppermute | solution.py:211
  88.9 4.3 %collective-permute-start.16 = (f32[4,4,8,128]{3,2,1,0:T(8,128)S(1)}, f32[4,4,8,128]{3,2,1,0:T(8,128)S(1)}, u32[]{:S(2)}, u32[]{:S(2)}) collective-permute-start(f32[4,4,8,128]{3,2,1,0:T(8,128)S(1)} %get-tuple-element.10), channel_id=1, source_target_pairs={{0,32},{32,64},{64,96},{96,0},{1,33},{33,65},{65,97},{97,1},{2,34}... | collective-permute-start | bytes 196616 | tf_op jit(solution)/shard_map/ppermute | solution.py:211
  89.0 5.5 %collective-permute-start.17 = (f32[4,4,8,128]{3,2,1,0:T(8,128)S(1)}, f32[4,4,8,128]{3,2,1,0:T(8,128)S(1)}, u32[]{:S(2)}, u32[]{:S(2)}) collective-permute-start(f32[4,4,8,128]{3,2,1,0:T(8,128)S(1)} %get-tuple-element.11), channel_id=1, source_target_pairs={{32,0},{64,32},{96,64},{0,96},{33,1},{65,33},{97,65},{1,97},{34,2}... | collective-permute-start | bytes 196616 | tf_op jit(solution)/shard_map/ppermute | solution.py:211

commit v7 on v4

--- a/solution.py
+++ b/solution.py
@@ -193,7 +193,7 @@
         scratch_shapes=scratch,
         compiler_params=pltpu.CompilerParams(vmem_limit_bytes=48 * 1024 * 1024),
         cost_estimate=pl.CostEstimate(
-            flops=40_000_000, transcendentals=0, bytes_accessed=2_000_000
+            flops=4_000_000_000, transcendentals=0, bytes_accessed=2_000_000
         ),
     )(*args)
 

time: 95.1 us -> 97.1 us (1.021)
  starting transfers between devices: 25.7 us -> 28.9 us
  waiting for transfers between devices: 32.3 us -> 30.6 us
    ppermute x16, starting transfers between devices: 18.4 us -> 22.2 us  [shift_from(): return lax.ppermute(piece, axis, pairs)]
    ppermute x16, waiting for transfers between devices: 31.2 us -> 29.5 us  [shift_from(): return lax.ppermute(piece, axis, pairs)]
    unnamed x16 -> x18, local copies, waits for them, and re-layouts: 3.59 us -> 4.8 us
  transfers between devices with their start and end apart: 24 -> 24, of which waited for: 11 -> 12; matrix products, arithmetic and copies ran while one was open for 3% -> 2% of each run, Pallas kernels for 16% -> 9%
where the time goes in v7:
time: 97.1 us; the launch traced here: 96.7 us
  waiting for transfers between devices  30.6 us (32%)
  starting transfers between devices  28.9 us (30%)
  Pallas kernels  25.6 us (26%)
  local copies, waits for them, and re-layouts  9.64 us (10%)
  other arithmetic  1.04 us (1%)
  between operations  1 us (1%)
    ppermute x16, waiting for transfers between devices, shift_from(): return lax.ppermute(piece, axis, pairs)  29.5 us
    pallas_call x4, Pallas kernels, vmem_call(): pl.pallas_call(kernel, out_shape=out_shapes, in_specs=[pl.BlockSpec(memor...  25.6 us
    ppermute x16, starting transfers between devices, shift_from(): return lax.ppermute(piece, axis, pairs)  22.2 us
    ppermute x8, starting transfers between devices, shift_from(): flat = lax.ppermute(piece.reshape(-1, 128), axis, pairs)  6.64 us
    unnamed x18, local copies, waits for them, and re-layouts  4.8 us
  transfers between devices with their start and end apart: 24, of which 12 were waited for; matrix products, arithmetic and copies ran while one was open for 2% of the time, Pallas kernels for 9%

profile of v7, /device:TPU:102, one launch (start us, length us, event | category | flops | bytes accessed | tf_op | source)
XLA Modules:
  0.0 96.7 jit_solution(13094566107712752995)
XLA Ops:
  0.6 1.0 %copy-done = s32[2,2,3,8,8,128]{5,4,3,2,1,0:T(8,128)S(1)} copy-done((s32[2,2,3,8,8,128]{5,4,3,2,1,0:T(8,128)S(1)}, s32[2,2,3,8,8,128]{5,4,3,2,1,0:T(8,128)}, u32[]{:S(2)}) %copy-start) | copy-done | bytes 393240
  1.6 1.0 %copy-done.2 = f32[2,2,3,8,8,128]{5,4,3,2,1,0:T(8,128)S(1)} copy-done((f32[2,2,3,8,8,128]{5,4,3,2,1,0:T(8,128)S(1)}, f32[2,2,3,8,8,128]{5,4,3,2,1,0:T(8,128)}, u32[]{:S(2)}) %copy-start.2) | copy-done | bytes 393240
  2.6 0.8 copy-done.4
  3.4 2.4 %shard_map.59 = f32[16,16,256]{2,1,0:T(8,128)S(1)} custom-call(f32[8,8,128]{2,1,0:T(8,128)S(1)} %copy-done.4, s32[2,2,3,8,8,128]{5,4,3,2,1,0:T(8,128)S(1)} %copy-done, f32[2,2,3,8,8,128]{5,4,3,2,1,0:T(8,128)S(1)} %copy-done.2), custom_call_target="tpu_custom_call" | custom-call | flops 4000000000 | bytes 2000000 | tf_op jit(solution)/shard_map/pallas_call | solution.py:188
  6.0 1.1 %collective-permute-start.1 = (f32[8,128]{1,0:T(8,128)S(1)}, f32[8,128]{1,0:T(8,128)S(1)}, u32[]{:S(2)}, u32[]{:S(2)}) collective-permute-start(f32[8,128]{1,0:T(8,128)S(1)} %reshape.54), channel_id=1, source_target_pairs={{1,0},{2,1},{3,2},{0,3},{5,4},{6,5},{7,6},{4,7},{9,8},{10,9},{11,1... | collective-permute-start | bytes 12296 | tf_op jit(solution)/shard_map/ppermute | solution.py:209
  7.3 0.6 copy-done.6
  7.9 0.8 collective-permute-start.7
  8.7 2.4 %collective-permute-start.6 = (f32[4,8,128]{2,1,0:T(8,128)S(1)}, f32[4,8,128]{2,1,0:T(8,128)S(1)}, u32[]{:S(2)}, u32[]{:S(2)}) collective-permute-start(f32[4,8,128]{2,1,0:T(8,128)S(1)} %get-tuple-element.29), channel_id=1, source_target_pairs={{0,32},{32,64},{64,96},{96,0},{1,33},{33,65},{65,97},{97,1},{2,34}... | collective-permute-start | bytes 49160 | tf_op jit(solution)/shard_map/ppermute | solution.py:211
  11.2 0.1 reshape.53
  11.6 1.0 collective-permute-done.6
  12.6 0.3 collective-permute-done.7
  12.8 1.6 %collective-permute-start.8 = (f32[16,4,128]{2,1,0:T(4,128)S(1)}, f32[16,4,128]{2,1,0:T(4,128)S(1)}, u32[]{:S(2)}, u32[]{:S(2)}) collective-permute-start(f32[16,4,128]{2,1,0:T(4,128)S(1)} %get-tuple-element.24), channel_id=1, source_target_pairs={{0,4},{4,8},{8,12},{12,16},{16,20},{20,24},{24,28},{28,0},{1,5},{5... | collective-permute-start | bytes 98312 | tf_op jit(solution)/shard_map/ppermute | solution.py:211
  14.4 0.5 collective-permute-start.9
  15.0 5.2 %collective-permute-start.2 = (f32[1,16,4,128]{3,2,1,0:T(4,128)S(1)}, f32[1,16,4,128]{3,2,1,0:T(4,128)S(1)}, u32[]{:S(2)}, u32[]{:S(2)}) collective-permute-start(f32[1,16,4,128]{3,2,1,0:T(4,128)S(1)} %get-tuple-element.14), channel_id=1, source_target_pairs={{0,4},{4,8},{8,12},{12,16},{16,20},{20,24},{24,28},{28,0},{1,5},{5... | collective-permute-start | bytes 98312 | tf_op jit(solution)/shard_map/ppermute | solution.py:211
  20.2 1.8 %collective-permute-done.9 = f32[16,4,128]{2,1,0:T(4,128)S(1)} collective-permute-done((f32[16,4,128]{2,1,0:T(4,128)S(1)}, f32[16,4,128]{2,1,0:T(4,128)S(1)}, u32[]{:S(2)}, u32[]{:S(2)}) %collective-permute-start.9) | collective-permute-done | bytes 32800 | tf_op jit(solution)/shard_map/ppermute | solution.py:211
  22.4 1.7 %collective-permute-start.10 = (f32[8,128]{1,0:T(8,128)S(1)}, f32[8,128]{1,0:T(8,128)S(1)}, u32[]{:S(2)}, u32[]{:S(2)}) collective-permute-start(f32[8,128]{1,0:T(8,128)S(1)} %reshape.56), channel_id=1, source_target_pairs={{1,0},{2,1},{3,2},{0,3},{5,4},{6,5},{7,6},{4,7},{9,8},{10,9},{11,1... | collective-permute-start | bytes 12296 | tf_op jit(solution)/shard_map/ppermute | solution.py:209
  24.2 3.5 %collective-permute-done.3 = f32[1,16,4,128]{3,2,1,0:T(4,128)S(1)} collective-permute-done((f32[1,16,4,128]{3,2,1,0:T(4,128)S(1)}, f32[1,16,4,128]{3,2,1,0:T(4,128)S(1)}, u32[]{:S(2)}, u32[]{:S(2)}) %collective-permute-start.3) | collective-permute-done | bytes 32800 | tf_op jit(solution)/shard_map/ppermute | solution.py:211
  28.2 0.7 copy-done.1
  29.0 4.2 %shard_map.60 = (f32[8,8,128]{2,1,0:T(8,128)S(1)}, f32[3,8,8,128]{3,2,1,0:T(8,128)S(1)}) custom-call(f32[16,16,256]{2,1,0:T(8,128)S(1)} %pad_maximum_fusion.1.wrapped_ref, s32[2,2,3,8,8,128]{5,4,3,2,1,0:T(8,128)S(1)} %copy-done.1, f32[2,2,3,8,8,128]{5,4,3,2,1,0:T(8,128)S(1)} %copy-done.3), custom_call_target="tpu_custom_call" | custom-call | flops 4000000000 | bytes 2000000 | tf_op jit(solution)/shard_map/pallas_call | solution.py:188
  33.2 3.3 %collective-permute-start.12 = (f32[4,8,128]{2,1,0:T(8,128)S(1)}, f32[4,8,128]{2,1,0:T(8,128)S(1)}, u32[]{:S(2)}, u32[]{:S(2)}) collective-permute-start(f32[4,8,128]{2,1,0:T(8,128)S(1)} %get-tuple-element.27), channel_id=1, source_target_pairs={{0,32},{32,64},{64,96},{96,0},{1,33},{33,65},{65,97},{97,1},{2,34}... | collective-permute-start | bytes 49160 | tf_op jit(solution)/shard_map/ppermute | solution.py:211
  36.6 1.9 %collective-permute-start.5 = (f32[1,4,8,128]{3,2,1,0:T(8,128)S(1)}, f32[1,4,8,128]{3,2,1,0:T(8,128)S(1)}, u32[]{:S(2)}, u32[]{:S(2)}) collective-permute-start(f32[1,4,8,128]{3,2,1,0:T(8,128)S(1)} %get-tuple-element.21), channel_id=1, source_target_pairs={{32,0},{64,32},{96,64},{0,96},{33,1},{65,33},{97,65},{1,97},{34,2}... | collective-permute-start | bytes 49160 | tf_op jit(solution)/shard_map/ppermute | solution.py:211
  38.6 4.9 %collective-permute-done.13 = f32[4,8,128]{2,1,0:T(8,128)S(1)} collective-permute-done((f32[4,8,128]{2,1,0:T(8,128)S(1)}, f32[4,8,128]{2,1,0:T(8,128)S(1)}, u32[]{:S(2)}, u32[]{:S(2)}) %collective-permute-start.13) | collective-permute-done | bytes 16416 | tf_op jit(solution)/shard_map/ppermute | solution.py:211
  43.5 1.7 %collective-permute-start.14 = (f32[16,4,128]{2,1,0:T(4,128)S(1)}, f32[16,4,128]{2,1,0:T(4,128)S(1)}, u32[]{:S(2)}, u32[]{:S(2)}) collective-permute-start(f32[16,4,128]{2,1,0:T(4,128)S(1)} %get-tuple-element.22), channel_id=1, source_target_pairs={{0,4},{4,8},{8,12},{12,16},{16,20},{20,24},{24,28},{28,0},{1,5},{5... | collective-permute-start | bytes 98312 | tf_op jit(solution)/shard_map/ppermute | solution.py:211
  45.2 0.4 collective-permute-start.15
  45.7 1.9 %collective-permute-done.14 = f32[16,4,128]{2,1,0:T(4,128)S(1)} collective-permute-done((f32[16,4,128]{2,1,0:T(4,128)S(1)}, f32[16,4,128]{2,1,0:T(4,128)S(1)}, u32[]{:S(2)}, u32[]{:S(2)}) %collective-permute-start.14) | collective-permute-done | bytes 32800 | tf_op jit(solution)/shard_map/ppermute | solution.py:211
  47.5 5.2 %collective-permute-done.15 = f32[16,4,128]{2,1,0:T(4,128)S(1)} collective-permute-done((f32[16,4,128]{2,1,0:T(4,128)S(1)}, f32[16,4,128]{2,1,0:T(4,128)S(1)}, u32[]{:S(2)}, u32[]{:S(2)}) %collective-permute-start.15) | collective-permute-done | bytes 32800 | tf_op jit(solution)/shard_map/ppermute | solution.py:211
  53.2 1.7 %collective-permute-start.16 = (f32[8,128]{1,0:T(8,128)S(1)}, f32[8,128]{1,0:T(8,128)S(1)}, u32[]{:S(2)}, u32[]{:S(2)}) collective-permute-start(f32[8,128]{1,0:T(8,128)S(1)} %reshape.60), channel_id=1, source_target_pairs={{1,0},{2,1},{3,2},{0,3},{5,4},{6,5},{7,6},{4,7},{9,8},{10,9},{11,1... | collective-permute-start | bytes 12296 | tf_op jit(solution)/shard_map/ppermute | solution.py:209
  54.9 8.4 %shard_map.61 = f32[4,16,16,256]{3,2,1,0:T(8,128)S(1)} custom-call(f32[8,8,128]{2,1,0:T(8,128)S(1)} %fusion.9.adjoint_ref, f32[3,8,8,128]{3,2,1,0:T(8,128)S(1)} %get-tuple-element.4.grad_ref, s32[2,2,3,8,8,128]{5,4,3,2,1,0:T(8,128)S(1)} %copy-done.1, f32[2,2,3,8,8,128]{5,4,3,2,1,0:T(8,128)S(1)} %copy-done.3), custom_call_target="tpu_custom_call" | custom-call | flops 4000000000 | bytes 2000000 | tf_op jit(solution)/shard_map/pallas_call | solution.py:188
  63.8 0.6 copy-done.5
  64.4 10.6 %shard_map.62 = f32[3,16,16,256]{3,2,1,0:T(8,128)S(1)} custom-call(f32[16,16,256]{2,1,0:T(8,128)S(1)} %pad_maximum_fusion.2.wrapped_ref, f32[8,8,128]{2,1,0:T(8,128)S(1)} %copy-done.5, s32[2,2,3,8,8,128]{5,4,3,2,1,0:T(8,128)S(1)} %copy-done.1, f32[2,2,3,8,8,128]{5,4,3,2,1,0:T(8,128)S(1)} %copy-done.3), custom_call_target="tpu_custom_call" | custom-call | flops 4000000000 | bytes 2000000 | tf_op jit(solution)/shard_map/pallas_call | solution.py:188
  75.0 0.1 slice_add_fusion
  75.1 0.2 fusion
  75.4 0.3 reshape.64
  75.7 0.3 reshape.66
  76.0 1.8 %collective-permute-start.19 = (f32[32,128]{1,0:T(8,128)S(1)}, f32[32,128]{1,0:T(8,128)S(1)}, u32[]{:S(2)}, u32[]{:S(2)}) collective-permute-start(f32[32,128]{1,0:T(8,128)S(1)} %reshape.66), channel_id=1, source_target_pairs={{1,0},{2,1},{3,2},{0,3},{5,4},{6,5},{7,6},{4,7},{9,8},{10,9},{11,1... | collective-permute-start | bytes 49160 | tf_op jit(solution)/shard_map/ppermute | solution.py:209
  77.8 1.1 %collective-permute-done.18 = f32[32,128]{1,0:T(8,128)S(1)} collective-permute-done((f32[32,128]{1,0:T(8,128)S(1)}, f32[32,128]{1,0:T(8,128)S(1)}, u32[]{:S(2)}, u32[]{:S(2)}) %collective-permute-start.18) | collective-permute-done | bytes 16416 | tf_op jit(solution)/shard_map/ppermute | solution.py:209
  78.9 0.5 reshape.65
  79.4 0.5 reshape.67
  79.9 0.2 fusion.3
  80.3 2.0 %collective-permute-start.21 = (f32[4,16,4,128]{3,2,1,0:T(4,128)S(1)}, f32[4,16,4,128]{3,2,1,0:T(4,128)S(1)}, u32[]{:S(2)}, u32[]{:S(2)}) collective-permute-start(f32[4,16,4,128]{3,2,1,0:T(4,128)S(1)} %get-tuple-element.9), channel_id=1, source_target_pairs={{4,0},{8,4},{12,8},{16,12},{20,16},{24,20},{28,24},{0,28},{5,1},{9... | collective-permute-start | bytes 393224 | tf_op jit(solution)/shard_map/ppermute | solution.py:211
  82.3 3.4 %collective-permute-done.20 = f32[4,16,4,128]{3,2,1,0:T(4,128)S(1)} collective-permute-done((f32[4,16,4,128]{3,2,1,0:T(4,128)S(1)}, f32[4,16,4,128]{3,2,1,0:T(4,128)S(1)}, u32[]{:S(2)}, u32[]{:S(2)}) %collective-permute-start.20) | collective-permute-done | bytes 131104 | tf_op jit(solution)/shard_map/ppermute | solution.py:211
  85.7 3.9 %collective-permute-done.21 = f32[4,16,4,128]{3,2,1,0:T(4,128)S(1)} collective-permute-done((f32[4,16,4,128]{3,2,1,0:T(4,128)S(1)}, f32[4,16,4,128]{3,2,1,0:T(4,128)S(1)}, u32[]{:S(2)}, u32[]{:S(2)}) %collective-permute-start.21) | collective-permute-done | bytes 131104 | tf_op jit(solution)/shard_map/ppermute | solution.py:211
  89.8 0.2 collective-permute-start.22
  89.9 1.9 %collective-permute-start.23 = (f32[4,4,8,128]{3,2,1,0:T(8,128)S(1)}, f32[4,4,8,128]{3,2,1,0:T(8,128)S(1)}, u32[]{:S(2)}, u32[]{:S(2)}) collective-permute-start(f32[4,4,8,128]{3,2,1,0:T(8,128)S(1)} %get-tuple-element.11), channel_id=1, source_target_pairs={{32,0},{64,32},{96,64},{0,96},{33,1},{65,33},{97,65},{1,97},{34,2}... | collective-permute-start | bytes 196616 | tf_op jit(solution)/shard_map/ppermute | solution.py:211
  91.9 2.2 %collective-permute-done.22 = f32[4,4,8,128]{3,2,1,0:T(8,128)S(1)} collective-permute-done((f32[4,4,8,128]{3,2,1,0:T(8,128)S(1)}, f32[4,4,8,128]{3,2,1,0:T(8,128)S(1)}, u32[]{:S(2)}, u32[]{:S(2)}) %collective-permute-start.22) | collective-permute-done | bytes 65568 | tf_op jit(solution)/shard_map/ppermute | solution.py:211
  94.1 1.3 %collective-permute-done.23 = f32[4,4,8,128]{3,2,1,0:T(8,128)S(1)} collective-permute-done((f32[4,4,8,128]{3,2,1,0:T(8,128)S(1)}, f32[4,4,8,128]{3,2,1,0:T(8,128)S(1)}, u32[]{:S(2)}, u32[]{:S(2)}) %collective-permute-start.23) | collective-permute-done | bytes 65568 | tf_op jit(solution)/shard_map/ppermute | solution.py:211
  95.4 0.6 slice_bitcast_fusion
  96.0 0.6 slice.166
  (68 shorter events, 3.0 us)
Async XLA Ops:
  0.6 1.0 %copy-start = (s32[2,2,3,8,8,128]{5,4,3,2,1,0:T(8,128)S(1)}, s32[2,2,3,8,8,128]{5,4,3,2,1,0:T(8,128)}, u32[]{:S(2)}) copy-start(s32[2,2,3,8,8,128]{5,4,3,2,1,0:T(8,128)} %cells_ref.7) | copy-start | bytes 1179652
  1.6 1.0 %copy-start.2 = (f32[2,2,3,8,8,128]{5,4,3,2,1,0:T(8,128)S(1)}, f32[2,2,3,8,8,128]{5,4,3,2,1,0:T(8,128)}, u32[]{:S(2)}) copy-start(f32[2,2,3,8,8,128]{5,4,3,2,1,0:T(8,128)} %fracs_ref.7) | copy-start | bytes 1179652
  2.6 0.8 copy-start.4
  6.0 5.3 %collective-permute-start.1 = (f32[8,128]{1,0:T(8,128)S(1)}, f32[8,128]{1,0:T(8,128)S(1)}, u32[]{:S(2)}, u32[]{:S(2)}) collective-permute-start(f32[8,128]{1,0:T(8,128)S(1)} %reshape.54), channel_id=1, source_target_pairs={{1,0},{2,1},{3,2},{0,3},{5,4},{6,5},{7,6},{4,7},{9,8},{10,9},{11,1... | collective-permute-start | bytes 12296 | tf_op jit(solution)/shard_map/ppermute | solution.py:209
  7.1 0.8 copy-start.6
  7.2 4.0 %collective-permute-start = (f32[8,128]{1,0:T(8,128)S(1)}, f32[8,128]{1,0:T(8,128)S(1)}, u32[]{:S(2)}, u32[]{:S(2)}) collective-permute-start(f32[8,128]{1,0:T(8,128)S(1)} %reshape.52), channel_id=1, source_target_pairs={{0,1},{1,2},{2,3},{3,0},{4,5},{5,6},{6,7},{7,4},{8,9},{9,10},{10,1... | collective-permute-start | bytes 12296 | tf_op jit(solution)/shard_map/ppermute | solution.py:209
  7.9 4.9 %collective-permute-start.7 = (f32[4,8,128]{2,1,0:T(8,128)S(1)}, f32[4,8,128]{2,1,0:T(8,128)S(1)}, u32[]{:S(2)}, u32[]{:S(2)}) collective-permute-start(f32[4,8,128]{2,1,0:T(8,128)S(1)} %get-tuple-element.28), channel_id=1, source_target_pairs={{32,0},{64,32},{96,64},{0,96},{33,1},{65,33},{97,65},{1,97},{34,2}... | collective-permute-start | bytes 49160 | tf_op jit(solution)/shard_map/ppermute | solution.py:211
  8.7 3.9 %collective-permute-start.6 = (f32[4,8,128]{2,1,0:T(8,128)S(1)}, f32[4,8,128]{2,1,0:T(8,128)S(1)}, u32[]{:S(2)}, u32[]{:S(2)}) collective-permute-start(f32[4,8,128]{2,1,0:T(8,128)S(1)} %get-tuple-element.29), channel_id=1, source_target_pairs={{0,32},{32,64},{64,96},{96,0},{1,33},{33,65},{65,97},{97,1},{2,34}... | collective-permute-start | bytes 49160 | tf_op jit(solution)/shard_map/ppermute | solution.py:211
  12.8 7.3 %collective-permute-start.8 = (f32[16,4,128]{2,1,0:T(4,128)S(1)}, f32[16,4,128]{2,1,0:T(4,128)S(1)}, u32[]{:S(2)}, u32[]{:S(2)}) collective-permute-start(f32[16,4,128]{2,1,0:T(4,128)S(1)} %get-tuple-element.24), channel_id=1, source_target_pairs={{0,4},{4,8},{8,12},{12,16},{16,20},{20,24},{24,28},{28,0},{1,5},{5... | collective-permute-start | bytes 98312 | tf_op jit(solution)/shard_map/ppermute | solution.py:211
  14.4 7.5 %collective-permute-start.9 = (f32[16,4,128]{2,1,0:T(4,128)S(1)}, f32[16,4,128]{2,1,0:T(4,128)S(1)}, u32[]{:S(2)}, u32[]{:S(2)}) collective-permute-start(f32[16,4,128]{2,1,0:T(4,128)S(1)} %get-tuple-element.25), channel_id=1, source_target_pairs={{4,0},{8,4},{12,8},{16,12},{20,16},{24,20},{28,24},{0,28},{5,1},{9... | collective-permute-start | bytes 98312 | tf_op jit(solution)/shard_map/ppermute | solution.py:211
  15.0 9.2 %collective-permute-start.2 = (f32[1,16,4,128]{3,2,1,0:T(4,128)S(1)}, f32[1,16,4,128]{3,2,1,0:T(4,128)S(1)}, u32[]{:S(2)}, u32[]{:S(2)}) collective-permute-start(f32[1,16,4,128]{3,2,1,0:T(4,128)S(1)} %get-tuple-element.14), channel_id=1, source_target_pairs={{0,4},{4,8},{8,12},{12,16},{16,20},{20,24},{24,28},{28,0},{1,5},{5... | collective-permute-start | bytes 98312 | tf_op jit(solution)/shard_map/ppermute | solution.py:211
  20.2 7.5 %collective-permute-start.3 = (f32[1,16,4,128]{3,2,1,0:T(4,128)S(1)}, f32[1,16,4,128]{3,2,1,0:T(4,128)S(1)}, u32[]{:S(2)}, u32[]{:S(2)}) collective-permute-start(f32[1,16,4,128]{3,2,1,0:T(4,128)S(1)} %get-tuple-element.15), channel_id=1, source_target_pairs={{4,0},{8,4},{12,8},{16,12},{20,16},{24,20},{28,24},{0,28},{5,1},{9... | collective-permute-start | bytes 98312 | tf_op jit(solution)/shard_map/ppermute | solution.py:211
  22.3 5.6 %collective-permute-start.11 = (f32[8,128]{1,0:T(8,128)S(1)}, f32[8,128]{1,0:T(8,128)S(1)}, u32[]{:S(2)}, u32[]{:S(2)}) collective-permute-start(f32[8,128]{1,0:T(8,128)S(1)} %reshape.58), channel_id=1, source_target_pairs={{0,1},{1,2},{2,3},{3,0},{4,5},{5,6},{6,7},{7,4},{8,9},{9,10},{10,1... | collective-permute-start | bytes 12296 | tf_op jit(solution)/shard_map/ppermute | solution.py:209
  22.4 5.3 %collective-permute-start.10 = (f32[8,128]{1,0:T(8,128)S(1)}, f32[8,128]{1,0:T(8,128)S(1)}, u32[]{:S(2)}, u32[]{:S(2)}) collective-permute-start(f32[8,128]{1,0:T(8,128)S(1)} %reshape.56), channel_id=1, source_target_pairs={{1,0},{2,1},{3,2},{0,3},{5,4},{6,5},{7,6},{4,7},{9,8},{10,9},{11,1... | collective-permute-start | bytes 12296 | tf_op jit(solution)/shard_map/ppermute | solution.py:209
  27.9 1.0 %copy-start.1 = (s32[2,2,3,8,8,128]{5,4,3,2,1,0:T(8,128)S(1)}, s32[2,2,3,8,8,128]{5,4,3,2,1,0:T(8,128)}, u32[]{:S(2)}) copy-start(s32[2,2,3,8,8,128]{5,4,3,2,1,0:T(8,128)} %cells_ref.7) | copy-start | bytes 1179652
  27.9 1.1 %copy-start.3 = (f32[2,2,3,8,8,128]{5,4,3,2,1,0:T(8,128)S(1)}, f32[2,2,3,8,8,128]{5,4,3,2,1,0:T(8,128)}, u32[]{:S(2)}) copy-start(f32[2,2,3,8,8,128]{5,4,3,2,1,0:T(8,128)} %fracs_ref.7) | copy-start | bytes 1179652
  33.2 5.4 %collective-permute-start.12 = (f32[4,8,128]{2,1,0:T(8,128)S(1)}, f32[4,8,128]{2,1,0:T(8,128)S(1)}, u32[]{:S(2)}, u32[]{:S(2)}) collective-permute-start(f32[4,8,128]{2,1,0:T(8,128)S(1)} %get-tuple-element.27), channel_id=1, source_target_pairs={{0,32},{32,64},{64,96},{96,0},{1,33},{33,65},{65,97},{97,1},{2,34}... | collective-permute-start | bytes 49160 | tf_op jit(solution)/shard_map/ppermute | solution.py:211
  36.6 9.1 %collective-permute-start.4 = (f32[1,4,8,128]{3,2,1,0:T(8,128)S(1)}, f32[1,4,8,128]{3,2,1,0:T(8,128)S(1)}, u32[]{:S(2)}, u32[]{:S(2)}) collective-permute-start(f32[1,4,8,128]{3,2,1,0:T(8,128)S(1)} %get-tuple-element.20), channel_id=1, source_target_pairs={{0,32},{32,64},{64,96},{96,0},{1,33},{33,65},{65,97},{97,1},{2,34}... | collective-permute-start | bytes 49160 | tf_op jit(solution)/shard_map/ppermute | solution.py:211
  36.6 9.0 %collective-permute-start.5 = (f32[1,4,8,128]{3,2,1,0:T(8,128)S(1)}, f32[1,4,8,128]{3,2,1,0:T(8,128)S(1)}, u32[]{:S(2)}, u32[]{:S(2)}) collective-permute-start(f32[1,4,8,128]{3,2,1,0:T(8,128)S(1)} %get-tuple-element.21), channel_id=1, source_target_pairs={{32,0},{64,32},{96,64},{0,96},{33,1},{65,33},{97,65},{1,97},{34,2}... | collective-permute-start | bytes 49160 | tf_op jit(solution)/shard_map/ppermute | solution.py:211
  38.6 4.9 %collective-permute-start.13 = (f32[4,8,128]{2,1,0:T(8,128)S(1)}, f32[4,8,128]{2,1,0:T(8,128)S(1)}, u32[]{:S(2)}, u32[]{:S(2)}) collective-permute-start(f32[4,8,128]{2,1,0:T(8,128)S(1)} %get-tuple-element.26), channel_id=1, source_target_pairs={{32,0},{64,32},{96,64},{0,96},{33,1},{65,33},{97,65},{1,97},{34,2}... | collective-permute-start | bytes 49160 | tf_op jit(solution)/shard_map/ppermute | solution.py:211
  43.5 4.0 %collective-permute-start.14 = (f32[16,4,128]{2,1,0:T(4,128)S(1)}, f32[16,4,128]{2,1,0:T(4,128)S(1)}, u32[]{:S(2)}, u32[]{:S(2)}) collective-permute-start(f32[16,4,128]{2,1,0:T(4,128)S(1)} %get-tuple-element.22), channel_id=1, source_target_pairs={{0,4},{4,8},{8,12},{12,16},{16,20},{20,24},{24,28},{28,0},{1,5},{5... | collective-permute-start | bytes 98312 | tf_op jit(solution)/shard_map/ppermute | solution.py:211
  45.2 7.5 %collective-permute-start.15 = (f32[16,4,128]{2,1,0:T(4,128)S(1)}, f32[16,4,128]{2,1,0:T(4,128)S(1)}, u32[]{:S(2)}, u32[]{:S(2)}) collective-permute-start(f32[16,4,128]{2,1,0:T(4,128)S(1)} %get-tuple-element.23), channel_id=1, source_target_pairs={{4,0},{8,4},{12,8},{16,12},{20,16},{24,20},{28,24},{0,28},{5,1},{9... | collective-permute-start | bytes 98312 | tf_op jit(solution)/shard_map/ppermute | solution.py:211
  53.1 10.4 %collective-permute-start.17 = (f32[8,128]{1,0:T(8,128)S(1)}, f32[8,128]{1,0:T(8,128)S(1)}, u32[]{:S(2)}, u32[]{:S(2)}) collective-permute-start(f32[8,128]{1,0:T(8,128)S(1)} %reshape.62), channel_id=1, source_target_pairs={{0,1},{1,2},{2,3},{3,0},{4,5},{5,6},{6,7},{7,4},{8,9},{9,10},{10,1... | collective-permute-start | bytes 12296 | tf_op jit(solution)/shard_map/ppermute | solution.py:209
  53.2 10.1 %collective-permute-start.16 = (f32[8,128]{1,0:T(8,128)S(1)}, f32[8,128]{1,0:T(8,128)S(1)}, u32[]{:S(2)}, u32[]{:S(2)}) collective-permute-start(f32[8,128]{1,0:T(8,128)S(1)} %reshape.60), channel_id=1, source_target_pairs={{1,0},{2,1},{3,2},{0,3},{5,4},{6,5},{7,6},{4,7},{9,8},{10,9},{11,1... | collective-permute-start | bytes 12296 | tf_op jit(solution)/shard_map/ppermute | solution.py:209
  63.6 0.8 copy-start.5
  75.6 3.2 %collective-permute-start.18 = (f32[32,128]{1,0:T(8,128)S(1)}, f32[32,128]{1,0:T(8,128)S(1)}, u32[]{:S(2)}, u32[]{:S(2)}) collective-permute-start(f32[32,128]{1,0:T(8,128)S(1)} %reshape.64), channel_id=1, source_target_pairs={{0,1},{1,2},{2,3},{3,0},{4,5},{5,6},{6,7},{7,4},{8,9},{9,10},{10,1... | collective-permute-start | bytes 49160 | tf_op jit(solution)/shard_map/ppermute | solution.py:209
  76.0 3.4 %collective-permute-start.19 = (f32[32,128]{1,0:T(8,128)S(1)}, f32[32,128]{1,0:T(8,128)S(1)}, u32[]{:S(2)}, u32[]{:S(2)}) collective-permute-start(f32[32,128]{1,0:T(8,128)S(1)} %reshape.66), channel_id=1, source_target_pairs={{1,0},{2,1},{3,2},{0,3},{5,4},{6,5},{7,6},{4,7},{9,8},{10,9},{11,1... | collective-permute-start | bytes 49160 | tf_op jit(solution)/shard_map/ppermute | solution.py:209
  80.2 5.5 %collective-permute-start.20 = (f32[4,16,4,128]{3,2,1,0:T(4,128)S(1)}, f32[4,16,4,128]{3,2,1,0:T(4,128)S(1)}, u32[]{:S(2)}, u32[]{:S(2)}) collective-permute-start(f32[4,16,4,128]{3,2,1,0:T(4,128)S(1)} %get-tuple-element.8), channel_id=1, source_target_pairs={{0,4},{4,8},{8,12},{12,16},{16,20},{20,24},{24,28},{28,0},{1,5},{5... | collective-permute-start | bytes 393224 | tf_op jit(solution)/shard_map/ppermute | solution.py:211
  80.3 9.4 %collective-permute-start.21 = (f32[4,16,4,128]{3,2,1,0:T(4,128)S(1)}, f32[4,16,4,128]{3,2,1,0:T(4,128)S(1)}, u32[]{:S(2)}, u32[]{:S(2)}) collective-permute-start(f32[4,16,4,128]{3,2,1,0:T(4,128)S(1)} %get-tuple-element.9), channel_id=1, source_target_pairs={{4,0},{8,4},{12,8},{16,12},{20,16},{24,20},{28,24},{0,28},{5,1},{9... | collective-permute-start | bytes 393224 | tf_op jit(solution)/shard_map/ppermute | solution.py:211
  89.8 4.3 %collective-permute-start.22 = (f32[4,4,8,128]{3,2,1,0:T(8,128)S(1)}, f32[4,4,8,128]{3,2,1,0:T(8,128)S(1)}, u32[]{:S(2)}, u32[]{:S(2)}) collective-permute-start(f32[4,4,8,128]{3,2,1,0:T(8,128)S(1)} %get-tuple-element.10), channel_id=1, source_target_pairs={{0,32},{32,64},{64,96},{96,0},{1,33},{33,65},{65,97},{97,1},{2,34}... | collective-permute-start | bytes 196616 | tf_op jit(solution)/shard_map/ppermute | solution.py:211
  89.9 5.5 %collective-permute-start.23 = (f32[4,4,8,128]{3,2,1,0:T(8,128)S(1)}, f32[4,4,8,128]{3,2,1,0:T(8,128)S(1)}, u32[]{:S(2)}, u32[]{:S(2)}) collective-permute-start(f32[4,4,8,128]{3,2,1,0:T(8,128)S(1)} %get-tuple-element.11), channel_id=1, source_target_pairs={{32,0},{64,32},{96,64},{0,96},{33,1},{65,33},{97,65},{1,97},{34,2}... | collective-permute-start | bytes 196616 | tf_op jit(solution)/shard_map/ppermute | solution.py:211

commit v8 on v4

--- a/solution.py
+++ b/solution.py
@@ -93,7 +93,7 @@
         return value, grad_x, grad_y, grad_z
 
     zero = jnp.zeros(shape, jnp.float32)
-    value, grad_x, grad_y, grad_z = lax.fori_loop(0, SHIFTS, along_y, (zero,) * 4)
+    value, grad_x, grad_y, grad_z = lax.fori_loop(0, SHIFTS, along_y, (zero,) * 4, unroll=2)
     return value, (grad_x, grad_y, grad_z)
 
 
@@ -123,7 +123,7 @@
         summed_ref[sz] = summed
         return carry
 
-    lax.fori_loop(0, SHIFTS, along_z, 0)
+    lax.fori_loop(0, SHIFTS, along_z, 0, unroll=2)
     total = jnp.zeros((px, py, pz), jnp.float32)
     gap = jnp.zeros((px, py, pz - nz), jnp.float32)
     for sz in range(SHIFTS):

time: 95.1 us -> 94.8 us (level)
  no operation moved by 1% of the time
where the time goes in v8:
time: 94.8 us; the launch traced here: 94.5 us
  waiting for transfers between devices  32.3 us (34%)
  starting transfers between devices  25.7 us (27%)
  Pallas kernels  25.3 us (27%)
  local copies, waits for them, and re-layouts  9.17 us (10%)
  other arithmetic  1.04 us (1%)
  between operations  1.01 us (1%)
    ppermute x16, waiting for transfers between devices, shift_from(): return lax.ppermute(piece, axis, pairs)  31.2 us
    pallas_call x4, Pallas kernels, vmem_call(): pl.pallas_call(kernel, out_shape=out_shapes, in_specs=[pl.BlockSpec(memor...  25.3 us
    ppermute x16, starting transfers between devices, shift_from(): return lax.ppermute(piece, axis, pairs)  18.4 us
    ppermute x8, starting transfers between devices, shift_from(): flat = lax.ppermute(piece.reshape(-1, 128), axis, pairs)  7.36 us
    unnamed x16, local copies, waits for them, and re-layouts  3.59 us
  transfers between devices with their start and end apart: 24, of which 11 were waited for; matrix products, arithmetic and copies ran while one was open for 3% of the time, Pallas kernels for 16%

profile of v8, /device:TPU:102, one launch (start us, length us, event | category | flops | bytes accessed | tf_op | source)
XLA Modules:
  0.0 94.5 jit_solution(465558239503540160)
XLA Ops:
  0.6 0.7 fusion.20
  1.4 0.5 collective-permute-start.6
  1.9 1.0 %copy-done = s32[2,2,3,8,8,128]{5,4,3,2,1,0:T(8,128)S(1)} copy-done((s32[2,2,3,8,8,128]{5,4,3,2,1,0:T(8,128)S(1)}, s32[2,2,3,8,8,128]{5,4,3,2,1,0:T(8,128)}, u32[]{:S(2)}) %copy-start) | copy-done | bytes 393240
  2.9 1.0 %copy-done.2 = f32[2,2,3,8,8,128]{5,4,3,2,1,0:T(8,128)S(1)} copy-done((f32[2,2,3,8,8,128]{5,4,3,2,1,0:T(8,128)S(1)}, f32[2,2,3,8,8,128]{5,4,3,2,1,0:T(8,128)}, u32[]{:S(2)}) %copy-start.2) | copy-done | bytes 393240
  3.9 2.4 %shard_map.59 = f32[16,16,256]{2,1,0:T(8,128)S(1)} custom-call(f32[8,8,128]{2,1,0:T(8,128)S(1)} %copy-done.4, s32[2,2,3,8,8,128]{5,4,3,2,1,0:T(8,128)S(1)} %copy-done, f32[2,2,3,8,8,128]{5,4,3,2,1,0:T(8,128)S(1)} %copy-done.2), custom_call_target="tpu_custom_call" | custom-call | flops 40000000 | bytes 2000000 | tf_op jit(solution)/shard_map/pallas_call | solution.py:188
  6.7 1.8 %collective-permute-start.1 = (f32[8,128]{1,0:T(8,128)S(1)}, f32[8,128]{1,0:T(8,128)S(1)}, u32[]{:S(2)}, u32[]{:S(2)}) collective-permute-start(f32[8,128]{1,0:T(8,128)S(1)} %reshape.54), channel_id=1, source_target_pairs={{1,0},{2,1},{3,2},{0,3},{5,4},{6,5},{7,6},{4,7},{9,8},{10,9},{11,1... | collective-permute-start | bytes 12296 | tf_op jit(solution)/shard_map/ppermute | solution.py:209
  8.5 1.5 %collective-permute-start.7 = (f32[4,8,128]{2,1,0:T(8,128)S(1)}, f32[4,8,128]{2,1,0:T(8,128)S(1)}, u32[]{:S(2)}, u32[]{:S(2)}) collective-permute-start(f32[4,8,128]{2,1,0:T(8,128)S(1)} %get-tuple-element.28), channel_id=1, source_target_pairs={{32,0},{64,32},{96,64},{0,96},{33,1},{65,33},{97,65},{1,97},{34,2}... | collective-permute-start | bytes 49160 | tf_op jit(solution)/shard_map/ppermute | solution.py:211
  10.3 0.1 reshape.55
  10.4 0.7 copy-done.5
  11.2 2.3 %collective-permute-done.7 = f32[4,8,128]{2,1,0:T(8,128)S(1)} collective-permute-done((f32[4,8,128]{2,1,0:T(8,128)S(1)}, f32[4,8,128]{2,1,0:T(8,128)S(1)}, u32[]{:S(2)}, u32[]{:S(2)}) %collective-permute-start.7) | collective-permute-done | bytes 16416 | tf_op jit(solution)/shard_map/ppermute | solution.py:211
  13.4 1.9 %collective-permute-start.8 = (f32[16,4,128]{2,1,0:T(4,128)S(1)}, f32[16,4,128]{2,1,0:T(4,128)S(1)}, u32[]{:S(2)}, u32[]{:S(2)}) collective-permute-start(f32[16,4,128]{2,1,0:T(4,128)S(1)} %get-tuple-element.24), channel_id=1, source_target_pairs={{0,4},{4,8},{8,12},{12,16},{16,20},{20,24},{24,28},{28,0},{1,5},{5... | collective-permute-start | bytes 98312 | tf_op jit(solution)/shard_map/ppermute | solution.py:211
  15.3 0.2 collective-permute-start.9
  15.6 1.8 %collective-permute-done.8 = f32[16,4,128]{2,1,0:T(4,128)S(1)} collective-permute-done((f32[16,4,128]{2,1,0:T(4,128)S(1)}, f32[16,4,128]{2,1,0:T(4,128)S(1)}, u32[]{:S(2)}, u32[]{:S(2)}) %collective-permute-start.8) | collective-permute-done | bytes 32800 | tf_op jit(solution)/shard_map/ppermute | solution.py:211
  17.4 5.4 %collective-permute-done.9 = f32[16,4,128]{2,1,0:T(4,128)S(1)} collective-permute-done((f32[16,4,128]{2,1,0:T(4,128)S(1)}, f32[16,4,128]{2,1,0:T(4,128)S(1)}, u32[]{:S(2)}, u32[]{:S(2)}) %collective-permute-start.9) | collective-permute-done | bytes 32800 | tf_op jit(solution)/shard_map/ppermute | solution.py:211
  23.3 1.7 %collective-permute-start.10 = (f32[8,128]{1,0:T(8,128)S(1)}, f32[8,128]{1,0:T(8,128)S(1)}, u32[]{:S(2)}, u32[]{:S(2)}) collective-permute-start(f32[8,128]{1,0:T(8,128)S(1)} %reshape.56), channel_id=1, source_target_pairs={{1,0},{2,1},{3,2},{0,3},{5,4},{6,5},{7,6},{4,7},{9,8},{10,9},{11,1... | collective-permute-start | bytes 12296 | tf_op jit(solution)/shard_map/ppermute | solution.py:209
  25.2 2.0 %collective-permute-start.3 = (f32[1,16,4,128]{3,2,1,0:T(4,128)S(1)}, f32[1,16,4,128]{3,2,1,0:T(4,128)S(1)}, u32[]{:S(2)}, u32[]{:S(2)}) collective-permute-start(f32[1,16,4,128]{3,2,1,0:T(4,128)S(1)} %get-tuple-element.15), channel_id=1, source_target_pairs={{4,0},{8,4},{12,8},{16,12},{20,16},{24,20},{28,24},{0,28},{5,1},{9... | collective-permute-start | bytes 98312 | tf_op jit(solution)/shard_map/ppermute | solution.py:211
  27.6 0.7 copy-done.1
  28.4 4.2 %shard_map.60 = (f32[8,8,128]{2,1,0:T(8,128)S(1)}, f32[3,8,8,128]{3,2,1,0:T(8,128)S(1)}) custom-call(f32[16,16,256]{2,1,0:T(8,128)S(1)} %pad_maximum_fusion.1.wrapped_ref, s32[2,2,3,8,8,128]{5,4,3,2,1,0:T(8,128)S(1)} %copy-done.1, f32[2,2,3,8,8,128]{5,4,3,2,1,0:T(8,128)S(1)} %copy-done.3), custom_call_target="tpu_custom_call" | custom-call | flops 40000000 | bytes 2000000 | tf_op jit(solution)/shard_map/pallas_call | solution.py:188
  32.6 0.3 collective-permute-start.12
  33.0 1.8 %collective-permute-start.13 = (f32[4,8,128]{2,1,0:T(8,128)S(1)}, f32[4,8,128]{2,1,0:T(8,128)S(1)}, u32[]{:S(2)}, u32[]{:S(2)}) collective-permute-start(f32[4,8,128]{2,1,0:T(8,128)S(1)} %get-tuple-element.26), channel_id=1, source_target_pairs={{32,0},{64,32},{96,64},{0,96},{33,1},{65,33},{97,65},{1,97},{34,2}... | collective-permute-start | bytes 49160 | tf_op jit(solution)/shard_map/ppermute | solution.py:211
  34.8 1.6 %collective-permute-done.12 = f32[4,8,128]{2,1,0:T(8,128)S(1)} collective-permute-done((f32[4,8,128]{2,1,0:T(8,128)S(1)}, f32[4,8,128]{2,1,0:T(8,128)S(1)}, u32[]{:S(2)}, u32[]{:S(2)}) %collective-permute-start.12) | collective-permute-done | bytes 16416 | tf_op jit(solution)/shard_map/ppermute | solution.py:211
  36.4 1.6 %collective-permute-done.13 = f32[4,8,128]{2,1,0:T(8,128)S(1)} collective-permute-done((f32[4,8,128]{2,1,0:T(8,128)S(1)}, f32[4,8,128]{2,1,0:T(8,128)S(1)}, u32[]{:S(2)}, u32[]{:S(2)}) %collective-permute-start.13) | collective-permute-done | bytes 16416 | tf_op jit(solution)/shard_map/ppermute | solution.py:211
  38.0 3.8 %collective-permute-start.14 = (f32[16,4,128]{2,1,0:T(4,128)S(1)}, f32[16,4,128]{2,1,0:T(4,128)S(1)}, u32[]{:S(2)}, u32[]{:S(2)}) collective-permute-start(f32[16,4,128]{2,1,0:T(4,128)S(1)} %get-tuple-element.22), channel_id=1, source_target_pairs={{0,4},{4,8},{8,12},{12,16},{16,20},{20,24},{24,28},{28,0},{1,5},{5... | collective-permute-start | bytes 98312 | tf_op jit(solution)/shard_map/ppermute | solution.py:211
  41.8 0.3 collective-permute-start.4
  42.1 1.7 %collective-permute-start.5 = (f32[1,4,8,128]{3,2,1,0:T(8,128)S(1)}, f32[1,4,8,128]{3,2,1,0:T(8,128)S(1)}, u32[]{:S(2)}, u32[]{:S(2)}) collective-permute-start(f32[1,4,8,128]{3,2,1,0:T(8,128)S(1)} %get-tuple-element.21), channel_id=1, source_target_pairs={{32,0},{64,32},{96,64},{0,96},{33,1},{65,33},{97,65},{1,97},{34,2}... | collective-permute-start | bytes 49160 | tf_op jit(solution)/shard_map/ppermute | solution.py:211
  43.8 5.5 %collective-permute-done.15 = f32[16,4,128]{2,1,0:T(4,128)S(1)} collective-permute-done((f32[16,4,128]{2,1,0:T(4,128)S(1)}, f32[16,4,128]{2,1,0:T(4,128)S(1)}, u32[]{:S(2)}, u32[]{:S(2)}) %collective-permute-start.15) | collective-permute-done | bytes 32800 | tf_op jit(solution)/shard_map/ppermute | solution.py:211
  49.8 1.7 %collective-permute-start.16 = (f32[8,128]{1,0:T(8,128)S(1)}, f32[8,128]{1,0:T(8,128)S(1)}, u32[]{:S(2)}, u32[]{:S(2)}) collective-permute-start(f32[8,128]{1,0:T(8,128)S(1)} %reshape.60), channel_id=1, source_target_pairs={{1,0},{2,1},{3,2},{0,3},{5,4},{6,5},{7,6},{4,7},{9,8},{10,9},{11,1... | collective-permute-start | bytes 12296 | tf_op jit(solution)/shard_map/ppermute | solution.py:209
  51.5 8.3 %shard_map.61 = f32[4,16,16,256]{3,2,1,0:T(8,128)S(1)} custom-call(f32[8,8,128]{2,1,0:T(8,128)S(1)} %fusion.9.adjoint_ref, f32[3,8,8,128]{3,2,1,0:T(8,128)S(1)} %get-tuple-element.4.grad_ref, s32[2,2,3,8,8,128]{5,4,3,2,1,0:T(8,128)S(1)} %copy-done.1, f32[2,2,3,8,8,128]{5,4,3,2,1,0:T(8,128)S(1)} %copy-done.3), custom_call_target="tpu_custom_call" | custom-call | flops 40000000 | bytes 2000000 | tf_op jit(solution)/shard_map/pallas_call | solution.py:188
  60.2 10.5 %shard_map.62 = f32[3,16,16,256]{3,2,1,0:T(8,128)S(1)} custom-call(f32[16,16,256]{2,1,0:T(8,128)S(1)} %pad_maximum_fusion.2.wrapped_ref, f32[8,8,128]{2,1,0:T(8,128)S(1)} %copy-done.4, s32[2,2,3,8,8,128]{5,4,3,2,1,0:T(8,128)S(1)} %copy-done.1, f32[2,2,3,8,8,128]{5,4,3,2,1,0:T(8,128)S(1)} %copy-done.3), custom_call_target="tpu_custom_call" | custom-call | flops 40000000 | bytes 2000000 | tf_op jit(solution)/shard_map/pallas_call | solution.py:188
  70.7 0.1 slice_add_fusion
  70.9 0.2 fusion
  71.1 0.3 reshape.64
  71.4 0.3 reshape.66
  71.7 1.8 %collective-permute-start.19 = (f32[32,128]{1,0:T(8,128)S(1)}, f32[32,128]{1,0:T(8,128)S(1)}, u32[]{:S(2)}, u32[]{:S(2)}) collective-permute-start(f32[32,128]{1,0:T(8,128)S(1)} %reshape.66), channel_id=1, source_target_pairs={{1,0},{2,1},{3,2},{0,3},{5,4},{6,5},{7,6},{4,7},{9,8},{10,9},{11,1... | collective-permute-start | bytes 49160 | tf_op jit(solution)/shard_map/ppermute | solution.py:209
  73.5 1.1 %collective-permute-done.18 = f32[32,128]{1,0:T(8,128)S(1)} collective-permute-done((f32[32,128]{1,0:T(8,128)S(1)}, f32[32,128]{1,0:T(8,128)S(1)}, u32[]{:S(2)}, u32[]{:S(2)}) %collective-permute-start.18) | collective-permute-done | bytes 16416 | tf_op jit(solution)/shard_map/ppermute | solution.py:209
  74.6 0.5 reshape.65
  75.1 0.5 reshape.67
  75.7 0.2 fusion.3
  75.9 1.2 %collective-permute-start.20 = (f32[4,16,4,128]{3,2,1,0:T(4,128)S(1)}, f32[4,16,4,128]{3,2,1,0:T(4,128)S(1)}, u32[]{:S(2)}, u32[]{:S(2)}) collective-permute-start(f32[4,16,4,128]{3,2,1,0:T(4,128)S(1)} %get-tuple-element.8), channel_id=1, source_target_pairs={{0,4},{4,8},{8,12},{12,16},{16,20},{20,24},{24,28},{28,0},{1,5},{5... | collective-permute-start | bytes 393224 | tf_op jit(solution)/shard_map/ppermute | solution.py:211
  77.1 0.9 collective-permute-start.21
  78.0 4.0 %collective-permute-done.20 = f32[4,16,4,128]{3,2,1,0:T(4,128)S(1)} collective-permute-done((f32[4,16,4,128]{3,2,1,0:T(4,128)S(1)}, f32[4,16,4,128]{3,2,1,0:T(4,128)S(1)}, u32[]{:S(2)}, u32[]{:S(2)}) %collective-permute-start.20) | collective-permute-done | bytes 131104 | tf_op jit(solution)/shard_map/ppermute | solution.py:211
  82.0 5.1 %collective-permute-done.21 = f32[4,16,4,128]{3,2,1,0:T(4,128)S(1)} collective-permute-done((f32[4,16,4,128]{3,2,1,0:T(4,128)S(1)}, f32[4,16,4,128]{3,2,1,0:T(4,128)S(1)}, u32[]{:S(2)}, u32[]{:S(2)}) %collective-permute-start.21) | collective-permute-done | bytes 131104 | tf_op jit(solution)/shard_map/ppermute | solution.py:211
  87.2 0.6 collective-permute-start.22
  87.7 1.5 %collective-permute-start.23 = (f32[4,4,8,128]{3,2,1,0:T(8,128)S(1)}, f32[4,4,8,128]{3,2,1,0:T(8,128)S(1)}, u32[]{:S(2)}, u32[]{:S(2)}) collective-permute-start(f32[4,4,8,128]{3,2,1,0:T(8,128)S(1)} %get-tuple-element.11), channel_id=1, source_target_pairs={{32,0},{64,32},{96,64},{0,96},{33,1},{65,33},{97,65},{1,97},{34,2}... | collective-permute-start | bytes 196616 | tf_op jit(solution)/shard_map/ppermute | solution.py:211
  89.3 2.2 %collective-permute-done.22 = f32[4,4,8,128]{3,2,1,0:T(8,128)S(1)} collective-permute-done((f32[4,4,8,128]{3,2,1,0:T(8,128)S(1)}, f32[4,4,8,128]{3,2,1,0:T(8,128)S(1)}, u32[]{:S(2)}, u32[]{:S(2)}) %collective-permute-start.22) | collective-permute-done | bytes 65568 | tf_op jit(solution)/shard_map/ppermute | solution.py:211
  91.5 1.7 %collective-permute-done.23 = f32[4,4,8,128]{3,2,1,0:T(8,128)S(1)} collective-permute-done((f32[4,4,8,128]{3,2,1,0:T(8,128)S(1)}, f32[4,4,8,128]{3,2,1,0:T(8,128)S(1)}, u32[]{:S(2)}, u32[]{:S(2)}) %collective-permute-start.23) | collective-permute-done | bytes 65568 | tf_op jit(solution)/shard_map/ppermute | solution.py:211
  93.2 0.6 slice_bitcast_fusion
  93.8 0.6 slice.166
  (66 shorter events, 2.9 us)
Async XLA Ops:
  0.6 1.2 %copy-start.4 = (f32[8,8,128]{2,1,0:T(8,128)S(1)}, f32[8,8,128]{2,1,0:T(8,128)}, u32[]{:S(2)}) copy-start(f32[8,8,128]{2,1,0:T(8,128)} %cot_ref.3) | copy-start | bytes 98308
  1.4 9.0 %collective-permute-start.6 = (f32[4,8,128]{2,1,0:T(8,128)S(1)}, f32[4,8,128]{2,1,0:T(8,128)S(1)}, u32[]{:S(2)}, u32[]{:S(2)}) collective-permute-start(f32[4,8,128]{2,1,0:T(8,128)S(1)} %get-tuple-element.29), channel_id=1, source_target_pairs={{0,32},{32,64},{64,96},{96,0},{1,33},{33,65},{65,97},{97,1},{2,34}... | collective-permute-start | bytes 49160 | tf_op jit(solution)/shard_map/ppermute | solution.py:211
  1.9 1.0 %copy-start = (s32[2,2,3,8,8,128]{5,4,3,2,1,0:T(8,128)S(1)}, s32[2,2,3,8,8,128]{5,4,3,2,1,0:T(8,128)}, u32[]{:S(2)}) copy-start(s32[2,2,3,8,8,128]{5,4,3,2,1,0:T(8,128)} %cells_ref.7) | copy-start | bytes 1179652
  2.9 1.0 %copy-start.2 = (f32[2,2,3,8,8,128]{5,4,3,2,1,0:T(8,128)S(1)}, f32[2,2,3,8,8,128]{5,4,3,2,1,0:T(8,128)}, u32[]{:S(2)}) copy-start(f32[2,2,3,8,8,128]{5,4,3,2,1,0:T(8,128)} %fracs_ref.7) | copy-start | bytes 1179652
  6.5 3.6 %collective-permute-start = (f32[8,128]{1,0:T(8,128)S(1)}, f32[8,128]{1,0:T(8,128)S(1)}, u32[]{:S(2)}, u32[]{:S(2)}) collective-permute-start(f32[8,128]{1,0:T(8,128)S(1)} %reshape.52), channel_id=1, source_target_pairs={{0,1},{1,2},{2,3},{3,0},{4,5},{5,6},{6,7},{7,4},{8,9},{9,10},{10,1... | collective-permute-start | bytes 12296 | tf_op jit(solution)/shard_map/ppermute | solution.py:209
  6.7 3.6 %collective-permute-start.1 = (f32[8,128]{1,0:T(8,128)S(1)}, f32[8,128]{1,0:T(8,128)S(1)}, u32[]{:S(2)}, u32[]{:S(2)}) collective-permute-start(f32[8,128]{1,0:T(8,128)S(1)} %reshape.54), channel_id=1, source_target_pairs={{1,0},{2,1},{3,2},{0,3},{5,4},{6,5},{7,6},{4,7},{9,8},{10,9},{11,1... | collective-permute-start | bytes 12296 | tf_op jit(solution)/shard_map/ppermute | solution.py:209
  8.5 4.9 %collective-permute-start.7 = (f32[4,8,128]{2,1,0:T(8,128)S(1)}, f32[4,8,128]{2,1,0:T(8,128)S(1)}, u32[]{:S(2)}, u32[]{:S(2)}) collective-permute-start(f32[4,8,128]{2,1,0:T(8,128)S(1)} %get-tuple-element.28), channel_id=1, source_target_pairs={{32,0},{64,32},{96,64},{0,96},{33,1},{65,33},{97,65},{1,97},{34,2}... | collective-permute-start | bytes 49160 | tf_op jit(solution)/shard_map/ppermute | solution.py:211
  10.4 0.8 copy-start.5
  13.4 4.0 %collective-permute-start.8 = (f32[16,4,128]{2,1,0:T(4,128)S(1)}, f32[16,4,128]{2,1,0:T(4,128)S(1)}, u32[]{:S(2)}, u32[]{:S(2)}) collective-permute-start(f32[16,4,128]{2,1,0:T(4,128)S(1)} %get-tuple-element.24), channel_id=1, source_target_pairs={{0,4},{4,8},{8,12},{12,16},{16,20},{20,24},{24,28},{28,0},{1,5},{5... | collective-permute-start | bytes 98312 | tf_op jit(solution)/shard_map/ppermute | solution.py:211
  15.3 7.5 %collective-permute-start.9 = (f32[16,4,128]{2,1,0:T(4,128)S(1)}, f32[16,4,128]{2,1,0:T(4,128)S(1)}, u32[]{:S(2)}, u32[]{:S(2)}) collective-permute-start(f32[16,4,128]{2,1,0:T(4,128)S(1)} %get-tuple-element.25), channel_id=1, source_target_pairs={{4,0},{8,4},{12,8},{16,12},{20,16},{24,20},{28,24},{0,28},{5,1},{9... | collective-permute-start | bytes 98312 | tf_op jit(solution)/shard_map/ppermute | solution.py:211
  23.2 4.1 %collective-permute-start.11 = (f32[8,128]{1,0:T(8,128)S(1)}, f32[8,128]{1,0:T(8,128)S(1)}, u32[]{:S(2)}, u32[]{:S(2)}) collective-permute-start(f32[8,128]{1,0:T(8,128)S(1)} %reshape.58), channel_id=1, source_target_pairs={{0,1},{1,2},{2,3},{3,0},{4,5},{5,6},{6,7},{7,4},{8,9},{9,10},{10,1... | collective-permute-start | bytes 12296 | tf_op jit(solution)/shard_map/ppermute | solution.py:209
  23.3 3.8 %collective-permute-start.10 = (f32[8,128]{1,0:T(8,128)S(1)}, f32[8,128]{1,0:T(8,128)S(1)}, u32[]{:S(2)}, u32[]{:S(2)}) collective-permute-start(f32[8,128]{1,0:T(8,128)S(1)} %reshape.56), channel_id=1, source_target_pairs={{1,0},{2,1},{3,2},{0,3},{5,4},{6,5},{7,6},{4,7},{9,8},{10,9},{11,1... | collective-permute-start | bytes 12296 | tf_op jit(solution)/shard_map/ppermute | solution.py:209
  25.1 7.9 %collective-permute-start.2 = (f32[1,16,4,128]{3,2,1,0:T(4,128)S(1)}, f32[1,16,4,128]{3,2,1,0:T(4,128)S(1)}, u32[]{:S(2)}, u32[]{:S(2)}) collective-permute-start(f32[1,16,4,128]{3,2,1,0:T(4,128)S(1)} %get-tuple-element.14), channel_id=1, source_target_pairs={{0,4},{4,8},{8,12},{12,16},{16,20},{20,24},{24,28},{28,0},{1,5},{5... | collective-permute-start | bytes 98312 | tf_op jit(solution)/shard_map/ppermute | solution.py:211
  25.2 7.8 %collective-permute-start.3 = (f32[1,16,4,128]{3,2,1,0:T(4,128)S(1)}, f32[1,16,4,128]{3,2,1,0:T(4,128)S(1)}, u32[]{:S(2)}, u32[]{:S(2)}) collective-permute-start(f32[1,16,4,128]{3,2,1,0:T(4,128)S(1)} %get-tuple-element.15), channel_id=1, source_target_pairs={{4,0},{8,4},{12,8},{16,12},{20,16},{24,20},{28,24},{0,28},{5,1},{9... | collective-permute-start | bytes 98312 | tf_op jit(solution)/shard_map/ppermute | solution.py:211
  27.3 1.0 %copy-start.1 = (s32[2,2,3,8,8,128]{5,4,3,2,1,0:T(8,128)S(1)}, s32[2,2,3,8,8,128]{5,4,3,2,1,0:T(8,128)}, u32[]{:S(2)}) copy-start(s32[2,2,3,8,8,128]{5,4,3,2,1,0:T(8,128)} %cells_ref.7) | copy-start | bytes 1179652
  27.3 1.1 %copy-start.3 = (f32[2,2,3,8,8,128]{5,4,3,2,1,0:T(8,128)S(1)}, f32[2,2,3,8,8,128]{5,4,3,2,1,0:T(8,128)}, u32[]{:S(2)}) copy-start(f32[2,2,3,8,8,128]{5,4,3,2,1,0:T(8,128)} %fracs_ref.7) | copy-start | bytes 1179652
  32.6 3.8 %collective-permute-start.12 = (f32[4,8,128]{2,1,0:T(8,128)S(1)}, f32[4,8,128]{2,1,0:T(8,128)S(1)}, u32[]{:S(2)}, u32[]{:S(2)}) collective-permute-start(f32[4,8,128]{2,1,0:T(8,128)S(1)} %get-tuple-element.27), channel_id=1, source_target_pairs={{0,32},{32,64},{64,96},{96,0},{1,33},{33,65},{65,97},{97,1},{2,34}... | collective-permute-start | bytes 49160 | tf_op jit(solution)/shard_map/ppermute | solution.py:211
  33.0 5.0 %collective-permute-start.13 = (f32[4,8,128]{2,1,0:T(8,128)S(1)}, f32[4,8,128]{2,1,0:T(8,128)S(1)}, u32[]{:S(2)}, u32[]{:S(2)}) collective-permute-start(f32[4,8,128]{2,1,0:T(8,128)S(1)} %get-tuple-element.26), channel_id=1, source_target_pairs={{32,0},{64,32},{96,64},{0,96},{33,1},{65,33},{97,65},{1,97},{34,2}... | collective-permute-start | bytes 49160 | tf_op jit(solution)/shard_map/ppermute | solution.py:211
  38.0 5.8 %collective-permute-start.14 = (f32[16,4,128]{2,1,0:T(4,128)S(1)}, f32[16,4,128]{2,1,0:T(4,128)S(1)}, u32[]{:S(2)}, u32[]{:S(2)}) collective-permute-start(f32[16,4,128]{2,1,0:T(4,128)S(1)} %get-tuple-element.22), channel_id=1, source_target_pairs={{0,4},{4,8},{8,12},{12,16},{16,20},{20,24},{24,28},{28,0},{1,5},{5... | collective-permute-start | bytes 98312 | tf_op jit(solution)/shard_map/ppermute | solution.py:211
  41.8 7.5 %collective-permute-start.15 = (f32[16,4,128]{2,1,0:T(4,128)S(1)}, f32[16,4,128]{2,1,0:T(4,128)S(1)}, u32[]{:S(2)}, u32[]{:S(2)}) collective-permute-start(f32[16,4,128]{2,1,0:T(4,128)S(1)} %get-tuple-element.23), channel_id=1, source_target_pairs={{4,0},{8,4},{12,8},{16,12},{20,16},{24,20},{28,24},{0,28},{5,1},{9... | collective-permute-start | bytes 98312 | tf_op jit(solution)/shard_map/ppermute | solution.py:211
  41.8 9.7 %collective-permute-start.4 = (f32[1,4,8,128]{3,2,1,0:T(8,128)S(1)}, f32[1,4,8,128]{3,2,1,0:T(8,128)S(1)}, u32[]{:S(2)}, u32[]{:S(2)}) collective-permute-start(f32[1,4,8,128]{3,2,1,0:T(8,128)S(1)} %get-tuple-element.20), channel_id=1, source_target_pairs={{0,32},{32,64},{64,96},{96,0},{1,33},{33,65},{65,97},{97,1},{2,34}... | collective-permute-start | bytes 49160 | tf_op jit(solution)/shard_map/ppermute | solution.py:211
  42.1 9.4 %collective-permute-start.5 = (f32[1,4,8,128]{3,2,1,0:T(8,128)S(1)}, f32[1,4,8,128]{3,2,1,0:T(8,128)S(1)}, u32[]{:S(2)}, u32[]{:S(2)}) collective-permute-start(f32[1,4,8,128]{3,2,1,0:T(8,128)S(1)} %get-tuple-element.21), channel_id=1, source_target_pairs={{32,0},{64,32},{96,64},{0,96},{33,1},{65,33},{97,65},{1,97},{34,2}... | collective-permute-start | bytes 49160 | tf_op jit(solution)/shard_map/ppermute | solution.py:211
  49.7 10.3 %collective-permute-start.17 = (f32[8,128]{1,0:T(8,128)S(1)}, f32[8,128]{1,0:T(8,128)S(1)}, u32[]{:S(2)}, u32[]{:S(2)}) collective-permute-start(f32[8,128]{1,0:T(8,128)S(1)} %reshape.62), channel_id=1, source_target_pairs={{0,1},{1,2},{2,3},{3,0},{4,5},{5,6},{6,7},{7,4},{8,9},{9,10},{10,1... | collective-permute-start | bytes 12296 | tf_op jit(solution)/shard_map/ppermute | solution.py:209
  49.8 10.1 %collective-permute-start.16 = (f32[8,128]{1,0:T(8,128)S(1)}, f32[8,128]{1,0:T(8,128)S(1)}, u32[]{:S(2)}, u32[]{:S(2)}) collective-permute-start(f32[8,128]{1,0:T(8,128)S(1)} %reshape.60), channel_id=1, source_target_pairs={{1,0},{2,1},{3,2},{0,3},{5,4},{6,5},{7,6},{4,7},{9,8},{10,9},{11,1... | collective-permute-start | bytes 12296 | tf_op jit(solution)/shard_map/ppermute | solution.py:209
  71.3 3.2 %collective-permute-start.18 = (f32[32,128]{1,0:T(8,128)S(1)}, f32[32,128]{1,0:T(8,128)S(1)}, u32[]{:S(2)}, u32[]{:S(2)}) collective-permute-start(f32[32,128]{1,0:T(8,128)S(1)} %reshape.64), channel_id=1, source_target_pairs={{0,1},{1,2},{2,3},{3,0},{4,5},{5,6},{6,7},{7,4},{8,9},{9,10},{10,1... | collective-permute-start | bytes 49160 | tf_op jit(solution)/shard_map/ppermute | solution.py:209
  71.7 3.4 %collective-permute-start.19 = (f32[32,128]{1,0:T(8,128)S(1)}, f32[32,128]{1,0:T(8,128)S(1)}, u32[]{:S(2)}, u32[]{:S(2)}) collective-permute-start(f32[32,128]{1,0:T(8,128)S(1)} %reshape.66), channel_id=1, source_target_pairs={{1,0},{2,1},{3,2},{0,3},{5,4},{6,5},{7,6},{4,7},{9,8},{10,9},{11,1... | collective-permute-start | bytes 49160 | tf_op jit(solution)/shard_map/ppermute | solution.py:209
  75.9 6.1 %collective-permute-start.20 = (f32[4,16,4,128]{3,2,1,0:T(4,128)S(1)}, f32[4,16,4,128]{3,2,1,0:T(4,128)S(1)}, u32[]{:S(2)}, u32[]{:S(2)}) collective-permute-start(f32[4,16,4,128]{3,2,1,0:T(4,128)S(1)} %get-tuple-element.8), channel_id=1, source_target_pairs={{0,4},{4,8},{8,12},{12,16},{16,20},{20,24},{24,28},{28,0},{1,5},{5... | collective-permute-start | bytes 393224 | tf_op jit(solution)/shard_map/ppermute | solution.py:211
  77.1 9.9 %collective-permute-start.21 = (f32[4,16,4,128]{3,2,1,0:T(4,128)S(1)}, f32[4,16,4,128]{3,2,1,0:T(4,128)S(1)}, u32[]{:S(2)}, u32[]{:S(2)}) collective-permute-start(f32[4,16,4,128]{3,2,1,0:T(4,128)S(1)} %get-tuple-element.9), channel_id=1, source_target_pairs={{4,0},{8,4},{12,8},{16,12},{20,16},{24,20},{28,24},{0,28},{5,1},{9... | collective-permute-start | bytes 393224 | tf_op jit(solution)/shard_map/ppermute | solution.py:211
  87.2 4.3 %collective-permute-start.22 = (f32[4,4,8,128]{3,2,1,0:T(8,128)S(1)}, f32[4,4,8,128]{3,2,1,0:T(8,128)S(1)}, u32[]{:S(2)}, u32[]{:S(2)}) collective-permute-start(f32[4,4,8,128]{3,2,1,0:T(8,128)S(1)} %get-tuple-element.10), channel_id=1, source_target_pairs={{0,32},{32,64},{64,96},{96,0},{1,33},{33,65},{65,97},{97,1},{2,34}... | collective-permute-start | bytes 196616 | tf_op jit(solution)/shard_map/ppermute | solution.py:211
  87.7 5.5 %collective-permute-start.23 = (f32[4,4,8,128]{3,2,1,0:T(8,128)S(1)}, f32[4,4,8,128]{3,2,1,0:T(8,128)S(1)}, u32[]{:S(2)}, u32[]{:S(2)}) collective-permute-start(f32[4,4,8,128]{3,2,1,0:T(8,128)S(1)} %get-tuple-element.11), channel_id=1, source_target_pairs={{32,0},{64,32},{96,64},{0,96},{33,1},{65,33},{97,65},{1,97},{34,2}... | collective-permute-start | bytes 196616 | tf_op jit(solution)/shard_map/ppermute | solution.py:211

commit v9 on v4

--- a/solution.py
+++ b/solution.py
@@ -140,14 +140,11 @@
     staged_ref[...] = jnp.zeros(staged_ref.shape, jnp.float32)
 
 
-def early_sample_kernel(wrapped_ref, cells_ref, fracs_ref, image_ref, grad_ref,
-                        rolled_ref, window_ref, *tables):
-    weights, slopes = tables[:3], tables[3:]
-    build_tables(cells_ref, fracs_ref, 0, 1, weights, slopes)
-    value, grads = sample_block(wrapped_ref, rolled_ref, window_ref, weights, slopes, True)
+def early_sample_kernel(wrapped_ref, cells_ref, fracs_ref, image_ref, rolled_ref, window_ref,
+                        *tables):
+    build_tables(cells_ref, fracs_ref, 0, 1, tables, None)
+    value, _ = sample_block(wrapped_ref, rolled_ref, window_ref, tables, None, True)
     image_ref[...] = value
-    for component in range(3):
-        grad_ref[component] = grads[component]
 
 
 def late_spread_kernel(cot_ref, cells_ref, fracs_ref, out_ref, product_ref, staged_ref, summed_ref, *tables):
@@ -170,17 +167,18 @@
                                           out_ref.shape[-1])
 
 
-def early_spread_kernel(adjoint_ref, grad_ref, cells_ref, fracs_ref, out_ref,
-                        product_ref, staged_ref, summed_ref, *tables):
-    dep, mid = tables[:3], tables[3:]
-    build_tables(cells_ref, fracs_ref, 0, 1, dep, None)
+def early_spread_kernel(adjoint_ref, wrapped_ref, cells_ref, fracs_ref, out_ref, rolled_ref,
+                        window_ref, product_ref, staged_ref, summed_ref, *tables):
+    dep, slopes, mid = tables[:3], tables[3:6], tables[6:]
+    build_tables(cells_ref, fracs_ref, 0, 1, dep, slopes)
     build_tables(cells_ref, fracs_ref, 0, 0, mid, None)
+    _, grads = sample_block(wrapped_ref, rolled_ref, window_ref, dep, slopes, False)
     adjoint = adjoint_ref[...]
     clear_rims(staged_ref)
     pz = out_ref.shape[-1]
     out_ref[0] = spread_block(adjoint, dep, product_ref, staged_ref, summed_ref, pz)
     for component in range(3):
-        out_ref[1 + component] = spread_block(adjoint * grad_ref[component], mid, product_ref,
+        out_ref[1 + component] = spread_block(adjoint * grads[component], mid, product_ref,
                                               staged_ref, summed_ref, pz)
 
 
@@ -269,10 +267,10 @@
     summed = pltpu.VMEM((SHIFTS, px, py, nz), f32)
 
     wrapped = widen(intensity, pz)
-    image_mid, grad_raw = vmem_call(
+    image_mid = vmem_call(
         early_sample_kernel,
-        (jax.ShapeDtypeStruct(block, f32), jax.ShapeDtypeStruct((3,) + block, f32)),
-        [rolled, windows] + table_scratch(block, 6),
+        jax.ShapeDtypeStruct(block, f32),
+        [rolled, windows] + table_scratch(block, 3),
         wrapped, cells, fracs,
     )
     adjoint_padded = vmem_call(
@@ -285,8 +283,8 @@
     early_padded = vmem_call(
         early_spread_kernel,
         jax.ShapeDtypeStruct((4, px, py, pz), f32),
-        [products, staged, summed] + table_scratch(block, 6),
-        adjoint_mid, grad_raw, cells, fracs,
+        [rolled, windows, products, staged, summed] + table_scratch(block, 9),
+        adjoint_mid, wrapped, cells, fracs,
     )
     wrapped_mid = widen(image_mid, pz)
     velocity_padded = vmem_call(

time: 95.1 us -> 97.5 us (1.025)
  Pallas kernels: 25.6 us -> 28 us
    pallas_call x4, Pallas kernels: 25.6 us -> 28 us  [vmem_call(): pl.pallas_call(kernel, out_shape=out_shapes, in_specs=[pl.BlockSpec(memor...]
    unnamed x16 -> x14, local copies, waits for them, and re-layouts: 3.59 us -> 3.58 us
  transfers between devices with their start and end apart: 24 -> 24, of which waited for: 11 -> 11; matrix products, arithmetic and copies ran while one was open for 3% -> 3% of each run, Pallas kernels for 16% -> 18%
where the time goes in v9:
time: 97.5 us; the launch traced here: 97.1 us
  waiting for transfers between devices  32.3 us (33%)
  Pallas kernels  28 us (29%)
  starting transfers between devices  25.6 us (26%)
  local copies, waits for them, and re-layouts  9.16 us (9%)
  other arithmetic  1.04 us (1%)
  between operations  1.01 us (1%)
    ppermute x16, waiting for transfers between devices, shift_from(): return lax.ppermute(piece, axis, pairs)  31.2 us
    pallas_call x4, Pallas kernels, vmem_call(): pl.pallas_call(kernel, out_shape=out_shapes, in_specs=[pl.BlockSpec(memor...  28 us
    ppermute x16, starting transfers between devices, shift_from(): return lax.ppermute(piece, axis, pairs)  18.3 us
    ppermute x8, starting transfers between devices, shift_from(): flat = lax.ppermute(piece.reshape(-1, 128), axis, pairs)  7.36 us
    unnamed x14, local copies, waits for them, and re-layouts  3.58 us
  transfers between devices with their start and end apart: 24, of which 11 were waited for; matrix products, arithmetic and copies ran while one was open for 3% of the time, Pallas kernels for 18%

profile of v9, /device:TPU:102, one launch (start us, length us, event | category | flops | bytes accessed | tf_op | source)
XLA Modules:
  0.0 97.1 jit_solution(593091076881224813)
XLA Ops:
  0.6 0.7 fusion.20
  1.4 0.5 collective-permute-start.6
  1.9 1.0 %copy-done = s32[2,2,3,8,8,128]{5,4,3,2,1,0:T(8,128)S(1)} copy-done((s32[2,2,3,8,8,128]{5,4,3,2,1,0:T(8,128)S(1)}, s32[2,2,3,8,8,128]{5,4,3,2,1,0:T(8,128)}, u32[]{:S(2)}) %copy-start) | copy-done | bytes 393240
  2.9 1.0 %copy-done.2 = f32[2,2,3,8,8,128]{5,4,3,2,1,0:T(8,128)S(1)} copy-done((f32[2,2,3,8,8,128]{5,4,3,2,1,0:T(8,128)S(1)}, f32[2,2,3,8,8,128]{5,4,3,2,1,0:T(8,128)}, u32[]{:S(2)}) %copy-start.2) | copy-done | bytes 393240
  3.9 2.4 %shard_map.59 = f32[16,16,256]{2,1,0:T(8,128)S(1)} custom-call(f32[8,8,128]{2,1,0:T(8,128)S(1)} %copy-done.4, s32[2,2,3,8,8,128]{5,4,3,2,1,0:T(8,128)S(1)} %copy-done, f32[2,2,3,8,8,128]{5,4,3,2,1,0:T(8,128)S(1)} %copy-done.2), custom_call_target="tpu_custom_call" | custom-call | flops 40000000 | bytes 2000000 | tf_op jit(solution)/shard_map/pallas_call | solution.py:186
  6.7 1.8 %collective-permute-start.1 = (f32[8,128]{1,0:T(8,128)S(1)}, f32[8,128]{1,0:T(8,128)S(1)}, u32[]{:S(2)}, u32[]{:S(2)}) collective-permute-start(f32[8,128]{1,0:T(8,128)S(1)} %reshape.54), channel_id=1, source_target_pairs={{1,0},{2,1},{3,2},{0,3},{5,4},{6,5},{7,6},{4,7},{9,8},{10,9},{11,1... | collective-permute-start | bytes 12296 | tf_op jit(solution)/shard_map/ppermute | solution.py:207
  8.5 1.5 %collective-permute-start.7 = (f32[4,8,128]{2,1,0:T(8,128)S(1)}, f32[4,8,128]{2,1,0:T(8,128)S(1)}, u32[]{:S(2)}, u32[]{:S(2)}) collective-permute-start(f32[4,8,128]{2,1,0:T(8,128)S(1)} %get-tuple-element.24), channel_id=1, source_target_pairs={{32,0},{64,32},{96,64},{0,96},{33,1},{65,33},{97,65},{1,97},{34,2}... | collective-permute-start | bytes 49160 | tf_op jit(solution)/shard_map/ppermute | solution.py:209
  10.5 0.7 copy-done.5
  11.2 2.3 %collective-permute-done.7 = f32[4,8,128]{2,1,0:T(8,128)S(1)} collective-permute-done((f32[4,8,128]{2,1,0:T(8,128)S(1)}, f32[4,8,128]{2,1,0:T(8,128)S(1)}, u32[]{:S(2)}, u32[]{:S(2)}) %collective-permute-start.7) | collective-permute-done | bytes 16416 | tf_op jit(solution)/shard_map/ppermute | solution.py:209
  13.5 1.9 %collective-permute-start.8 = (f32[16,4,128]{2,1,0:T(4,128)S(1)}, f32[16,4,128]{2,1,0:T(4,128)S(1)}, u32[]{:S(2)}, u32[]{:S(2)}) collective-permute-start(f32[16,4,128]{2,1,0:T(4,128)S(1)} %get-tuple-element.20), channel_id=1, source_target_pairs={{0,4},{4,8},{8,12},{12,16},{16,20},{20,24},{24,28},{28,0},{1,5},{5... | collective-permute-start | bytes 98312 | tf_op jit(solution)/shard_map/ppermute | solution.py:209
  15.4 0.2 collective-permute-start.9
  15.7 1.8 %collective-permute-done.8 = f32[16,4,128]{2,1,0:T(4,128)S(1)} collective-permute-done((f32[16,4,128]{2,1,0:T(4,128)S(1)}, f32[16,4,128]{2,1,0:T(4,128)S(1)}, u32[]{:S(2)}, u32[]{:S(2)}) %collective-permute-start.8) | collective-permute-done | bytes 32800 | tf_op jit(solution)/shard_map/ppermute | solution.py:209
  17.5 5.4 %collective-permute-done.9 = f32[16,4,128]{2,1,0:T(4,128)S(1)} collective-permute-done((f32[16,4,128]{2,1,0:T(4,128)S(1)}, f32[16,4,128]{2,1,0:T(4,128)S(1)}, u32[]{:S(2)}, u32[]{:S(2)}) %collective-permute-start.9) | collective-permute-done | bytes 32800 | tf_op jit(solution)/shard_map/ppermute | solution.py:209
  23.3 1.7 %collective-permute-start.10 = (f32[8,128]{1,0:T(8,128)S(1)}, f32[8,128]{1,0:T(8,128)S(1)}, u32[]{:S(2)}, u32[]{:S(2)}) collective-permute-start(f32[8,128]{1,0:T(8,128)S(1)} %reshape.56), channel_id=1, source_target_pairs={{1,0},{2,1},{3,2},{0,3},{5,4},{6,5},{7,6},{4,7},{9,8},{10,9},{11,1... | collective-permute-start | bytes 12296 | tf_op jit(solution)/shard_map/ppermute | solution.py:207
  25.2 2.0 %collective-permute-start.3 = (f32[1,16,4,128]{3,2,1,0:T(4,128)S(1)}, f32[1,16,4,128]{3,2,1,0:T(4,128)S(1)}, u32[]{:S(2)}, u32[]{:S(2)}) collective-permute-start(f32[1,16,4,128]{3,2,1,0:T(4,128)S(1)} %get-tuple-element.11), channel_id=1, source_target_pairs={{4,0},{8,4},{12,8},{16,12},{20,16},{24,20},{28,24},{0,28},{5,1},{9... | collective-permute-start | bytes 98312 | tf_op jit(solution)/shard_map/ppermute | solution.py:209
  27.2 0.1 reshape.57
  27.6 0.7 copy-done.1
  28.5 2.5 %shard_map.61 = f32[8,8,128]{2,1,0:T(8,128)S(1)} custom-call(f32[16,16,256]{2,1,0:T(8,128)S(1)} %pad_maximum_fusion.1.wrapped_ref, s32[2,2,3,8,8,128]{5,4,3,2,1,0:T(8,128)S(1)} %copy-done.1, f32[2,2,3,8,8,128]{5,4,3,2,1,0:T(8,128)S(1)} %copy-done.3), custom_call_target="tpu_custom_call" | custom-call | flops 40000000 | bytes 2000000 | tf_op jit(solution)/shard_map/pallas_call | solution.py:186
  31.0 0.3 collective-permute-start.12
  31.3 1.7 %collective-permute-start.13 = (f32[4,8,128]{2,1,0:T(8,128)S(1)}, f32[4,8,128]{2,1,0:T(8,128)S(1)}, u32[]{:S(2)}, u32[]{:S(2)}) collective-permute-start(f32[4,8,128]{2,1,0:T(8,128)S(1)} %get-tuple-element.23), channel_id=1, source_target_pairs={{32,0},{64,32},{96,64},{0,96},{33,1},{65,33},{97,65},{1,97},{34,2}... | collective-permute-start | bytes 49160 | tf_op jit(solution)/shard_map/ppermute | solution.py:209
  33.1 1.7 %collective-permute-done.12 = f32[4,8,128]{2,1,0:T(8,128)S(1)} collective-permute-done((f32[4,8,128]{2,1,0:T(8,128)S(1)}, f32[4,8,128]{2,1,0:T(8,128)S(1)}, u32[]{:S(2)}, u32[]{:S(2)}) %collective-permute-start.12) | collective-permute-done | bytes 16416 | tf_op jit(solution)/shard_map/ppermute | solution.py:209
  34.8 1.5 %collective-permute-done.13 = f32[4,8,128]{2,1,0:T(8,128)S(1)} collective-permute-done((f32[4,8,128]{2,1,0:T(8,128)S(1)}, f32[4,8,128]{2,1,0:T(8,128)S(1)}, u32[]{:S(2)}, u32[]{:S(2)}) %collective-permute-start.13) | collective-permute-done | bytes 16416 | tf_op jit(solution)/shard_map/ppermute | solution.py:209
  36.3 3.8 %collective-permute-start.14 = (f32[16,4,128]{2,1,0:T(4,128)S(1)}, f32[16,4,128]{2,1,0:T(4,128)S(1)}, u32[]{:S(2)}, u32[]{:S(2)}) collective-permute-start(f32[16,4,128]{2,1,0:T(4,128)S(1)} %get-tuple-element.18), channel_id=1, source_target_pairs={{0,4},{4,8},{8,12},{12,16},{16,20},{20,24},{24,28},{28,0},{1,5},{5... | collective-permute-start | bytes 98312 | tf_op jit(solution)/shard_map/ppermute | solution.py:209
  40.1 0.3 collective-permute-start.4
  40.4 1.7 %collective-permute-start.5 = (f32[1,4,8,128]{3,2,1,0:T(8,128)S(1)}, f32[1,4,8,128]{3,2,1,0:T(8,128)S(1)}, u32[]{:S(2)}, u32[]{:S(2)}) collective-permute-start(f32[1,4,8,128]{3,2,1,0:T(8,128)S(1)} %get-tuple-element.17), channel_id=1, source_target_pairs={{32,0},{64,32},{96,64},{0,96},{33,1},{65,33},{97,65},{1,97},{34,2}... | collective-permute-start | bytes 49160 | tf_op jit(solution)/shard_map/ppermute | solution.py:209
  42.1 5.5 %collective-permute-done.15 = f32[16,4,128]{2,1,0:T(4,128)S(1)} collective-permute-done((f32[16,4,128]{2,1,0:T(4,128)S(1)}, f32[16,4,128]{2,1,0:T(4,128)S(1)}, u32[]{:S(2)}, u32[]{:S(2)}) %collective-permute-start.15) | collective-permute-done | bytes 32800 | tf_op jit(solution)/shard_map/ppermute | solution.py:209
  48.1 1.7 %collective-permute-start.16 = (f32[8,128]{1,0:T(8,128)S(1)}, f32[8,128]{1,0:T(8,128)S(1)}, u32[]{:S(2)}, u32[]{:S(2)}) collective-permute-start(f32[8,128]{1,0:T(8,128)S(1)} %reshape.60), channel_id=1, source_target_pairs={{1,0},{2,1},{3,2},{0,3},{5,4},{6,5},{7,6},{4,7},{9,8},{10,9},{11,1... | collective-permute-start | bytes 12296 | tf_op jit(solution)/shard_map/ppermute | solution.py:207
  49.8 12.5 %shard_map.60 = f32[4,16,16,256]{3,2,1,0:T(8,128)S(1)} custom-call(f32[8,8,128]{2,1,0:T(8,128)S(1)} %fusion.9.adjoint_ref, f32[16,16,256]{2,1,0:T(8,128)S(1)} %pad_maximum_fusion.1.wrapped_ref, s32[2,2,3,8,8,128]{5,4,3,2,1,0:T(8,128)S(1)} %copy-done.1, f32[2,2,3,8,8,128]{5,4,3,2,1,0:T(8,128)S(1)} %copy-done.3), custom_call_target="tpu_custom_call" | custom-call | flops 40000000 | bytes 2000000 | tf_op jit(solution)/shard_map/pallas_call | solution.py:186
  62.8 10.6 %shard_map.62 = f32[3,16,16,256]{3,2,1,0:T(8,128)S(1)} custom-call(f32[16,16,256]{2,1,0:T(8,128)S(1)} %pad_maximum_fusion.2.wrapped_ref, f32[8,8,128]{2,1,0:T(8,128)S(1)} %copy-done.4, s32[2,2,3,8,8,128]{5,4,3,2,1,0:T(8,128)S(1)} %copy-done.1, f32[2,2,3,8,8,128]{5,4,3,2,1,0:T(8,128)S(1)} %copy-done.3), custom_call_target="tpu_custom_call" | custom-call | flops 40000000 | bytes 2000000 | tf_op jit(solution)/shard_map/pallas_call | solution.py:186
  73.4 0.1 slice_add_fusion
  73.5 0.2 fusion
  73.7 0.3 reshape.64
  74.1 0.3 reshape.66
  74.3 1.8 %collective-permute-start.19 = (f32[32,128]{1,0:T(8,128)S(1)}, f32[32,128]{1,0:T(8,128)S(1)}, u32[]{:S(2)}, u32[]{:S(2)}) collective-permute-start(f32[32,128]{1,0:T(8,128)S(1)} %reshape.66), channel_id=1, source_target_pairs={{1,0},{2,1},{3,2},{0,3},{5,4},{6,5},{7,6},{4,7},{9,8},{10,9},{11,1... | collective-permute-start | bytes 49160 | tf_op jit(solution)/shard_map/ppermute | solution.py:207
  76.1 1.1 %collective-permute-done.18 = f32[32,128]{1,0:T(8,128)S(1)} collective-permute-done((f32[32,128]{1,0:T(8,128)S(1)}, f32[32,128]{1,0:T(8,128)S(1)}, u32[]{:S(2)}, u32[]{:S(2)}) %collective-permute-start.18) | collective-permute-done | bytes 16416 | tf_op jit(solution)/shard_map/ppermute | solution.py:207
  77.2 0.5 reshape.65
  77.8 0.5 reshape.67
  78.3 0.2 fusion.3
  78.6 1.2 %collective-permute-start.20 = (f32[4,16,4,128]{3,2,1,0:T(4,128)S(1)}, f32[4,16,4,128]{3,2,1,0:T(4,128)S(1)}, u32[]{:S(2)}, u32[]{:S(2)}) collective-permute-start(f32[4,16,4,128]{3,2,1,0:T(4,128)S(1)} %get-tuple-element.4), channel_id=1, source_target_pairs={{0,4},{4,8},{8,12},{12,16},{16,20},{20,24},{24,28},{28,0},{1,5},{5... | collective-permute-start | bytes 393224 | tf_op jit(solution)/shard_map/ppermute | solution.py:209
  79.8 0.9 collective-permute-start.21
  80.7 4.0 %collective-permute-done.20 = f32[4,16,4,128]{3,2,1,0:T(4,128)S(1)} collective-permute-done((f32[4,16,4,128]{3,2,1,0:T(4,128)S(1)}, f32[4,16,4,128]{3,2,1,0:T(4,128)S(1)}, u32[]{:S(2)}, u32[]{:S(2)}) %collective-permute-start.20) | collective-permute-done | bytes 131104 | tf_op jit(solution)/shard_map/ppermute | solution.py:209
  84.6 5.1 %collective-permute-done.21 = f32[4,16,4,128]{3,2,1,0:T(4,128)S(1)} collective-permute-done((f32[4,16,4,128]{3,2,1,0:T(4,128)S(1)}, f32[4,16,4,128]{3,2,1,0:T(4,128)S(1)}, u32[]{:S(2)}, u32[]{:S(2)}) %collective-permute-start.21) | collective-permute-done | bytes 131104 | tf_op jit(solution)/shard_map/ppermute | solution.py:209
  89.8 0.6 collective-permute-start.22
  90.4 1.5 %collective-permute-start.23 = (f32[4,4,8,128]{3,2,1,0:T(8,128)S(1)}, f32[4,4,8,128]{3,2,1,0:T(8,128)S(1)}, u32[]{:S(2)}, u32[]{:S(2)}) collective-permute-start(f32[4,4,8,128]{3,2,1,0:T(8,128)S(1)} %get-tuple-element.7), channel_id=1, source_target_pairs={{32,0},{64,32},{96,64},{0,96},{33,1},{65,33},{97,65},{1,97},{34,2}... | collective-permute-start | bytes 196616 | tf_op jit(solution)/shard_map/ppermute | solution.py:209
  91.9 2.2 %collective-permute-done.22 = f32[4,4,8,128]{3,2,1,0:T(8,128)S(1)} collective-permute-done((f32[4,4,8,128]{3,2,1,0:T(8,128)S(1)}, f32[4,4,8,128]{3,2,1,0:T(8,128)S(1)}, u32[]{:S(2)}, u32[]{:S(2)}) %collective-permute-start.22) | collective-permute-done | bytes 65568 | tf_op jit(solution)/shard_map/ppermute | solution.py:209
  94.2 1.7 %collective-permute-done.23 = f32[4,4,8,128]{3,2,1,0:T(8,128)S(1)} collective-permute-done((f32[4,4,8,128]{3,2,1,0:T(8,128)S(1)}, f32[4,4,8,128]{3,2,1,0:T(8,128)S(1)}, u32[]{:S(2)}, u32[]{:S(2)}) %collective-permute-start.23) | collective-permute-done | bytes 65568 | tf_op jit(solution)/shard_map/ppermute | solution.py:209
  95.9 0.6 slice_bitcast_fusion
  96.5 0.6 slice.168
  (64 shorter events, 2.9 us)
Async XLA Ops:
  0.6 1.2 %copy-start.4 = (f32[8,8,128]{2,1,0:T(8,128)S(1)}, f32[8,8,128]{2,1,0:T(8,128)}, u32[]{:S(2)}) copy-start(f32[8,8,128]{2,1,0:T(8,128)} %cot_ref.3) | copy-start | bytes 98308
  1.4 9.1 %collective-permute-start.6 = (f32[4,8,128]{2,1,0:T(8,128)S(1)}, f32[4,8,128]{2,1,0:T(8,128)S(1)}, u32[]{:S(2)}, u32[]{:S(2)}) collective-permute-start(f32[4,8,128]{2,1,0:T(8,128)S(1)} %get-tuple-element.25), channel_id=1, source_target_pairs={{0,32},{32,64},{64,96},{96,0},{1,33},{33,65},{65,97},{97,1},{2,34}... | collective-permute-start | bytes 49160 | tf_op jit(solution)/shard_map/ppermute | solution.py:209
  1.9 1.0 %copy-start = (s32[2,2,3,8,8,128]{5,4,3,2,1,0:T(8,128)S(1)}, s32[2,2,3,8,8,128]{5,4,3,2,1,0:T(8,128)}, u32[]{:S(2)}) copy-start(s32[2,2,3,8,8,128]{5,4,3,2,1,0:T(8,128)} %cells_ref.7) | copy-start | bytes 1179652
  2.9 1.0 %copy-start.2 = (f32[2,2,3,8,8,128]{5,4,3,2,1,0:T(8,128)S(1)}, f32[2,2,3,8,8,128]{5,4,3,2,1,0:T(8,128)}, u32[]{:S(2)}) copy-start(f32[2,2,3,8,8,128]{5,4,3,2,1,0:T(8,128)} %fracs_ref.7) | copy-start | bytes 1179652
  6.5 3.6 %collective-permute-start = (f32[8,128]{1,0:T(8,128)S(1)}, f32[8,128]{1,0:T(8,128)S(1)}, u32[]{:S(2)}, u32[]{:S(2)}) collective-permute-start(f32[8,128]{1,0:T(8,128)S(1)} %reshape.52), channel_id=1, source_target_pairs={{0,1},{1,2},{2,3},{3,0},{4,5},{5,6},{6,7},{7,4},{8,9},{9,10},{10,1... | collective-permute-start | bytes 12296 | tf_op jit(solution)/shard_map/ppermute | solution.py:207
  6.7 3.6 %collective-permute-start.1 = (f32[8,128]{1,0:T(8,128)S(1)}, f32[8,128]{1,0:T(8,128)S(1)}, u32[]{:S(2)}, u32[]{:S(2)}) collective-permute-start(f32[8,128]{1,0:T(8,128)S(1)} %reshape.54), channel_id=1, source_target_pairs={{1,0},{2,1},{3,2},{0,3},{5,4},{6,5},{7,6},{4,7},{9,8},{10,9},{11,1... | collective-permute-start | bytes 12296 | tf_op jit(solution)/shard_map/ppermute | solution.py:207
  8.5 4.9 %collective-permute-start.7 = (f32[4,8,128]{2,1,0:T(8,128)S(1)}, f32[4,8,128]{2,1,0:T(8,128)S(1)}, u32[]{:S(2)}, u32[]{:S(2)}) collective-permute-start(f32[4,8,128]{2,1,0:T(8,128)S(1)} %get-tuple-element.24), channel_id=1, source_target_pairs={{32,0},{64,32},{96,64},{0,96},{33,1},{65,33},{97,65},{1,97},{34,2}... | collective-permute-start | bytes 49160 | tf_op jit(solution)/shard_map/ppermute | solution.py:209
  10.4 0.8 copy-start.5
  13.5 4.0 %collective-permute-start.8 = (f32[16,4,128]{2,1,0:T(4,128)S(1)}, f32[16,4,128]{2,1,0:T(4,128)S(1)}, u32[]{:S(2)}, u32[]{:S(2)}) collective-permute-start(f32[16,4,128]{2,1,0:T(4,128)S(1)} %get-tuple-element.20), channel_id=1, source_target_pairs={{0,4},{4,8},{8,12},{12,16},{16,20},{20,24},{24,28},{28,0},{1,5},{5... | collective-permute-start | bytes 98312 | tf_op jit(solution)/shard_map/ppermute | solution.py:209
  15.4 7.5 %collective-permute-start.9 = (f32[16,4,128]{2,1,0:T(4,128)S(1)}, f32[16,4,128]{2,1,0:T(4,128)S(1)}, u32[]{:S(2)}, u32[]{:S(2)}) collective-permute-start(f32[16,4,128]{2,1,0:T(4,128)S(1)} %get-tuple-element.21), channel_id=1, source_target_pairs={{4,0},{8,4},{12,8},{16,12},{20,16},{24,20},{28,24},{0,28},{5,1},{9... | collective-permute-start | bytes 98312 | tf_op jit(solution)/shard_map/ppermute | solution.py:209
  23.3 4.1 %collective-permute-start.11 = (f32[8,128]{1,0:T(8,128)S(1)}, f32[8,128]{1,0:T(8,128)S(1)}, u32[]{:S(2)}, u32[]{:S(2)}) collective-permute-start(f32[8,128]{1,0:T(8,128)S(1)} %reshape.58), channel_id=1, source_target_pairs={{0,1},{1,2},{2,3},{3,0},{4,5},{5,6},{6,7},{7,4},{8,9},{9,10},{10,1... | collective-permute-start | bytes 12296 | tf_op jit(solution)/shard_map/ppermute | solution.py:207
  23.3 3.8 %collective-permute-start.10 = (f32[8,128]{1,0:T(8,128)S(1)}, f32[8,128]{1,0:T(8,128)S(1)}, u32[]{:S(2)}, u32[]{:S(2)}) collective-permute-start(f32[8,128]{1,0:T(8,128)S(1)} %reshape.56), channel_id=1, source_target_pairs={{1,0},{2,1},{3,2},{0,3},{5,4},{6,5},{7,6},{4,7},{9,8},{10,9},{11,1... | collective-permute-start | bytes 12296 | tf_op jit(solution)/shard_map/ppermute | solution.py:207
  25.1 8.0 %collective-permute-start.2 = (f32[1,16,4,128]{3,2,1,0:T(4,128)S(1)}, f32[1,16,4,128]{3,2,1,0:T(4,128)S(1)}, u32[]{:S(2)}, u32[]{:S(2)}) collective-permute-start(f32[1,16,4,128]{3,2,1,0:T(4,128)S(1)} %get-tuple-element.10), channel_id=1, source_target_pairs={{0,4},{4,8},{8,12},{12,16},{16,20},{20,24},{24,28},{28,0},{1,5},{5... | collective-permute-start | bytes 98312 | tf_op jit(solution)/shard_map/ppermute | solution.py:209
  25.2 7.9 %collective-permute-start.3 = (f32[1,16,4,128]{3,2,1,0:T(4,128)S(1)}, f32[1,16,4,128]{3,2,1,0:T(4,128)S(1)}, u32[]{:S(2)}, u32[]{:S(2)}) collective-permute-start(f32[1,16,4,128]{3,2,1,0:T(4,128)S(1)} %get-tuple-element.11), channel_id=1, source_target_pairs={{4,0},{8,4},{12,8},{16,12},{20,16},{24,20},{28,24},{0,28},{5,1},{9... | collective-permute-start | bytes 98312 | tf_op jit(solution)/shard_map/ppermute | solution.py:209
  27.3 1.0 %copy-start.1 = (s32[2,2,3,8,8,128]{5,4,3,2,1,0:T(8,128)S(1)}, s32[2,2,3,8,8,128]{5,4,3,2,1,0:T(8,128)}, u32[]{:S(2)}) copy-start(s32[2,2,3,8,8,128]{5,4,3,2,1,0:T(8,128)} %cells_ref.7) | copy-start | bytes 1179652
  27.3 1.1 %copy-start.3 = (f32[2,2,3,8,8,128]{5,4,3,2,1,0:T(8,128)S(1)}, f32[2,2,3,8,8,128]{5,4,3,2,1,0:T(8,128)}, u32[]{:S(2)}) copy-start(f32[2,2,3,8,8,128]{5,4,3,2,1,0:T(8,128)} %fracs_ref.7) | copy-start | bytes 1179652
  31.0 3.8 %collective-permute-start.12 = (f32[4,8,128]{2,1,0:T(8,128)S(1)}, f32[4,8,128]{2,1,0:T(8,128)S(1)}, u32[]{:S(2)}, u32[]{:S(2)}) collective-permute-start(f32[4,8,128]{2,1,0:T(8,128)S(1)} %get-tuple-element.22), channel_id=1, source_target_pairs={{0,32},{32,64},{64,96},{96,0},{1,33},{33,65},{65,97},{97,1},{2,34}... | collective-permute-start | bytes 49160 | tf_op jit(solution)/shard_map/ppermute | solution.py:209
  31.3 4.9 %collective-permute-start.13 = (f32[4,8,128]{2,1,0:T(8,128)S(1)}, f32[4,8,128]{2,1,0:T(8,128)S(1)}, u32[]{:S(2)}, u32[]{:S(2)}) collective-permute-start(f32[4,8,128]{2,1,0:T(8,128)S(1)} %get-tuple-element.23), channel_id=1, source_target_pairs={{32,0},{64,32},{96,64},{0,96},{33,1},{65,33},{97,65},{1,97},{34,2}... | collective-permute-start | bytes 49160 | tf_op jit(solution)/shard_map/ppermute | solution.py:209
  36.3 5.8 %collective-permute-start.14 = (f32[16,4,128]{2,1,0:T(4,128)S(1)}, f32[16,4,128]{2,1,0:T(4,128)S(1)}, u32[]{:S(2)}, u32[]{:S(2)}) collective-permute-start(f32[16,4,128]{2,1,0:T(4,128)S(1)} %get-tuple-element.18), channel_id=1, source_target_pairs={{0,4},{4,8},{8,12},{12,16},{16,20},{20,24},{24,28},{28,0},{1,5},{5... | collective-permute-start | bytes 98312 | tf_op jit(solution)/shard_map/ppermute | solution.py:209
  40.1 7.5 %collective-permute-start.15 = (f32[16,4,128]{2,1,0:T(4,128)S(1)}, f32[16,4,128]{2,1,0:T(4,128)S(1)}, u32[]{:S(2)}, u32[]{:S(2)}) collective-permute-start(f32[16,4,128]{2,1,0:T(4,128)S(1)} %get-tuple-element.19), channel_id=1, source_target_pairs={{4,0},{8,4},{12,8},{16,12},{20,16},{24,20},{28,24},{0,28},{5,1},{9... | collective-permute-start | bytes 98312 | tf_op jit(solution)/shard_map/ppermute | solution.py:209
  40.1 9.7 %collective-permute-start.4 = (f32[1,4,8,128]{3,2,1,0:T(8,128)S(1)}, f32[1,4,8,128]{3,2,1,0:T(8,128)S(1)}, u32[]{:S(2)}, u32[]{:S(2)}) collective-permute-start(f32[1,4,8,128]{3,2,1,0:T(8,128)S(1)} %get-tuple-element.16), channel_id=1, source_target_pairs={{0,32},{32,64},{64,96},{96,0},{1,33},{33,65},{65,97},{97,1},{2,34}... | collective-permute-start | bytes 49160 | tf_op jit(solution)/shard_map/ppermute | solution.py:209
  40.4 9.4 %collective-permute-start.5 = (f32[1,4,8,128]{3,2,1,0:T(8,128)S(1)}, f32[1,4,8,128]{3,2,1,0:T(8,128)S(1)}, u32[]{:S(2)}, u32[]{:S(2)}) collective-permute-start(f32[1,4,8,128]{3,2,1,0:T(8,128)S(1)} %get-tuple-element.17), channel_id=1, source_target_pairs={{32,0},{64,32},{96,64},{0,96},{33,1},{65,33},{97,65},{1,97},{34,2}... | collective-permute-start | bytes 49160 | tf_op jit(solution)/shard_map/ppermute | solution.py:209
  48.0 14.5 %collective-permute-start.17 = (f32[8,128]{1,0:T(8,128)S(1)}, f32[8,128]{1,0:T(8,128)S(1)}, u32[]{:S(2)}, u32[]{:S(2)}) collective-permute-start(f32[8,128]{1,0:T(8,128)S(1)} %reshape.62), channel_id=1, source_target_pairs={{0,1},{1,2},{2,3},{3,0},{4,5},{5,6},{6,7},{7,4},{8,9},{9,10},{10,1... | collective-permute-start | bytes 12296 | tf_op jit(solution)/shard_map/ppermute | solution.py:207
  48.1 14.3 %collective-permute-start.16 = (f32[8,128]{1,0:T(8,128)S(1)}, f32[8,128]{1,0:T(8,128)S(1)}, u32[]{:S(2)}, u32[]{:S(2)}) collective-permute-start(f32[8,128]{1,0:T(8,128)S(1)} %reshape.60), channel_id=1, source_target_pairs={{1,0},{2,1},{3,2},{0,3},{5,4},{6,5},{7,6},{4,7},{9,8},{10,9},{11,1... | collective-permute-start | bytes 12296 | tf_op jit(solution)/shard_map/ppermute | solution.py:207
  74.0 3.2 %collective-permute-start.18 = (f32[32,128]{1,0:T(8,128)S(1)}, f32[32,128]{1,0:T(8,128)S(1)}, u32[]{:S(2)}, u32[]{:S(2)}) collective-permute-start(f32[32,128]{1,0:T(8,128)S(1)} %reshape.64), channel_id=1, source_target_pairs={{0,1},{1,2},{2,3},{3,0},{4,5},{5,6},{6,7},{7,4},{8,9},{9,10},{10,1... | collective-permute-start | bytes 49160 | tf_op jit(solution)/shard_map/ppermute | solution.py:207
  74.3 3.4 %collective-permute-start.19 = (f32[32,128]{1,0:T(8,128)S(1)}, f32[32,128]{1,0:T(8,128)S(1)}, u32[]{:S(2)}, u32[]{:S(2)}) collective-permute-start(f32[32,128]{1,0:T(8,128)S(1)} %reshape.66), channel_id=1, source_target_pairs={{1,0},{2,1},{3,2},{0,3},{5,4},{6,5},{7,6},{4,7},{9,8},{10,9},{11,1... | collective-permute-start | bytes 49160 | tf_op jit(solution)/shard_map/ppermute | solution.py:207
  78.6 6.1 %collective-permute-start.20 = (f32[4,16,4,128]{3,2,1,0:T(4,128)S(1)}, f32[4,16,4,128]{3,2,1,0:T(4,128)S(1)}, u32[]{:S(2)}, u32[]{:S(2)}) collective-permute-start(f32[4,16,4,128]{3,2,1,0:T(4,128)S(1)} %get-tuple-element.4), channel_id=1, source_target_pairs={{0,4},{4,8},{8,12},{12,16},{16,20},{20,24},{24,28},{28,0},{1,5},{5... | collective-permute-start | bytes 393224 | tf_op jit(solution)/shard_map/ppermute | solution.py:209
  79.8 9.9 %collective-permute-start.21 = (f32[4,16,4,128]{3,2,1,0:T(4,128)S(1)}, f32[4,16,4,128]{3,2,1,0:T(4,128)S(1)}, u32[]{:S(2)}, u32[]{:S(2)}) collective-permute-start(f32[4,16,4,128]{3,2,1,0:T(4,128)S(1)} %get-tuple-element.5), channel_id=1, source_target_pairs={{4,0},{8,4},{12,8},{16,12},{20,16},{24,20},{28,24},{0,28},{5,1},{9... | collective-permute-start | bytes 393224 | tf_op jit(solution)/shard_map/ppermute | solution.py:209
  89.8 4.3 %collective-permute-start.22 = (f32[4,4,8,128]{3,2,1,0:T(8,128)S(1)}, f32[4,4,8,128]{3,2,1,0:T(8,128)S(1)}, u32[]{:S(2)}, u32[]{:S(2)}) collective-permute-start(f32[4,4,8,128]{3,2,1,0:T(8,128)S(1)} %get-tuple-element.6), channel_id=1, source_target_pairs={{0,32},{32,64},{64,96},{96,0},{1,33},{33,65},{65,97},{97,1},{2,34}... | collective-permute-start | bytes 196616 | tf_op jit(solution)/shard_map/ppermute | solution.py:209
  90.4 5.5 %collective-permute-start.23 = (f32[4,4,8,128]{3,2,1,0:T(8,128)S(1)}, f32[4,4,8,128]{3,2,1,0:T(8,128)S(1)}, u32[]{:S(2)}, u32[]{:S(2)}) collective-permute-start(f32[4,4,8,128]{3,2,1,0:T(8,128)S(1)} %get-tuple-element.7), channel_id=1, source_target_pairs={{32,0},{64,32},{96,64},{0,96},{33,1},{65,33},{97,65},{1,97},{34,2}... | collective-permute-start | bytes 196616 | tf_op jit(solution)/shard_map/ppermute | solution.py:209

commit v10 on v4

--- a/solution.py
+++ b/solution.py
@@ -157,7 +157,7 @@
                                 out_ref.shape[-1])
 
 
-def late_velocity_kernel(wrapped_ref, cot_ref, cells_ref, fracs_ref, out_ref,
+def late_velocity_kernel(wrapped_ref, cot_ref, early_ref, cells_ref, fracs_ref, out_ref,
                          rolled_ref, window_ref, product_ref, staged_ref, summed_ref, *tables):
     weights, slopes, mid = tables[:3], tables[3:6], tables[6:]
     build_tables(cells_ref, fracs_ref, 1, 1, weights, slopes)
@@ -165,9 +165,10 @@
     _, grads = sample_block(wrapped_ref, rolled_ref, window_ref, weights, slopes, False)
     cot = cot_ref[...]
     clear_rims(staged_ref)
+    out_ref[0] = early_ref[0]
     for component in range(3):
-        out_ref[component] = spread_block(cot * grads[component], mid, product_ref, staged_ref, summed_ref,
-                                          out_ref.shape[-1])
+        out_ref[1 + component] = early_ref[1 + component] + spread_block(
+            cot * grads[component], mid, product_ref, staged_ref, summed_ref, out_ref.shape[-1])
 
 
 def early_spread_kernel(adjoint_ref, grad_ref, cells_ref, fracs_ref, out_ref,
@@ -291,12 +292,11 @@
     wrapped_mid = widen(image_mid, pz)
     velocity_padded = vmem_call(
         late_velocity_kernel,
-        jax.ShapeDtypeStruct((3, px, py, pz), f32),
+        jax.ShapeDtypeStruct((4, px, py, pz), f32),
         [rolled, windows, products, staged, summed] + table_scratch(block, 9),
-        wrapped_mid, cotangent, cells, fracs,
-    )
-    deposits = jnp.concatenate([early_padded[:1], early_padded[1:] + velocity_padded])
-    folded = fold(deposits, nz)
+        wrapped_mid, cotangent, early_padded, cells, fracs,
+    )
+    folded = fold(velocity_padded, nz)
     return (folded[0], folded[1:])
 
 

time: 95.1 us -> 95 us (level)
  no operation moved by 1% of the time
where the time goes in v10:
time: 95 us; the launch traced here: 94.7 us
  waiting for transfers between devices  32.3 us (34%)
  starting transfers between devices  25.7 us (27%)
  Pallas kernels  25.7 us (27%)
  local copies, waits for them, and re-layouts  9.35 us (10%)
  between operations  1 us (1%)
    ppermute x16, waiting for transfers between devices, shift_from(): return lax.ppermute(piece, axis, pairs)  31.2 us
    pallas_call x4, Pallas kernels, vmem_call(): pl.pallas_call(kernel, out_shape=out_shapes, in_specs=[pl.BlockSpec(memor...  25.7 us
    ppermute x16, starting transfers between devices, shift_from(): return lax.ppermute(piece, axis, pairs)  18.4 us
    ppermute x8, starting transfers between devices, shift_from(): flat = lax.ppermute(piece.reshape(-1, 128), axis, pairs)  7.36 us
    unnamed x16, local copies, waits for them, and re-layouts  3.59 us
  transfers between devices with their start and end apart: 24, of which 11 were waited for; matrix products, arithmetic and copies ran while one was open for 3% of the time, Pallas kernels for 16%

profile of v10, /device:TPU:102, one launch (start us, length us, event | category | flops | bytes accessed | tf_op | source)
XLA Modules:
  0.0 94.7 jit_solution(2528555272846017091)
XLA Ops:
  0.6 0.7 fusion.18
  1.4 0.5 collective-permute-start
  1.9 1.0 %copy-done = s32[2,2,3,8,8,128]{5,4,3,2,1,0:T(8,128)S(1)} copy-done((s32[2,2,3,8,8,128]{5,4,3,2,1,0:T(8,128)S(1)}, s32[2,2,3,8,8,128]{5,4,3,2,1,0:T(8,128)}, u32[]{:S(2)}) %copy-start) | copy-done | bytes 393240
  2.9 1.0 %copy-done.2 = f32[2,2,3,8,8,128]{5,4,3,2,1,0:T(8,128)S(1)} copy-done((f32[2,2,3,8,8,128]{5,4,3,2,1,0:T(8,128)S(1)}, f32[2,2,3,8,8,128]{5,4,3,2,1,0:T(8,128)}, u32[]{:S(2)}) %copy-start.2) | copy-done | bytes 393240
  3.9 2.4 %shard_map.60 = f32[16,16,256]{2,1,0:T(8,128)S(1)} custom-call(f32[8,8,128]{2,1,0:T(8,128)S(1)} %copy-done.4, s32[2,2,3,8,8,128]{5,4,3,2,1,0:T(8,128)S(1)} %copy-done, f32[2,2,3,8,8,128]{5,4,3,2,1,0:T(8,128)S(1)} %copy-done.2), custom_call_target="tpu_custom_call" | custom-call | flops 40000000 | bytes 2000000 | tf_op jit(solution)/shard_map/pallas_call | solution.py:189
  6.7 1.8 %collective-permute-start.13 = (f32[8,128]{1,0:T(8,128)S(1)}, f32[8,128]{1,0:T(8,128)S(1)}, u32[]{:S(2)}, u32[]{:S(2)}) collective-permute-start(f32[8,128]{1,0:T(8,128)S(1)} %reshape.62), channel_id=1, source_target_pairs={{1,0},{2,1},{3,2},{0,3},{5,4},{6,5},{7,6},{4,7},{9,8},{10,9},{11,1... | collective-permute-start | bytes 12296 | tf_op jit(solution)/shard_map/ppermute | solution.py:210
  8.5 1.5 %collective-permute-start.1 = (f32[4,8,128]{2,1,0:T(8,128)S(1)}, f32[4,8,128]{2,1,0:T(8,128)S(1)}, u32[]{:S(2)}, u32[]{:S(2)}) collective-permute-start(f32[4,8,128]{2,1,0:T(8,128)S(1)} %get-tuple-element.28), channel_id=1, source_target_pairs={{32,0},{64,32},{96,64},{0,96},{33,1},{65,33},{97,65},{1,97},{34,2}... | collective-permute-start | bytes 49160 | tf_op jit(solution)/shard_map/ppermute | solution.py:212
  10.5 0.7 copy-done.5
  11.2 2.3 %collective-permute-done.1 = f32[4,8,128]{2,1,0:T(8,128)S(1)} collective-permute-done((f32[4,8,128]{2,1,0:T(8,128)S(1)}, f32[4,8,128]{2,1,0:T(8,128)S(1)}, u32[]{:S(2)}, u32[]{:S(2)}) %collective-permute-start.1) | collective-permute-done | bytes 16416 | tf_op jit(solution)/shard_map/ppermute | solution.py:212
  13.5 1.9 %collective-permute-start.2 = (f32[16,4,128]{2,1,0:T(4,128)S(1)}, f32[16,4,128]{2,1,0:T(4,128)S(1)}, u32[]{:S(2)}, u32[]{:S(2)}) collective-permute-start(f32[16,4,128]{2,1,0:T(4,128)S(1)} %get-tuple-element.24), channel_id=1, source_target_pairs={{0,4},{4,8},{8,12},{12,16},{16,20},{20,24},{24,28},{28,0},{1,5},{5... | collective-permute-start | bytes 98312 | tf_op jit(solution)/shard_map/ppermute | solution.py:212
  15.4 0.2 collective-permute-start.3
  15.7 1.8 %collective-permute-done.2 = f32[16,4,128]{2,1,0:T(4,128)S(1)} collective-permute-done((f32[16,4,128]{2,1,0:T(4,128)S(1)}, f32[16,4,128]{2,1,0:T(4,128)S(1)}, u32[]{:S(2)}, u32[]{:S(2)}) %collective-permute-start.2) | collective-permute-done | bytes 32800 | tf_op jit(solution)/shard_map/ppermute | solution.py:212
  17.5 5.4 %collective-permute-done.3 = f32[16,4,128]{2,1,0:T(4,128)S(1)} collective-permute-done((f32[16,4,128]{2,1,0:T(4,128)S(1)}, f32[16,4,128]{2,1,0:T(4,128)S(1)}, u32[]{:S(2)}, u32[]{:S(2)}) %collective-permute-start.3) | collective-permute-done | bytes 32800 | tf_op jit(solution)/shard_map/ppermute | solution.py:212
  23.3 1.7 %collective-permute-start.4 = (f32[8,128]{1,0:T(8,128)S(1)}, f32[8,128]{1,0:T(8,128)S(1)}, u32[]{:S(2)}, u32[]{:S(2)}) collective-permute-start(f32[8,128]{1,0:T(8,128)S(1)} %reshape.52), channel_id=1, source_target_pairs={{1,0},{2,1},{3,2},{0,3},{5,4},{6,5},{7,6},{4,7},{9,8},{10,9},{11,1... | collective-permute-start | bytes 12296 | tf_op jit(solution)/shard_map/ppermute | solution.py:210
  25.2 2.0 %collective-permute-start.15 = (f32[1,16,4,128]{3,2,1,0:T(4,128)S(1)}, f32[1,16,4,128]{3,2,1,0:T(4,128)S(1)}, u32[]{:S(2)}, u32[]{:S(2)}) collective-permute-start(f32[1,16,4,128]{3,2,1,0:T(4,128)S(1)} %get-tuple-element.15), channel_id=1, source_target_pairs={{4,0},{8,4},{12,8},{16,12},{20,16},{24,20},{28,24},{0,28},{5,1},{9... | collective-permute-start | bytes 98312 | tf_op jit(solution)/shard_map/ppermute | solution.py:212
  27.2 0.1 reshape.53
  27.4 0.1 reshape.55
  27.6 0.7 copy-done.1
  28.5 4.2 %shard_map.59 = (f32[8,8,128]{2,1,0:T(8,128)S(1)}, f32[3,8,8,128]{3,2,1,0:T(8,128)S(1)}) custom-call(f32[16,16,256]{2,1,0:T(8,128)S(1)} %pad_maximum_fusion.wrapped_ref, s32[2,2,3,8,8,128]{5,4,3,2,1,0:T(8,128)S(1)} %copy-done.1, f32[2,2,3,8,8,128]{5,4,3,2,1,0:T(8,128)S(1)} %copy-done.3), custom_call_target="tpu_custom_call" | custom-call | flops 40000000 | bytes 2000000 | tf_op jit(solution)/shard_map/pallas_call | solution.py:189
  32.7 0.3 collective-permute-start.6
  33.1 1.8 %collective-permute-start.7 = (f32[4,8,128]{2,1,0:T(8,128)S(1)}, f32[4,8,128]{2,1,0:T(8,128)S(1)}, u32[]{:S(2)}, u32[]{:S(2)}) collective-permute-start(f32[4,8,128]{2,1,0:T(8,128)S(1)} %get-tuple-element.26), channel_id=1, source_target_pairs={{32,0},{64,32},{96,64},{0,96},{33,1},{65,33},{97,65},{1,97},{34,2}... | collective-permute-start | bytes 49160 | tf_op jit(solution)/shard_map/ppermute | solution.py:212
  34.9 1.6 %collective-permute-done.6 = f32[4,8,128]{2,1,0:T(8,128)S(1)} collective-permute-done((f32[4,8,128]{2,1,0:T(8,128)S(1)}, f32[4,8,128]{2,1,0:T(8,128)S(1)}, u32[]{:S(2)}, u32[]{:S(2)}) %collective-permute-start.6) | collective-permute-done | bytes 16416 | tf_op jit(solution)/shard_map/ppermute | solution.py:212
  36.5 1.6 %collective-permute-done.7 = f32[4,8,128]{2,1,0:T(8,128)S(1)} collective-permute-done((f32[4,8,128]{2,1,0:T(8,128)S(1)}, f32[4,8,128]{2,1,0:T(8,128)S(1)}, u32[]{:S(2)}, u32[]{:S(2)}) %collective-permute-start.7) | collective-permute-done | bytes 16416 | tf_op jit(solution)/shard_map/ppermute | solution.py:212
  38.1 3.8 %collective-permute-start.8 = (f32[16,4,128]{2,1,0:T(4,128)S(1)}, f32[16,4,128]{2,1,0:T(4,128)S(1)}, u32[]{:S(2)}, u32[]{:S(2)}) collective-permute-start(f32[16,4,128]{2,1,0:T(4,128)S(1)} %get-tuple-element.22), channel_id=1, source_target_pairs={{0,4},{4,8},{8,12},{12,16},{16,20},{20,24},{24,28},{28,0},{1,5},{5... | collective-permute-start | bytes 98312 | tf_op jit(solution)/shard_map/ppermute | solution.py:212
  41.9 0.3 collective-permute-start.16
  42.1 1.7 %collective-permute-start.17 = (f32[1,4,8,128]{3,2,1,0:T(8,128)S(1)}, f32[1,4,8,128]{3,2,1,0:T(8,128)S(1)}, u32[]{:S(2)}, u32[]{:S(2)}) collective-permute-start(f32[1,4,8,128]{3,2,1,0:T(8,128)S(1)} %get-tuple-element.21), channel_id=1, source_target_pairs={{32,0},{64,32},{96,64},{0,96},{33,1},{65,33},{97,65},{1,97},{34,2}... | collective-permute-start | bytes 49160 | tf_op jit(solution)/shard_map/ppermute | solution.py:212
  43.9 5.5 %collective-permute-done.9 = f32[16,4,128]{2,1,0:T(4,128)S(1)} collective-permute-done((f32[16,4,128]{2,1,0:T(4,128)S(1)}, f32[16,4,128]{2,1,0:T(4,128)S(1)}, u32[]{:S(2)}, u32[]{:S(2)}) %collective-permute-start.9) | collective-permute-done | bytes 32800 | tf_op jit(solution)/shard_map/ppermute | solution.py:212
  49.8 1.7 %collective-permute-start.10 = (f32[8,128]{1,0:T(8,128)S(1)}, f32[8,128]{1,0:T(8,128)S(1)}, u32[]{:S(2)}, u32[]{:S(2)}) collective-permute-start(f32[8,128]{1,0:T(8,128)S(1)} %reshape.56), channel_id=1, source_target_pairs={{1,0},{2,1},{3,2},{0,3},{5,4},{6,5},{7,6},{4,7},{9,8},{10,9},{11,1... | collective-permute-start | bytes 12296 | tf_op jit(solution)/shard_map/ppermute | solution.py:210
  51.6 8.4 %shard_map.61.early_ref = f32[4,16,16,256]{3,2,1,0:T(8,128)S(1)} custom-call(f32[8,8,128]{2,1,0:T(8,128)S(1)} %fusion.6.adjoint_ref, f32[3,8,8,128]{3,2,1,0:T(8,128)S(1)} %get-tuple-element.5.grad_ref, s32[2,2,3,8,8,128]{5,4,3,2,1,0:T(8,128)S(1)} %copy-done.1, f32[2,2,3,8,8,128]{5,4,3,2,1,0:T(8,128)S(1)} %copy-done.3), custom_call_target="tpu_custom_call" | custom-call | flops 40000000 | bytes 2000000 | tf_op jit(solution)/shard_map/pallas_call | solution.py:189
  60.4 10.7 %shard_map.62 = f32[4,16,16,256]{3,2,1,0:T(8,128)S(1)} custom-call(f32[16,16,256]{2,1,0:T(8,128)S(1)} %pad_maximum_fusion.1.wrapped_ref, f32[8,8,128]{2,1,0:T(8,128)S(1)} %copy-done.4, f32[4,16,16,256]{3,2,1,0:T(8,128)S(1)} %shard_map.61.early_ref, s32[2,2,3,8,8,128]{5,4,3,2,1,0:T(8,128)S(1)} %copy-done.1, f32[2,2,3,8,8,128]{5,4,3,2,1,0:T(8,128)S(1)} %copy-done.3), custom_call_target="tpu_custom_call" | custom-call | flops 40000000 | bytes 2000000 | tf_op jit(solution)/shard_map/pallas_call | solution.py:189
  71.1 0.2 fusion.7
  71.3 0.3 reshape.64
  71.6 0.3 reshape.66
  71.9 1.8 %collective-permute-start.19 = (f32[32,128]{1,0:T(8,128)S(1)}, f32[32,128]{1,0:T(8,128)S(1)}, u32[]{:S(2)}, u32[]{:S(2)}) collective-permute-start(f32[32,128]{1,0:T(8,128)S(1)} %reshape.66), channel_id=1, source_target_pairs={{1,0},{2,1},{3,2},{0,3},{5,4},{6,5},{7,6},{4,7},{9,8},{10,9},{11,1... | collective-permute-start | bytes 49160 | tf_op jit(solution)/shard_map/ppermute | solution.py:210
  73.7 1.1 %collective-permute-done.18 = f32[32,128]{1,0:T(8,128)S(1)} collective-permute-done((f32[32,128]{1,0:T(8,128)S(1)}, f32[32,128]{1,0:T(8,128)S(1)}, u32[]{:S(2)}, u32[]{:S(2)}) %collective-permute-start.18) | collective-permute-done | bytes 16416 | tf_op jit(solution)/shard_map/ppermute | solution.py:210
  74.8 0.5 reshape.65
  75.3 0.5 reshape.67
  75.9 0.2 fusion
  76.1 1.2 %collective-permute-start.20 = (f32[4,16,4,128]{3,2,1,0:T(4,128)S(1)}, f32[4,16,4,128]{3,2,1,0:T(4,128)S(1)}, u32[]{:S(2)}, u32[]{:S(2)}) collective-permute-start(f32[4,16,4,128]{3,2,1,0:T(4,128)S(1)} %get-tuple-element.8), channel_id=1, source_target_pairs={{0,4},{4,8},{8,12},{12,16},{16,20},{20,24},{24,28},{28,0},{1,5},{5... | collective-permute-start | bytes 393224 | tf_op jit(solution)/shard_map/ppermute | solution.py:212
  77.3 0.9 collective-permute-start.21
  78.2 4.0 %collective-permute-done.20 = f32[4,16,4,128]{3,2,1,0:T(4,128)S(1)} collective-permute-done((f32[4,16,4,128]{3,2,1,0:T(4,128)S(1)}, f32[4,16,4,128]{3,2,1,0:T(4,128)S(1)}, u32[]{:S(2)}, u32[]{:S(2)}) %collective-permute-start.20) | collective-permute-done | bytes 131104 | tf_op jit(solution)/shard_map/ppermute | solution.py:212
  82.2 5.1 %collective-permute-done.21 = f32[4,16,4,128]{3,2,1,0:T(4,128)S(1)} collective-permute-done((f32[4,16,4,128]{3,2,1,0:T(4,128)S(1)}, f32[4,16,4,128]{3,2,1,0:T(4,128)S(1)}, u32[]{:S(2)}, u32[]{:S(2)}) %collective-permute-start.21) | collective-permute-done | bytes 131104 | tf_op jit(solution)/shard_map/ppermute | solution.py:212
  87.4 0.6 collective-permute-start.22
  87.9 1.5 %collective-permute-start.23 = (f32[4,4,8,128]{3,2,1,0:T(8,128)S(1)}, f32[4,4,8,128]{3,2,1,0:T(8,128)S(1)}, u32[]{:S(2)}, u32[]{:S(2)}) collective-permute-start(f32[4,4,8,128]{3,2,1,0:T(8,128)S(1)} %get-tuple-element.11), channel_id=1, source_target_pairs={{32,0},{64,32},{96,64},{0,96},{33,1},{65,33},{97,65},{1,97},{34,2}... | collective-permute-start | bytes 196616 | tf_op jit(solution)/shard_map/ppermute | solution.py:212
  89.5 2.2 %collective-permute-done.22 = f32[4,4,8,128]{3,2,1,0:T(8,128)S(1)} collective-permute-done((f32[4,4,8,128]{3,2,1,0:T(8,128)S(1)}, f32[4,4,8,128]{3,2,1,0:T(8,128)S(1)}, u32[]{:S(2)}, u32[]{:S(2)}) %collective-permute-start.22) | collective-permute-done | bytes 65568 | tf_op jit(solution)/shard_map/ppermute | solution.py:212
  91.7 1.7 %collective-permute-done.23 = f32[4,4,8,128]{3,2,1,0:T(8,128)S(1)} collective-permute-done((f32[4,4,8,128]{3,2,1,0:T(8,128)S(1)}, f32[4,4,8,128]{3,2,1,0:T(8,128)S(1)}, u32[]{:S(2)}, u32[]{:S(2)}) %collective-permute-start.23) | collective-permute-done | bytes 65568 | tf_op jit(solution)/shard_map/ppermute | solution.py:212
  93.4 0.6 slice_bitcast_fusion
  94.0 0.6 slice.155
  (64 shorter events, 2.7 us)
Async XLA Ops:
  0.6 1.2 %copy-start.4 = (f32[8,8,128]{2,1,0:T(8,128)S(1)}, f32[8,8,128]{2,1,0:T(8,128)}, u32[]{:S(2)}) copy-start(f32[8,8,128]{2,1,0:T(8,128)} %cot_ref.3) | copy-start | bytes 98308
  1.4 9.1 %collective-permute-start = (f32[4,8,128]{2,1,0:T(8,128)S(1)}, f32[4,8,128]{2,1,0:T(8,128)S(1)}, u32[]{:S(2)}, u32[]{:S(2)}) collective-permute-start(f32[4,8,128]{2,1,0:T(8,128)S(1)} %get-tuple-element.29), channel_id=1, source_target_pairs={{0,32},{32,64},{64,96},{96,0},{1,33},{33,65},{65,97},{97,1},{2,34}... | collective-permute-start | bytes 49160 | tf_op jit(solution)/shard_map/ppermute | solution.py:212
  1.9 1.0 %copy-start = (s32[2,2,3,8,8,128]{5,4,3,2,1,0:T(8,128)S(1)}, s32[2,2,3,8,8,128]{5,4,3,2,1,0:T(8,128)}, u32[]{:S(2)}) copy-start(s32[2,2,3,8,8,128]{5,4,3,2,1,0:T(8,128)} %cells_ref.7) | copy-start | bytes 1179652
  2.9 1.0 %copy-start.2 = (f32[2,2,3,8,8,128]{5,4,3,2,1,0:T(8,128)S(1)}, f32[2,2,3,8,8,128]{5,4,3,2,1,0:T(8,128)}, u32[]{:S(2)}) copy-start(f32[2,2,3,8,8,128]{5,4,3,2,1,0:T(8,128)} %fracs_ref.7) | copy-start | bytes 1179652
  6.5 3.6 %collective-permute-start.12 = (f32[8,128]{1,0:T(8,128)S(1)}, f32[8,128]{1,0:T(8,128)S(1)}, u32[]{:S(2)}, u32[]{:S(2)}) collective-permute-start(f32[8,128]{1,0:T(8,128)S(1)} %reshape.60), channel_id=1, source_target_pairs={{0,1},{1,2},{2,3},{3,0},{4,5},{5,6},{6,7},{7,4},{8,9},{9,10},{10,1... | collective-permute-start | bytes 12296 | tf_op jit(solution)/shard_map/ppermute | solution.py:210
  6.7 3.6 %collective-permute-start.13 = (f32[8,128]{1,0:T(8,128)S(1)}, f32[8,128]{1,0:T(8,128)S(1)}, u32[]{:S(2)}, u32[]{:S(2)}) collective-permute-start(f32[8,128]{1,0:T(8,128)S(1)} %reshape.62), channel_id=1, source_target_pairs={{1,0},{2,1},{3,2},{0,3},{5,4},{6,5},{7,6},{4,7},{9,8},{10,9},{11,1... | collective-permute-start | bytes 12296 | tf_op jit(solution)/shard_map/ppermute | solution.py:210
  8.5 4.9 %collective-permute-start.1 = (f32[4,8,128]{2,1,0:T(8,128)S(1)}, f32[4,8,128]{2,1,0:T(8,128)S(1)}, u32[]{:S(2)}, u32[]{:S(2)}) collective-permute-start(f32[4,8,128]{2,1,0:T(8,128)S(1)} %get-tuple-element.28), channel_id=1, source_target_pairs={{32,0},{64,32},{96,64},{0,96},{33,1},{65,33},{97,65},{1,97},{34,2}... | collective-permute-start | bytes 49160 | tf_op jit(solution)/shard_map/ppermute | solution.py:212
  10.4 0.8 copy-start.5
  13.5 4.0 %collective-permute-start.2 = (f32[16,4,128]{2,1,0:T(4,128)S(1)}, f32[16,4,128]{2,1,0:T(4,128)S(1)}, u32[]{:S(2)}, u32[]{:S(2)}) collective-permute-start(f32[16,4,128]{2,1,0:T(4,128)S(1)} %get-tuple-element.24), channel_id=1, source_target_pairs={{0,4},{4,8},{8,12},{12,16},{16,20},{20,24},{24,28},{28,0},{1,5},{5... | collective-permute-start | bytes 98312 | tf_op jit(solution)/shard_map/ppermute | solution.py:212
  15.4 7.5 %collective-permute-start.3 = (f32[16,4,128]{2,1,0:T(4,128)S(1)}, f32[16,4,128]{2,1,0:T(4,128)S(1)}, u32[]{:S(2)}, u32[]{:S(2)}) collective-permute-start(f32[16,4,128]{2,1,0:T(4,128)S(1)} %get-tuple-element.25), channel_id=1, source_target_pairs={{4,0},{8,4},{12,8},{16,12},{20,16},{24,20},{28,24},{0,28},{5,1},{9... | collective-permute-start | bytes 98312 | tf_op jit(solution)/shard_map/ppermute | solution.py:212
  23.3 4.1 %collective-permute-start.5 = (f32[8,128]{1,0:T(8,128)S(1)}, f32[8,128]{1,0:T(8,128)S(1)}, u32[]{:S(2)}, u32[]{:S(2)}) collective-permute-start(f32[8,128]{1,0:T(8,128)S(1)} %reshape.54), channel_id=1, source_target_pairs={{0,1},{1,2},{2,3},{3,0},{4,5},{5,6},{6,7},{7,4},{8,9},{9,10},{10,1... | collective-permute-start | bytes 12296 | tf_op jit(solution)/shard_map/ppermute | solution.py:210
  23.3 3.8 %collective-permute-start.4 = (f32[8,128]{1,0:T(8,128)S(1)}, f32[8,128]{1,0:T(8,128)S(1)}, u32[]{:S(2)}, u32[]{:S(2)}) collective-permute-start(f32[8,128]{1,0:T(8,128)S(1)} %reshape.52), channel_id=1, source_target_pairs={{1,0},{2,1},{3,2},{0,3},{5,4},{6,5},{7,6},{4,7},{9,8},{10,9},{11,1... | collective-permute-start | bytes 12296 | tf_op jit(solution)/shard_map/ppermute | solution.py:210
  25.1 7.9 %collective-permute-start.14 = (f32[1,16,4,128]{3,2,1,0:T(4,128)S(1)}, f32[1,16,4,128]{3,2,1,0:T(4,128)S(1)}, u32[]{:S(2)}, u32[]{:S(2)}) collective-permute-start(f32[1,16,4,128]{3,2,1,0:T(4,128)S(1)} %get-tuple-element.14), channel_id=1, source_target_pairs={{0,4},{4,8},{8,12},{12,16},{16,20},{20,24},{24,28},{28,0},{1,5},{5... | collective-permute-start | bytes 98312 | tf_op jit(solution)/shard_map/ppermute | solution.py:212
  25.2 7.9 %collective-permute-start.15 = (f32[1,16,4,128]{3,2,1,0:T(4,128)S(1)}, f32[1,16,4,128]{3,2,1,0:T(4,128)S(1)}, u32[]{:S(2)}, u32[]{:S(2)}) collective-permute-start(f32[1,16,4,128]{3,2,1,0:T(4,128)S(1)} %get-tuple-element.15), channel_id=1, source_target_pairs={{4,0},{8,4},{12,8},{16,12},{20,16},{24,20},{28,24},{0,28},{5,1},{9... | collective-permute-start | bytes 98312 | tf_op jit(solution)/shard_map/ppermute | solution.py:212
  27.3 1.0 %copy-start.1 = (s32[2,2,3,8,8,128]{5,4,3,2,1,0:T(8,128)S(1)}, s32[2,2,3,8,8,128]{5,4,3,2,1,0:T(8,128)}, u32[]{:S(2)}) copy-start(s32[2,2,3,8,8,128]{5,4,3,2,1,0:T(8,128)} %cells_ref.7) | copy-start | bytes 1179652
  27.3 1.1 %copy-start.3 = (f32[2,2,3,8,8,128]{5,4,3,2,1,0:T(8,128)S(1)}, f32[2,2,3,8,8,128]{5,4,3,2,1,0:T(8,128)}, u32[]{:S(2)}) copy-start(f32[2,2,3,8,8,128]{5,4,3,2,1,0:T(8,128)} %fracs_ref.7) | copy-start | bytes 1179652
  32.7 3.8 %collective-permute-start.6 = (f32[4,8,128]{2,1,0:T(8,128)S(1)}, f32[4,8,128]{2,1,0:T(8,128)S(1)}, u32[]{:S(2)}, u32[]{:S(2)}) collective-permute-start(f32[4,8,128]{2,1,0:T(8,128)S(1)} %get-tuple-element.27), channel_id=1, source_target_pairs={{0,32},{32,64},{64,96},{96,0},{1,33},{33,65},{65,97},{97,1},{2,34}... | collective-permute-start | bytes 49160 | tf_op jit(solution)/shard_map/ppermute | solution.py:212
  33.1 5.0 %collective-permute-start.7 = (f32[4,8,128]{2,1,0:T(8,128)S(1)}, f32[4,8,128]{2,1,0:T(8,128)S(1)}, u32[]{:S(2)}, u32[]{:S(2)}) collective-permute-start(f32[4,8,128]{2,1,0:T(8,128)S(1)} %get-tuple-element.26), channel_id=1, source_target_pairs={{32,0},{64,32},{96,64},{0,96},{33,1},{65,33},{97,65},{1,97},{34,2}... | collective-permute-start | bytes 49160 | tf_op jit(solution)/shard_map/ppermute | solution.py:212
  38.1 5.8 %collective-permute-start.8 = (f32[16,4,128]{2,1,0:T(4,128)S(1)}, f32[16,4,128]{2,1,0:T(4,128)S(1)}, u32[]{:S(2)}, u32[]{:S(2)}) collective-permute-start(f32[16,4,128]{2,1,0:T(4,128)S(1)} %get-tuple-element.22), channel_id=1, source_target_pairs={{0,4},{4,8},{8,12},{12,16},{16,20},{20,24},{24,28},{28,0},{1,5},{5... | collective-permute-start | bytes 98312 | tf_op jit(solution)/shard_map/ppermute | solution.py:212
  41.9 7.5 %collective-permute-start.9 = (f32[16,4,128]{2,1,0:T(4,128)S(1)}, f32[16,4,128]{2,1,0:T(4,128)S(1)}, u32[]{:S(2)}, u32[]{:S(2)}) collective-permute-start(f32[16,4,128]{2,1,0:T(4,128)S(1)} %get-tuple-element.23), channel_id=1, source_target_pairs={{4,0},{8,4},{12,8},{16,12},{20,16},{24,20},{28,24},{0,28},{5,1},{9... | collective-permute-start | bytes 98312 | tf_op jit(solution)/shard_map/ppermute | solution.py:212
  41.9 9.7 %collective-permute-start.16 = (f32[1,4,8,128]{3,2,1,0:T(8,128)S(1)}, f32[1,4,8,128]{3,2,1,0:T(8,128)S(1)}, u32[]{:S(2)}, u32[]{:S(2)}) collective-permute-start(f32[1,4,8,128]{3,2,1,0:T(8,128)S(1)} %get-tuple-element.20), channel_id=1, source_target_pairs={{0,32},{32,64},{64,96},{96,0},{1,33},{33,65},{65,97},{97,1},{2,34}... | collective-permute-start | bytes 49160 | tf_op jit(solution)/shard_map/ppermute | solution.py:212
  42.1 9.4 %collective-permute-start.17 = (f32[1,4,8,128]{3,2,1,0:T(8,128)S(1)}, f32[1,4,8,128]{3,2,1,0:T(8,128)S(1)}, u32[]{:S(2)}, u32[]{:S(2)}) collective-permute-start(f32[1,4,8,128]{3,2,1,0:T(8,128)S(1)} %get-tuple-element.21), channel_id=1, source_target_pairs={{32,0},{64,32},{96,64},{0,96},{33,1},{65,33},{97,65},{1,97},{34,2}... | collective-permute-start | bytes 49160 | tf_op jit(solution)/shard_map/ppermute | solution.py:212
  49.8 10.4 %collective-permute-start.11 = (f32[8,128]{1,0:T(8,128)S(1)}, f32[8,128]{1,0:T(8,128)S(1)}, u32[]{:S(2)}, u32[]{:S(2)}) collective-permute-start(f32[8,128]{1,0:T(8,128)S(1)} %reshape.58), channel_id=1, source_target_pairs={{0,1},{1,2},{2,3},{3,0},{4,5},{5,6},{6,7},{7,4},{8,9},{9,10},{10,1... | collective-permute-start | bytes 12296 | tf_op jit(solution)/shard_map/ppermute | solution.py:210
  49.8 10.1 %collective-permute-start.10 = (f32[8,128]{1,0:T(8,128)S(1)}, f32[8,128]{1,0:T(8,128)S(1)}, u32[]{:S(2)}, u32[]{:S(2)}) collective-permute-start(f32[8,128]{1,0:T(8,128)S(1)} %reshape.56), channel_id=1, source_target_pairs={{1,0},{2,1},{3,2},{0,3},{5,4},{6,5},{7,6},{4,7},{9,8},{10,9},{11,1... | collective-permute-start | bytes 12296 | tf_op jit(solution)/shard_map/ppermute | solution.py:210
  71.5 3.2 %collective-permute-start.18 = (f32[32,128]{1,0:T(8,128)S(1)}, f32[32,128]{1,0:T(8,128)S(1)}, u32[]{:S(2)}, u32[]{:S(2)}) collective-permute-start(f32[32,128]{1,0:T(8,128)S(1)} %reshape.64), channel_id=1, source_target_pairs={{0,1},{1,2},{2,3},{3,0},{4,5},{5,6},{6,7},{7,4},{8,9},{9,10},{10,1... | collective-permute-start | bytes 49160 | tf_op jit(solution)/shard_map/ppermute | solution.py:210
  71.9 3.4 %collective-permute-start.19 = (f32[32,128]{1,0:T(8,128)S(1)}, f32[32,128]{1,0:T(8,128)S(1)}, u32[]{:S(2)}, u32[]{:S(2)}) collective-permute-start(f32[32,128]{1,0:T(8,128)S(1)} %reshape.66), channel_id=1, source_target_pairs={{1,0},{2,1},{3,2},{0,3},{5,4},{6,5},{7,6},{4,7},{9,8},{10,9},{11,1... | collective-permute-start | bytes 49160 | tf_op jit(solution)/shard_map/ppermute | solution.py:210
  76.1 6.1 %collective-permute-start.20 = (f32[4,16,4,128]{3,2,1,0:T(4,128)S(1)}, f32[4,16,4,128]{3,2,1,0:T(4,128)S(1)}, u32[]{:S(2)}, u32[]{:S(2)}) collective-permute-start(f32[4,16,4,128]{3,2,1,0:T(4,128)S(1)} %get-tuple-element.8), channel_id=1, source_target_pairs={{0,4},{4,8},{8,12},{12,16},{16,20},{20,24},{24,28},{28,0},{1,5},{5... | collective-permute-start | bytes 393224 | tf_op jit(solution)/shard_map/ppermute | solution.py:212
  77.3 9.9 %collective-permute-start.21 = (f32[4,16,4,128]{3,2,1,0:T(4,128)S(1)}, f32[4,16,4,128]{3,2,1,0:T(4,128)S(1)}, u32[]{:S(2)}, u32[]{:S(2)}) collective-permute-start(f32[4,16,4,128]{3,2,1,0:T(4,128)S(1)} %get-tuple-element.9), channel_id=1, source_target_pairs={{4,0},{8,4},{12,8},{16,12},{20,16},{24,20},{28,24},{0,28},{5,1},{9... | collective-permute-start | bytes 393224 | tf_op jit(solution)/shard_map/ppermute | solution.py:212
  87.4 4.3 %collective-permute-start.22 = (f32[4,4,8,128]{3,2,1,0:T(8,128)S(1)}, f32[4,4,8,128]{3,2,1,0:T(8,128)S(1)}, u32[]{:S(2)}, u32[]{:S(2)}) collective-permute-start(f32[4,4,8,128]{3,2,1,0:T(8,128)S(1)} %get-tuple-element.10), channel_id=1, source_target_pairs={{0,32},{32,64},{64,96},{96,0},{1,33},{33,65},{65,97},{97,1},{2,34}... | collective-permute-start | bytes 196616 | tf_op jit(solution)/shard_map/ppermute | solution.py:212
  87.9 5.5 %collective-permute-start.23 = (f32[4,4,8,128]{3,2,1,0:T(8,128)S(1)}, f32[4,4,8,128]{3,2,1,0:T(8,128)S(1)}, u32[]{:S(2)}, u32[]{:S(2)}) collective-permute-start(f32[4,4,8,128]{3,2,1,0:T(8,128)S(1)} %get-tuple-element.11), channel_id=1, source_target_pairs={{32,0},{64,32},{96,64},{0,96},{33,1},{65,33},{97,65},{1,97},{34,2}... | collective-permute-start | bytes 196616 | tf_op jit(solution)/shard_map/ppermute | solution.py:212
